TPU v7x, 512 devices: a whole 4x4x16 slice. The times are simulated.
512 devices in a mesh: row: 8 (over x, core), col: 16 (over z_hi, y), layer: 4 (over z_lo).
Axes of the slice: x: 4, y: 4, z: 16 (z_hi: 4, z_lo: 4; z = z_hi * 4 + z_lo), core: 2. Of those that a mesh axis runs over, the one named last changes fastest.
Arguments:
- a_tiles: bfloat16 [8, 64, 128, 4096], P('row', ('col', 'layer')), may hold values from -0.109375 to 0.109375
- a_rows: int32 [8, 64, 128], P('row', ('col', 'layer')), may hold values from 0 to 127
- a_cols: int32 [8, 64, 128], P('row', ('col', 'layer')), may hold values from 0 to 15
- a_count: int32 [8, 64], P('row', ('col', 'layer')), may hold values from 16 to 128, as said below
- p_tiles: bfloat16 [16, 64, 4, 4096], P('row', ('col', 'layer')), may hold values from -0.375 to 0.375
- p_cols: int32 [16, 64, 4], P('row', ('col', 'layer')), may hold values from -1 to 1
Outputs:
- coarse: float32 [64, 192], replicated
Inputs may be any that keep to these rules, and one draw needn't show every extreme that they name: `a_count`: some device uses all 128 slots and some device only 16 of them.
All inputs are finite; a program needn't handle non-finite values.
Results may differ from a plain program's by a relative error of at most 0.0037.
Values may be sent and summed in bfloat16 or wider, within the bound.
No kernel may reach another device: no remote copies, remote signals or barrier semaphores. Data moves between devices by JAX's collectives and lax.ppermute only.
A program may use at most 64 MiB of HBM per device.

v0:
```python
import math

import jax
import jax.numpy as jnp
from jax import lax
from jax.sharding import Mesh
from jax.sharding import PartitionSpec as P

TILE = 64
PB = 1
COL_LAYER = ("col_0", "col_1", "layer")
ROW_COL_LAYER = ("row", "col_0", "col_1", "layer")


def joined_along(tiles, dim):
    tiles = jnp.moveaxis(tiles, 0, dim)
    shape = tiles.shape
    return tiles.reshape(*shape[:dim], shape[dim] * shape[dim + 1], *shape[dim + 2 :])


def sent_to_all(shard, axis):
    peers = lax.axis_size(axis)
    return lax.all_to_all(
        jnp.broadcast_to(shard[None], (peers, *shard.shape)), axis, 0, 0, tiled=True
    )


def gather_directly(shard, axis, dim):
    return joined_along(sent_to_all(shard, axis), dim)


def all_blocks(shard, axes, turns):
    tiles = shard[None]
    for k in turns:
        tiles = lax.all_gather(tiles, axes[k], axis=0, tiled=True)
    block = [lax.axis_size(axes[k]) for k in reversed(turns)]
    tiles = tiles.reshape(*block, *shard.shape)
    turned = sorted(range(len(turns)), key=lambda place: turns[len(turns) - 1 - place])
    return tiles.transpose(*turned, *range(len(turns), tiles.ndim)).reshape(-1, *shard.shape)


def whole_of(shard, axes, turns, dim):
    return joined_along(all_blocks(shard, axes, turns), dim)


def densify(tile_list, column_ids, window_count):
    row_count = tile_list.shape[0]
    slot_count = tile_list.shape[2]
    onehot = (
        column_ids.reshape(row_count, slot_count)[..., None]
        == jnp.arange(window_count, dtype=jnp.int32)
    ).astype(jnp.bfloat16)
    blocks = tile_list.reshape(row_count, slot_count, TILE, TILE)
    densified = jnp.einsum("tsj,tsab->tajb", onehot, blocks, preferred_element_type=jnp.float32)
    return densified.reshape(row_count, TILE, window_count * TILE).astype(jnp.bfloat16)


def per_device(a_tiles, a_rows, a_cols, a_count, p_tiles, p_cols):
    window_count = 2 * PB
    window_width = window_count * TILE
    groups = lax.axis_size(COL_LAYER)
    local_rows = p_tiles.shape[0]
    block_rows = local_rows * groups
    slot_total = a_tiles.shape[2]
    own_window = densify(p_tiles, p_cols, window_count)
    column_window = gather_directly(own_window, "row", 0)
    tile_stack = a_tiles.reshape(slot_total, TILE, TILE)
    row_ids = a_rows.reshape(slot_total)
    col_ids = a_cols.reshape(slot_total)
    live_count = a_count.reshape(())
    slot_block = math.gcd(slot_total, 64)

    def accumulate(turn_index, running):
        first_slot = turn_index * slot_block
        tile_block = lax.dynamic_slice_in_dim(tile_stack, first_slot, slot_block, 0)
        live_mask = (first_slot + jnp.arange(slot_block, dtype=jnp.int32) < live_count).astype(
            jnp.bfloat16
        )
        tile_block = tile_block * live_mask[:, None, None]
        picked = jnp.take(
            column_window, lax.dynamic_slice_in_dim(col_ids, first_slot, slot_block, 0), axis=0
        )
        products = jnp.einsum(
            "sab,sbc->sac", tile_block, picked, preferred_element_type=jnp.float32
        )
        return running.at[lax.dynamic_slice_in_dim(row_ids, first_slot, slot_block, 0)].add(
            products
        )

    empty = jnp.zeros((block_rows, TILE, window_width), jnp.float32)
    loop_turns = slot_total // slot_block
    partial_product = lax.fori_loop(0, loop_turns, accumulate, empty)
    stacked = partial_product.reshape(local_rows, groups, TILE, window_width)
    own_rows = own_window.reshape(local_rows, 1, TILE, window_width)
    galerkin = jnp.einsum(
        "tmaj,tmak->jk",
        whole_of(own_rows, COL_LAYER, (0, 2, 1), 1).astype(jnp.float32),
        stacked,
        precision=lax.Precision.HIGHEST,
    )
    panel_size = PB * TILE
    upper_blocks = jnp.concatenate(
        [
            galerkin[:panel_size, :panel_size],
            galerkin[:panel_size, panel_size:],
            galerkin[panel_size:, panel_size:],
        ],
        axis=1,
    )
    return lax.psum(upper_blocks, ROW_COL_LAYER)


def solution(mesh):
    torus = Mesh(
        mesh.devices.reshape(mesh.shape["row"], 4, 4, mesh.shape["layer"]),
        ("row", "col_0", "col_1", "layer"),
    )
    in_specs = (
        P("row", COL_LAYER, None, None),
        P("row", COL_LAYER, None),
        P("row", COL_LAYER, None),
        P("row", COL_LAYER),
        P("row", COL_LAYER, None, None),
        P("row", COL_LAYER, None),
    )
    out_specs = P()
    return jax.shard_map(
        per_device, mesh=torus, in_specs=in_specs, out_specs=out_specs, check_vma=False
    )
```

profile of v0, /device:TPU:1, one launch (start us, length us, event | category | flops | bytes accessed | tf_op | source)
XLA Modules:
  0.0 212.0 jit_solution(6482381941543475081)
XLA Ops:
  6.5 1.0 reshape.60
  7.5 0.9 fusion.9
  8.4 0.1 convert_element_type.39
  8.5 23.9 %all_gather.9 = bf16[4,2,1,64,128]{4,3,2,1,0:T(8,128)(2,1)S(1)} all-gather(bf16[1,2,1,64,128]{4,3,2,1,0:T(8,128)(2,1)S(1)} %bitcast.32), channel_id=1, replica_groups=mesh['row'=8,'col_0'=4,'col_1'=4,'layer'=4] {'col_0'}, dimensions={0}, use_global_device_ids=true | all-gather | bytes 163840 | tf_op jit(solution)/shard_map/all_gather | solution.py:35
  32.4 13.5 %all_gather.10 = bf16[16,2,1,64,128]{4,3,2,1,0:T(8,128)(2,1)} all-gather(bf16[4,2,1,64,128]{4,3,2,1,0:T(8,128)(2,1)S(1)} %all_gather.9), channel_id=1, replica_groups=mesh['row'=8,'col_0'=4,'col_1'=4,'layer'=4] {'layer'}, dimensions={0}, use_global_device_ids=true | all-gather | bytes 655360 | tf_op jit(solution)/shard_map/all_gather | solution.py:35
  46.0 0.0 all-gather.2.cloned.1.call-update
  46.0 0.1 convert_element_type.40
  46.1 0.8 broadcast_in_dim.45
  46.9 10.4 %all-to-all-start = ((bf16[8,2,64,128]{3,2,1,0:T(8,128)(2,1)}), bf16[8,2,64,128]{3,2,1,0:T(8,128)(2,1)S(1)}, u32[]{:S(2)}, u32[]{:S(2)}) async-start(bf16[8,2,64,128]{3,2,1,0:T(8,128)(2,1)} %broadcast_in_dim.45), calls=%async_computation | async-start | bytes 524288 | tf_op jit(solution)/shard_map/all_to_all | solution.py:23
  57.3 2.3 %copy.18 = bf16[1,1,128,4096]{2,3,1,0:T(8,128)(2,1)} copy(bf16[1,1,128,4096]{3,2,1,0:T(8,128)(2,1)} %param.8) | data formatting | bytes 2097152 | tf_op args[0]
  59.6 4.2 %all-to-all-done = bf16[8,2,64,128]{3,2,1,0:T(8,128)(2,1)S(1)} async-done(((bf16[8,2,64,128]{3,2,1,0:T(8,128)(2,1)}), bf16[8,2,64,128]{3,2,1,0:T(8,128)(2,1)S(1)}, u32[]{:S(2)}, u32[]{:S(2)}) %all-to-all-start) | async-done | bytes 262176 | tf_op jit(solution)/shard_map/all_to_all | solution.py:23
  63.8 2.5 %broadcast_in_dim.44 = f32[128,64,128]{2,1,0:T(8,128)} broadcast(f32[]{:T(128)} %constant.62.clone.1), dimensions={} | broadcast | bytes 4194308 | tf_op jit(solution)/shard_map/broadcast_in_dim | solution.py:90
  66.2 32.7 %while.13 = (s32[]{:T(128)}, f32[128,64,128]{2,1,0:T(8,128)}, s32[128]{0:T(128)S(1)}, bf16[128,64,64]{0,2,1:T(8,128)(2,1)}, s32[]{:T(128)}, /*index=5*/s32[128]{...) while((s32[]{:T(128)}, f32[128,64,128]{2,1,0:T(8,128)}, ...), condition=%wide.region_2.3_spmd, body=%wide.region_0.2_spmd.sunk | while | flops 68421384 | bytes 14162223 | solution.py:92
  66.2 0.7 compare_and_fusion.2
  67.0 0.7 gather_fusion
  67.7 1.6 constant_dynamic-slice_fusion.2
  69.4 2.4 %copy.31 = bf16[64,64,64]{2,1,0:T(8,128)(2,1)} copy(bf16[64,64,64]{0,2,1:T(8,128)(2,1)S(1)} %constant_dynamic-slice_fusion.2) | data formatting | bytes 1048576 | tf_op jit(solution)/shard_map/while/body/eval_jaxpr/dynamic_slice | solution.py:75
  71.7 1.7 fusion.24
  73.5 0.1 compare_select_fusion.4
  73.5 9.1 %scatter_fusion = f32[128,64,128]{2,1,0:T(8,128)} fusion(f32[128,64,128]{2,1,0:T(8,128)} %get-tuple-element.222, s32[64]{0:T(128)S(1)} %compare_select_fusion.4, f32[64,64,128]{2,1,0:T(8,128)S(1)} %fusion.24), kind=kCustom, calls=%fused_computation.1.clone.1 | custom fusion | flops 524288 | bytes 6291712 | tf_op jit(solution)/shard_map/while/body/eval_jaxpr/scatter-add | solution.py:86
  82.7 0.7 compare_and_fusion.2
  83.4 0.7 gather_fusion
  84.1 1.6 constant_dynamic-slice_fusion.2
  85.8 2.4 %copy.31 = bf16[64,64,64]{2,1,0:T(8,128)(2,1)} copy(bf16[64,64,64]{0,2,1:T(8,128)(2,1)S(1)} %constant_dynamic-slice_fusion.2) | data formatting | bytes 1048576 | tf_op jit(solution)/shard_map/while/body/eval_jaxpr/dynamic_slice | solution.py:75
  88.1 1.7 fusion.24
  89.8 0.1 compare_select_fusion.4
  89.9 9.0 %scatter_fusion = f32[128,64,128]{2,1,0:T(8,128)} fusion(f32[128,64,128]{2,1,0:T(8,128)} %get-tuple-element.222, s32[64]{0:T(128)S(1)} %compare_select_fusion.4, f32[64,64,128]{2,1,0:T(8,128)S(1)} %fusion.24), kind=kCustom, calls=%fused_computation.1.clone.1 | custom fusion | flops 524288 | bytes 6291712 | tf_op jit(solution)/shard_map/while/body/eval_jaxpr/scatter-add | solution.py:86
  99.0 1.9 copy.17
  100.9 0.9 copy-done
  101.8 2.6 %fusion.10 = f32[128,128]{1,0:T(8,128)S(1)} fusion(bf16[2,64,64,128]{3,2,0,1:T(8,128)(2,1)S(1)} %bitcast.30, f32[2,64,64,128]{3,2,1,0:T(8,128)S(1)} %bitcast.29), kind=kOutput, calls=%fused_computation.19 | convolution fusion | flops 1610612736 | bytes 6356992 | tf_op jit(solution)/shard_map/tmaj,tmak->jk/dot_general | solution.py:95
  104.4 0.1 slice.13
  104.5 100.7 %psum.7 = f32[64,192]{1,0:T(8,128)} all-reduce(f32[64,192]{1,0:T(8,128)S(1)} %pad_maximum_fusion), channel_id=1, replica_groups=mesh['row'=8,'col_0'=4,'col_1'=4,'layer'=4] {'row','col_0','col_1','layer'}, use_global_device_ids=true, to_apply=%region_3.4 | all-reduce | flops 12288 | bytes 98304 | tf_op jit(solution)/shard_map/psum | solution.py:110
  (11 shorter events, 0.0 us)
Async XLA Ops:
  6.5 92.4 %all-gather.2.cloned.1.call-start = ((), (), s32[]{:S(2)}) async-start(), calls=%async_computation.1 | async-start | bytes 2621440 | tf_op jit(solution)/shard_map/all_gather | solution.py:35
  32.4 33.8 %copy-start.1 = (s32[1,1,128]{2,1,0:T(1,128)S(1)}, s32[1,1,128]{2,1,0:T(1,128)}, u32[]{:S(2)}) copy-start(s32[1,1,128]{2,1,0:T(1,128)} %param.10) | copy-start | bytes 1540
  32.4 33.8 %copy-start.2 = (s32[1,1,128]{2,1,0:T(1,128)S(1)}, s32[1,1,128]{2,1,0:T(1,128)}, u32[]{:S(2)}) copy-start(s32[1,1,128]{2,1,0:T(1,128)} %param.9) | copy-start | bytes 1540
  46.9 16.9 %all-to-all-start = ((bf16[8,2,64,128]{3,2,1,0:T(8,128)(2,1)}), bf16[8,2,64,128]{3,2,1,0:T(8,128)(2,1)S(1)}, u32[]{:S(2)}, u32[]{:S(2)}) async-start(bf16[8,2,64,128]{3,2,1,0:T(8,128)(2,1)} %broadcast_in_dim.45), calls=%async_computation | async-start | bytes 524288 | tf_op jit(solution)/shard_map/all_to_all | solution.py:23
  99.0 2.8 %copy-start = (f32[128,64,128]{2,1,0:T(8,128)S(1)}, f32[128,64,128]{2,1,0:T(8,128)}, u32[]{:S(2)}) copy-start(f32[128,64,128]{2,1,0:T(8,128)} %get-tuple-element.129) | copy-start | bytes 12582916
Sparse Core Ops, SparseCore 0:
  46.1 39.8 all-gather.1
where the time goes:
time: 213 us; the launch traced here: 212 us
  blocking collectives  138 us (65%)
  other arithmetic  19.8 us (9%)
  local copies, waits for them, and re-layouts  19 us (9%)
  between operations  13.4 us (6%)
  starting transfers between devices  10.4 us (5%)
  matrix products  6.92 us (3%)
  waiting for transfers between devices  4.22 us (2%)
    psum x1, blocking collectives, per_device(): return lax.psum(upper_blocks, ROW_COL_LAYER)  101 us
    all_gather x2, blocking collectives, all_blocks(): tiles = lax.all_gather(tiles, axes[k], axis=0, tiled=True)  37.4 us
    scatter-add x2, other arithmetic, accumulate(): running.at[lax.dynamic_slice_in_dim(row_ids, first_slot, slot_block, 0)]  18.2 us
    all_to_all x1, starting transfers between devices, sent_to_all(): lax.all_to_all(jnp.broadcast_to(shard[None], (peers, *shard.shape)), axis...  10.4 us
    dynamic_slice x4, local copies, waits for them, and re-layouts, accumulate(): tile_block = lax.dynamic_slice_in_dim(tile_stack, first_slot, slot_block, 0)  7.96 us
  transfers between devices with their start and end apart: 2, of which 1 were waited for; matrix products, arithmetic and copies ran while one was open for 18% of the time, Pallas kernels for 0%

commit v1 on v0

v1 whole, which is shorter than its diff:
```python
import jax
import jax.numpy as jnp
from jax import lax
from jax.experimental import pallas as pl
from jax.experimental.pallas import tpu as pltpu
from jax.sharding import Mesh
from jax.sharding import PartitionSpec as P

TILE = 64
HALF = TILE // 2
LANES = 2 * TILE
CHUNK = 16
GROUP = 4
COL_LAYER = ("zh", "y", "zl")
Z = ("zh", "zl")
ROW_Y = ("row", "y")


def lane_swapped(x):
    return pltpu.roll(x, TILE, axis=1)


def window_kernel(cols, p_ref, rows_ref, turned_ref, sums, natural):
    local_rows, slots = cols.shape
    lane = lax.broadcasted_iota(jnp.int32, (HALF, LANES), 1)
    for t in range(local_rows):
        tiles = p_ref[t].astype(jnp.float32)
        slot = lax.broadcasted_iota(jnp.int32, tiles.shape, 0)
        for j in range(2):
            chosen = jnp.zeros(tiles.shape, jnp.bool_)
            for s in range(slots):
                chosen = chosen | ((slot == s) & (cols[t, s] == j))
            total = jnp.sum(jnp.where(chosen, tiles, 0.0), axis=0, keepdims=True)
            for k in range(HALF):
                sums[t, j, k : k + 1] = total[:, k * LANES : (k + 1) * LANES]
    stacked = []
    for t in range(local_rows):
        first, second = sums[t, 0], sums[t, 1]
        even = jnp.where(lane < TILE, first, lane_swapped(second))
        odd = jnp.where(lane < TILE, lane_swapped(first), second)
        natural[t, pl.ds(0, HALF, stride=2)] = even
        natural[t, pl.ds(1, HALF, stride=2)] = odd
        stacked += [even, odd]
    rows = natural[...].astype(jnp.bfloat16)
    turned = jnp.concatenate(stacked, axis=0).T.astype(jnp.bfloat16)
    for r in range(rows_ref.shape[0]):
        rows_ref[r] = rows
    for z in range(turned_ref.shape[0]):
        turned_ref[z] = turned


def product_kernel(rows, cols, count, a_ref, w_ref, out_ref, split, total):
    live = count[0]
    total[...] = jnp.zeros_like(total)

    def place(row):
        f = row & (TILE - 1)
        z = ((f >> 4) << 2) | (f & 3)
        return ((((f >> 2) & 3) * 16 + z) * 2) + (row >> 6)

    def chunk(turn, carry):
        first = pl.multiple_of(turn * CHUNK, CHUNK)
        tiles = a_ref[pl.ds(first, CHUNK), :].astype(jnp.float32)
        slot = first + lax.broadcasted_iota(jnp.int32, tiles.shape, 0)
        tiles = jnp.where(slot < live, tiles, 0.0)
        for k in range(HALF):
            split[k] = tiles[:, k * LANES : (k + 1) * LANES]
        for g in range(0, CHUNK, GROUP):
            parts = []
            for i in range(g, g + GROUP):
                x = split[:, i, :]
                tile = jnp.concatenate([x, lane_swapped(x)], axis=0).astype(jnp.bfloat16)
                parts.append(
                    jnp.dot(
                        tile[:, :TILE], w_ref[cols[first + i]], preferred_element_type=jnp.float32
                    )
                )
            for i in range(g, g + GROUP):
                total[place(rows[first + i])] += parts[i - g]
        return carry

    lax.fori_loop(0, (live + CHUNK - 1) // CHUNK, chunk, 0)

    def store(turn, carry):
        out_ref[turn] = total[turn].astype(jnp.bfloat16)
        return carry

    lax.fori_loop(0, total.shape[0], store, 0, unroll=8)


def contract_kernel(p_ref, turned_ref, out_ref):
    peers, pieces = p_ref.shape[0], turned_ref.shape[0]
    galerkin = jnp.zeros((LANES, LANES), jnp.float32)
    for z in range(pieces):
        block = p_ref[0, z].astype(jnp.float32)
        for peer in range(1, peers):
            block += p_ref[peer, z].astype(jnp.float32)
        high = block.astype(jnp.bfloat16)
        low = (block - high.astype(jnp.float32)).astype(jnp.bfloat16)
        w = turned_ref[z]
        galerkin += jnp.dot(w, high, preferred_element_type=jnp.float32)
        galerkin += jnp.dot(w, low, preferred_element_type=jnp.float32)
    out_ref[:TILE] = galerkin[:TILE]
    out_ref[TILE:, :TILE] = galerkin[TILE : TILE + HALF, TILE:]
    out_ref[TILE:, TILE:] = galerkin[TILE + HALF :, TILE:]


def exchanged(x, axes):
    return lax.all_to_all(x, axes, 0, 0, tiled=True)


def summed_over_all(x):
    peers, depth = lax.axis_size(ROW_Y), lax.axis_size(Z)
    pieces = exchanged(x.reshape(peers, -1, LANES), ROW_Y)
    piece = jnp.sum(pieces, axis=0)
    piece = jnp.sum(exchanged(jnp.broadcast_to(piece, (depth, *piece.shape)), Z), axis=0)
    return exchanged(jnp.broadcast_to(piece, (peers, *piece.shape)), ROW_Y).reshape(x.shape)


def per_device(a_tiles, a_rows, a_cols, a_count, p_tiles, p_cols):
    local_rows, _, slots, area = p_tiles.shape
    total_slots = a_tiles.shape[2]
    n_row, n_y, n_z = lax.axis_size("row"), lax.axis_size("y"), lax.axis_size(Z)
    vmem = pl.BlockSpec(memory_space=pltpu.VMEM)
    own_rows, own_turned = pl.pallas_call(
        window_kernel,
        out_shape=(
            jax.ShapeDtypeStruct((n_row, local_rows, TILE, LANES), jnp.bfloat16),
            jax.ShapeDtypeStruct((n_z, LANES, LANES), jnp.bfloat16),
        ),
        grid_spec=pltpu.PrefetchScalarGridSpec(
            num_scalar_prefetch=1,
            in_specs=[vmem],
            out_specs=[vmem, vmem],
            scratch_shapes=[
                pltpu.VMEM((local_rows, 2, HALF, LANES), jnp.float32),
                pltpu.VMEM((local_rows, TILE, LANES), jnp.float32),
            ],
        ),
        name="window",
    )(p_cols.reshape(local_rows, slots), p_tiles.reshape(local_rows, slots, area))
    column_window = exchanged(own_rows, "row").reshape(n_row * local_rows, TILE, LANES)
    turned = exchanged(own_turned, Z)
    places = n_y * n_z * local_rows
    product = pl.pallas_call(
        product_kernel,
        out_shape=jax.ShapeDtypeStruct((places, TILE, LANES), jnp.bfloat16),
        grid_spec=pltpu.PrefetchScalarGridSpec(
            num_scalar_prefetch=3,
            in_specs=[vmem, vmem],
            out_specs=vmem,
            scratch_shapes=[
                pltpu.VMEM((HALF, CHUNK, LANES), jnp.float32),
                pltpu.VMEM((places, TILE, LANES), jnp.float32),
            ],
        ),
        name="product",
    )(
        a_rows.reshape(total_slots),
        a_cols.reshape(total_slots),
        a_count.reshape(1),
        a_tiles.reshape(total_slots, area),
        column_window,
    )
    gathered = exchanged(product.reshape(n_y, n_z, LANES, LANES), "y")
    galerkin = pl.pallas_call(
        contract_kernel,
        out_shape=jax.ShapeDtypeStruct((TILE + HALF, LANES), jnp.float32),
        in_specs=[vmem, vmem],
        out_specs=vmem,
        name="contract",
    )(gathered, turned)
    total = summed_over_all(galerkin)
    corner = jnp.concatenate([total[TILE:, :TILE], total[TILE:, TILE:]], axis=0)
    return jnp.concatenate([total[:TILE], corner], axis=1)


def solution(mesh):
    torus = Mesh(
        mesh.devices.reshape(mesh.shape["row"], 4, 4, mesh.shape["layer"]),
        ("row", "zh", "y", "zl"),
    )
    in_specs = (
        P("row", COL_LAYER, None, None),
        P("row", COL_LAYER, None),
        P("row", COL_LAYER, None),
        P("row", COL_LAYER),
        P("row", COL_LAYER, None, None),
        P("row", COL_LAYER, None),
    )
    return jax.shard_map(
        per_device, mesh=torus, in_specs=in_specs, out_specs=P(), check_vma=False
    )
```

time: 213 us -> 143 us (0.67)
  blocking collectives: 138 us -> 113 us
  other arithmetic: 19.8 us -> 0.71 us
  local copies, waits for them, and re-layouts: 19 us -> 1.64 us
  between operations: 13.4 us -> 0.68 us
  Pallas kernels: 0 us -> 10.5 us
  matrix products: 6.92 us -> 0 us
    all_to_all x0 -> x5, blocking collectives: none -> 113 us  [exchanged(): return lax.all_to_all(x, axes, 0, 0, tiled=True)]
    psum x1 -> x0, blocking collectives: 101 us -> none  [per_device(): return lax.psum(upper_blocks, ROW_COL_LAYER)]
    all_gather x2 -> x0, blocking collectives: 37.4 us -> none  [all_blocks(): tiles = lax.all_gather(tiles, axes[k], axis=0, tiled=True)]
    scatter-add x2 -> x0, other arithmetic: 18.2 us -> none  [accumulate(): running.at[lax.dynamic_slice_in_dim(row_ids, first_slot, slot_block, 0)]]
    pallas_call x0 -> x3, Pallas kernels: none -> 10.5 us  [the longest x1 4.92 us: per_device(): pl.pallas_call(product_kernel, out_shape=jax.ShapeDtypeStruct((places, TI...]
    dynamic_slice x4 -> x0, local copies, waits for them, and re-layouts: 7.96 us -> none  [accumulate(): tile_block = lax.dynamic_slice_in_dim(tile_stack, first_slot, slot_block, 0)]
    dot_general x4 -> x0, matrix products: 6.92 us -> none  [the longest x2 3.44 us: accumulate(): jnp.einsum('sab,sbc->sac', tile_block, picked, preferred_element_type=jnp...]
    broadcast_in_dim x2, local copies, waits for them, and re-layouts: 3.23 us -> 0.02 us  [the longest x1 0.01 us: summed_over_all(): jnp.broadcast_to(piece, (peers, *piece.shape))]
  transfers between devices with their start and end apart: 2 -> 1, of which waited for: 1 -> 1; matrix products, arithmetic and copies ran while one was open for 18% -> 0% of each run, Pallas kernels for 0% -> 0%
where the time goes in v1:
time: 143 us; the launch traced here: 142 us
  blocking collectives  113 us (79%)
  Pallas kernels  10.5 us (7%)
  starting transfers between devices  10.2 us (7%)
  waiting for transfers between devices  5.84 us (4%)
  local copies, waits for them, and re-layouts  1.64 us (1%)
    all_to_all x5, blocking collectives, exchanged(): return lax.all_to_all(x, axes, 0, 0, tiled=True)  113 us
    all_to_all x1, starting transfers between devices, exchanged(): return lax.all_to_all(x, axes, 0, 0, tiled=True)  10.2 us
    all_to_all x1, waiting for transfers between devices, exchanged(): return lax.all_to_all(x, axes, 0, 0, tiled=True)  5.84 us
    pallas_call x1, Pallas kernels, per_device(): pl.pallas_call(product_kernel, out_shape=jax.ShapeDtypeStruct((places, TI...  4.92 us
    pallas_call x1, Pallas kernels, per_device(): pl.pallas_call(contract_kernel, out_shape=jax.ShapeDtypeStruct((TILE + HA...  2.91 us
  transfers between devices with their start and end apart: 1, of which 1 were waited for; matrix products, arithmetic and copies ran while one was open for 0% of the time, Pallas kernels for 0%

profile of v1, /device:TPU:1, one launch (start us, length us, event | category | flops | bytes accessed | tf_op | source)
XLA Modules:
  0.0 142.1 jit_solution(10975973803881300689)
XLA Ops:
  0.0 2.7 %window.1 = (bf16[8,2,64,128]{3,2,1,0:T(8,128)(2,1)}, bf16[16,128,128]{2,1,0:T(8,128)(2,1)}) custom-call(s32[2,4]{1,0:T(2,128)} %bitcast.13, bf16[2,4,4096]{2,1,0:T(4,128)(2,1)} %bitcast.12), custom_call_target="tpu_custom_call" | custom-call | tf_op jit(solution)/shard_map/window/pallas_call | solution.py:125
  2.7 10.2 %all-to-all-start = ((bf16[8,2,64,128]{3,2,1,0:T(8,128)(2,1)}), bf16[8,2,64,128]{3,2,1,0:T(8,128)(2,1)S(1)}, u32[]{:S(2)}, u32[]{:S(2)}) async-start(bf16[8,2,64,128]{3,2,1,0:T(8,128)(2,1)} %get-tuple-element.7), calls=%async_computation | async-start | bytes 524288 | tf_op jit(solution)/shard_map/all_to_all | solution.py:109
  13.5 5.8 %all-to-all-done = bf16[8,2,64,128]{3,2,1,0:T(8,128)(2,1)S(1)} async-done(((bf16[8,2,64,128]{3,2,1,0:T(8,128)(2,1)}), bf16[8,2,64,128]{3,2,1,0:T(8,128)(2,1)S(1)}, u32[]{:S(2)}, u32[]{:S(2)}) %all-to-all-start) | async-done | bytes 262176 | tf_op jit(solution)/shard_map/all_to_all | solution.py:109
  19.3 0.0 copy-start
  19.3 0.7 copy-done
  20.0 4.9 %product.1 = bf16[128,64,128]{2,1,0:T(8,128)(2,1)} custom-call(s32[128]{0:T(128)} %bitcast.14, s32[128]{0:T(128)} %bitcast.15, s32[1]{0:T(128)} %bitcast.8.count, bf16[128,4096]{1,0:T(8,128)(2,1)} %bitcast.10, bf16[16,64,128]{2,1,0:T(8,128)(2,1)} %bitcast.11), custom_call_target="tpu_custom_call" | custom-call | tf_op jit(solution)/shard_map/product/pallas_call | solution.py:145
  24.9 0.0 copy-start.1
  24.9 30.0 %all_to_all.30.p_ref = bf16[4,16,128,128]{3,2,1,0:T(8,128)(2,1)} all-to-all(bf16[4,16,128,128]{3,2,1,0:T(8,128)(2,1)} %bitcast.9), channel_id=1, replica_groups=mesh['row'=8,'zh'=4,'y'=4,'zl'=4] {'y'}, dimensions={0} | all-to-all | bytes 4194304 | tf_op jit(solution)/shard_map/all_to_all | solution.py:109
  55.0 0.0 copy-done.1
  55.0 32.2 %all_to_all.31.turned_ref = bf16[16,128,128]{2,1,0:T(8,128)(2,1)} all-to-all(bf16[16,128,128]{2,1,0:T(8,128)(2,1)S(1)} %copy-done.1), channel_id=1, replica_groups=mesh['row'=8,'zh'=4,'y'=4,'zl'=4] {'zh','zl'}, dimensions={0} | all-to-all | bytes 1048576 | tf_op jit(solution)/shard_map/all_to_all | solution.py:109
  87.2 2.9 %contract.1 = f32[96,128]{1,0:T(8,128)} custom-call(bf16[4,16,128,128]{3,2,1,0:T(8,128)(2,1)} %all_to_all.30.p_ref, bf16[16,128,128]{2,1,0:T(8,128)(2,1)} %all_to_all.31.turned_ref), custom_call_target="tpu_custom_call" | custom-call | tf_op jit(solution)/shard_map/contract/pallas_call | solution.py:166
  90.1 0.8 reshape.38
  90.9 20.6 %all_to_all.32 = f32[32,3,128]{2,1,0:T(4,128)S(1)} all-to-all(f32[32,3,128]{2,1,0:T(4,128)S(1)} %reshape.38), channel_id=1, replica_groups=mesh['row'=8,'zh'=4,'y'=4,'zl'=4] {'row','y'}, dimensions={0} | all-to-all | bytes 98304 | tf_op jit(solution)/shard_map/all_to_all | solution.py:109
  111.6 17.4 %all_to_all.33 = f32[16,3,128]{2,1,0:T(4,128)S(1)} all-to-all(f32[16,3,128]{2,1,0:T(4,128)S(1)} %broadcast_in_dim.6), channel_id=1, replica_groups=mesh['row'=8,'zh'=4,'y'=4,'zl'=4] {'zh','zl'}, dimensions={0} | all-to-all | bytes 49152 | tf_op jit(solution)/shard_map/all_to_all | solution.py:109
  129.0 12.3 %all_to_all.34 = f32[32,3,128]{2,1,0:T(4,128)S(1)} all-to-all(f32[32,3,128]{2,1,0:T(4,128)S(1)} %broadcast_in_dim.7), channel_id=1, replica_groups=mesh['row'=8,'zh'=4,'y'=4,'zl'=4] {'row','y'}, dimensions={0} | all-to-all | bytes 98304 | tf_op jit(solution)/shard_map/all_to_all | solution.py:109
  141.4 0.1 fusion
  141.5 0.6 maximum_maximum_fusion
  (6 shorter events, 0.1 us)
Async XLA Ops:
  2.7 16.6 %all-to-all-start = ((bf16[8,2,64,128]{3,2,1,0:T(8,128)(2,1)}), bf16[8,2,64,128]{3,2,1,0:T(8,128)(2,1)S(1)}, u32[]{:S(2)}, u32[]{:S(2)}) async-start(bf16[8,2,64,128]{3,2,1,0:T(8,128)(2,1)} %get-tuple-element.7), calls=%async_computation | async-start | bytes 524288 | tf_op jit(solution)/shard_map/all_to_all | solution.py:109
  19.3 0.7 copy-start
  24.9 30.0 %copy-start.1 = (bf16[16,128,128]{2,1,0:T(8,128)(2,1)S(1)}, bf16[16,128,128]{2,1,0:T(8,128)(2,1)}, u32[]{:S(2)}) copy-start(bf16[16,128,128]{2,1,0:T(8,128)(2,1)} %get-tuple-element.8) | copy-start | bytes 1572868

commit v2 on v1

--- a/solution.py
+++ b/solution.py
@@ -14,6 +14,7 @@
 COL_LAYER = ("zh", "y", "zl")
 Z = ("zh", "zl")
 ROW_Y = ("row", "y")
+Y_ORDER = (1, 3, 2)
 
 
 def lane_swapped(x):
@@ -49,14 +50,16 @@
         turned_ref[z] = turned
 
 
-def product_kernel(rows, cols, count, a_ref, w_ref, out_ref, split, total):
+def product_kernel(rows, cols, count, own_y, a_ref, w_ref, *refs):
+    *out_refs, split, total = refs
     live = count[0]
     total[...] = jnp.zeros_like(total)
 
     def place(row):
         f = row & (TILE - 1)
         z = ((f >> 4) << 2) | (f & 3)
-        return ((((f >> 2) & 3) * 16 + z) * 2) + (row >> 6)
+        distance = ((f >> 2) - own_y[0]) & 3
+        return (distance * 16 + z) * 2 + (row >> 6)
 
     def chunk(turn, carry):
         first = pl.multiple_of(turn * CHUNK, CHUNK)
@@ -81,20 +84,21 @@
 
     lax.fori_loop(0, (live + CHUNK - 1) // CHUNK, chunk, 0)
 
-    def store(turn, carry):
-        out_ref[turn] = total[turn].astype(jnp.bfloat16)
-        return carry
-
-    lax.fori_loop(0, total.shape[0], store, 0, unroll=8)
-
-
-def contract_kernel(p_ref, turned_ref, out_ref):
-    peers, pieces = p_ref.shape[0], turned_ref.shape[0]
+    for distance, out_ref in enumerate(out_refs):
+
+        def store(turn, carry, out_ref=out_ref, first=distance * out_ref.shape[0]):
+            out_ref[turn] = total[first + turn].astype(out_ref.dtype)
+            return carry
+
+        lax.fori_loop(0, out_ref.shape[0], store, 0, unroll=8)
+
+
+def contract_kernel(*refs):
+    *p_refs, turned_ref, out_ref = refs
+    pieces = turned_ref.shape[0]
     galerkin = jnp.zeros((LANES, LANES), jnp.float32)
     for z in range(pieces):
-        block = p_ref[0, z].astype(jnp.float32)
-        for peer in range(1, peers):
-            block += p_ref[peer, z].astype(jnp.float32)
+        block = sum(p_ref[z].astype(jnp.float32) for p_ref in p_refs)
         high = block.astype(jnp.bfloat16)
         low = (block - high.astype(jnp.float32)).astype(jnp.bfloat16)
         w = turned_ref[z]
@@ -117,7 +121,7 @@
     return exchanged(jnp.broadcast_to(piece, (peers, *piece.shape)), ROW_Y).reshape(x.shape)
 
 
-def per_device(a_tiles, a_rows, a_cols, a_count, p_tiles, p_cols):
+def coarse_blocks(a_tiles, a_rows, a_cols, a_count, p_tiles, p_cols):
     local_rows, _, slots, area = p_tiles.shape
     total_slots = a_tiles.shape[2]
     n_row, n_y, n_z = lax.axis_size("row"), lax.axis_size("y"), lax.axis_size(Z)
@@ -141,17 +145,20 @@
     )(p_cols.reshape(local_rows, slots), p_tiles.reshape(local_rows, slots, area))
     column_window = exchanged(own_rows, "row").reshape(n_row * local_rows, TILE, LANES)
     turned = exchanged(own_turned, Z)
-    places = n_y * n_z * local_rows
-    product = pl.pallas_call(
+    places = n_z * local_rows
+    products = pl.pallas_call(
         product_kernel,
-        out_shape=jax.ShapeDtypeStruct((places, TILE, LANES), jnp.bfloat16),
+        out_shape=[
+            jax.ShapeDtypeStruct((places, TILE, LANES), jnp.bfloat16 if distance else jnp.float32)
+            for distance in range(n_y)
+        ],
         grid_spec=pltpu.PrefetchScalarGridSpec(
-            num_scalar_prefetch=3,
+            num_scalar_prefetch=4,
             in_specs=[vmem, vmem],
-            out_specs=vmem,
+            out_specs=[vmem] * n_y,
             scratch_shapes=[
                 pltpu.VMEM((HALF, CHUNK, LANES), jnp.float32),
-                pltpu.VMEM((places, TILE, LANES), jnp.float32),
+                pltpu.VMEM((n_y * places, TILE, LANES), jnp.float32),
             ],
         ),
         name="product",
@@ -159,17 +166,26 @@
         a_rows.reshape(total_slots),
         a_cols.reshape(total_slots),
         a_count.reshape(1),
+        lax.axis_index("y").reshape(1),
         a_tiles.reshape(total_slots, area),
         column_window,
     )
-    gathered = exchanged(product.reshape(n_y, n_z, LANES, LANES), "y")
+    gathered = [products[0].reshape(n_z, LANES, LANES)]
+    for distance in Y_ORDER:
+        gathered.append(
+            lax.ppermute(
+                products[distance].reshape(n_z, LANES, LANES),
+                "y",
+                [(y, (y + distance) % n_y) for y in range(n_y)],
+            )
+        )
     galerkin = pl.pallas_call(
         contract_kernel,
         out_shape=jax.ShapeDtypeStruct((TILE + HALF, LANES), jnp.float32),
-        in_specs=[vmem, vmem],
+        in_specs=[vmem] * (n_y + 1),
         out_specs=vmem,
         name="contract",
-    )(gathered, turned)
+    )(*gathered, turned)
     total = summed_over_all(galerkin)
     corner = jnp.concatenate([total[TILE:, :TILE], total[TILE:, TILE:]], axis=0)
     return jnp.concatenate([total[:TILE], corner], axis=1)
@@ -189,5 +205,5 @@
         P("row", COL_LAYER, None),
     )
     return jax.shard_map(
-        per_device, mesh=torus, in_specs=in_specs, out_specs=P(), check_vma=False
-    )
+        coarse_blocks, mesh=torus, in_specs=in_specs, out_specs=P(), check_vma=False
+    )

time: 143 us -> 122 us (0.85)
  blocking collectives: 113 us -> 68.5 us
  waiting for transfers between devices: 5.84 us -> 18.2 us
  starting transfers between devices: 10.2 us -> 20 us
    all_to_all x5 -> x4, blocking collectives: 113 us -> 68.5 us  [exchanged(): return lax.all_to_all(x, axes, 0, 0, tiled=True)]
    ppermute x0 -> x3, waiting for transfers between devices: none -> 18.2 us  [coarse_blocks(): lax.ppermute(products[distance].reshape(n_z, LANES, LANES), 'y', [(y, (y...]
    ppermute x0 -> x3, starting transfers between devices: none -> 10.1 us  [coarse_blocks(): lax.ppermute(products[distance].reshape(n_z, LANES, LANES), 'y', [(y, (y...]
    all_to_all x1, waiting for transfers between devices: 5.84 us -> 0.01 us  [exchanged(): return lax.all_to_all(x, axes, 0, 0, tiled=True)]
  transfers between devices with their start and end apart: 1 -> 4, of which waited for: 1 -> 3; matrix products, arithmetic and copies ran while one was open for 0% -> 0% of each run, Pallas kernels for 0% -> 4%
where the time goes in v2:
time: 122 us; the launch traced here: 121 us
  blocking collectives  68.5 us (56%)
  starting transfers between devices  20 us (16%)
  waiting for transfers between devices  18.2 us (15%)
  Pallas kernels  10.8 us (9%)
  local copies, waits for them, and re-layouts  1.97 us (2%)
    all_to_all x4, blocking collectives, exchanged(): return lax.all_to_all(x, axes, 0, 0, tiled=True)  68.5 us
    ppermute x3, waiting for transfers between devices, coarse_blocks(): lax.ppermute(products[distance].reshape(n_z, LANES, LANES), 'y', [(y, (y...  18.2 us
    ppermute x3, starting transfers between devices, coarse_blocks(): lax.ppermute(products[distance].reshape(n_z, LANES, LANES), 'y', [(y, (y...  10.1 us
    all_to_all x1, starting transfers between devices, exchanged(): return lax.all_to_all(x, axes, 0, 0, tiled=True)  9.95 us
    pallas_call x1, Pallas kernels, coarse_blocks(): pl.pallas_call(product_kernel, out_shape=[jax.ShapeDtypeStruct((places, T...  5.09 us
    pallas_call x1, Pallas kernels, coarse_blocks(): pl.pallas_call(contract_kernel, out_shape=jax.ShapeDtypeStruct((TILE + HA...  2.99 us
    pallas_call x1, Pallas kernels, coarse_blocks(): pl.pallas_call(window_kernel, out_shape=(jax.ShapeDtypeStruct((n_row, loc...  2.68 us
  transfers between devices with their start and end apart: 4, of which 3 were waited for; matrix products, arithmetic and copies ran while one was open for 0% of the time, Pallas kernels for 4%

profile of v2, /device:TPU:1, one launch (start us, length us, event | category | flops | bytes accessed | tf_op | source)
XLA Modules:
  0.0 120.9 jit_solution(6131727886258530489)
XLA Ops:
  0.0 2.7 %window.1 = (bf16[8,2,64,128]{3,2,1,0:T(8,128)(2,1)}, bf16[16,128,128]{2,1,0:T(8,128)(2,1)}) custom-call(s32[2,4]{1,0:T(2,128)} %bitcast.17, bf16[2,4,4096]{2,1,0:T(4,128)(2,1)} %bitcast.16), custom_call_target="tpu_custom_call" | custom-call | tf_op jit(solution)/shard_map/window/pallas_call | solution.py:129
  2.7 17.3 %all_to_all.25 = bf16[8,2,64,128]{3,2,1,0:T(8,128)(2,1)} all-to-all(bf16[8,2,64,128]{3,2,1,0:T(8,128)(2,1)} %get-tuple-element.11), channel_id=1, replica_groups=mesh['row'=8,'zh'=4,'y'=4,'zl'=4] {'row'}, dimensions={0} | all-to-all | bytes 524288 | tf_op jit(solution)/shard_map/all_to_all | solution.py:113
  20.0 9.9 %all-to-all-start.1 = ((bf16[16,128,128]{2,1,0:T(8,128)(2,1)}), bf16[16,128,128]{2,1,0:T(8,128)(2,1)S(1)}, u32[]{:S(2)}, u32[]{:S(2)}) async-start(bf16[16,128,128]{2,1,0:T(8,128)(2,1)} %get-tuple-element.16), calls=%async_computation.1 | async-start | bytes 1048576 | tf_op jit(solution)/shard_map/all_to_all | solution.py:113
  30.6 5.1 %product.1 = (f32[32,64,128]{2,1,0:T(8,128)}, bf16[32,64,128]{2,1,0:T(8,128)(2,1)}, bf16[32,64,128]{2,1,0:T(8,128)(2,1)}, bf16[32,64,128]{2,1,0:T(8,128)(2,1)}) custom-call(s32[128]{0:T(128)} %bitcast.18, s32[128]{0:T(128)} %bitcast.19, s32[1]{0:T(128)} %bitcast.12.count, s32[1]{0:T(128)} %bitcast.3.own_y, bf16[128,4096]{1,0:T(8,128)(2,1)} %bitcast.14, ...), custom_call_target="tpu_custom_call" | custom-call | tf_op jit(solution)/shard_map/product/pallas_call | solution.py:149
  35.7 2.8 %collective-permute-start = (bf16[16,128,128]{2,1,0:T(8,128)(2,1)}, bf16[16,128,128]{2,1,0:T(8,128)(2,1)S(1)}, u32[]{:S(2)}, u32[]{:S(2)}) collective-permute-start(bf16[16,128,128]{2,1,0:T(8,128)(2,1)} %bitcast.22), channel_id=1, source_target_pairs={{0,4},{4,8},{8,12},{12,0},{1,5},{5,9},{9,13},{13,1},{2,6},{6,10},{... | collective-permute-start | bytes 1572872 | tf_op jit(solution)/shard_map/ppermute | solution.py:176
  38.5 3.7 %collective-permute-start.1 = (bf16[16,128,128]{2,1,0:T(8,128)(2,1)}, bf16[16,128,128]{2,1,0:T(8,128)(2,1)S(1)}, u32[]{:S(2)}, u32[]{:S(2)}) collective-permute-start(bf16[16,128,128]{2,1,0:T(8,128)(2,1)} %bitcast.21), channel_id=1, source_target_pairs={{0,12},{4,0},{8,4},{12,8},{1,13},{5,1},{9,5},{13,9},{2,14},{6,2},{... | collective-permute-start | bytes 1572872 | tf_op jit(solution)/shard_map/ppermute | solution.py:176
  42.3 3.5 %collective-permute-start.2 = (bf16[16,128,128]{2,1,0:T(8,128)(2,1)}, bf16[16,128,128]{2,1,0:T(8,128)(2,1)S(1)}, u32[]{:S(2)}, u32[]{:S(2)}) collective-permute-start(bf16[16,128,128]{2,1,0:T(8,128)(2,1)} %bitcast.20), channel_id=1, source_target_pairs={{0,8},{4,12},{8,0},{12,4},{1,9},{5,13},{9,1},{13,5},{2,10},{6,14},... | collective-permute-start | bytes 1572872 | tf_op jit(solution)/shard_map/ppermute | solution.py:176
  45.8 5.1 %collective-permute-done.refs_1_ = bf16[16,128,128]{2,1,0:T(8,128)(2,1)S(1)} collective-permute-done((bf16[16,128,128]{2,1,0:T(8,128)(2,1)}, bf16[16,128,128]{2,1,0:T(8,128)(2,1)S(1)}, u32[]{:S(2)}, u32[]{:S(2)}) %collective-permute-start) | collective-permute-done | bytes 524320 | tf_op jit(solution)/shard_map/ppermute | solution.py:176
  50.9 0.0 copy-start.1
  50.9 2.0 %collective-permute-done.1.refs_2_ = bf16[16,128,128]{2,1,0:T(8,128)(2,1)S(1)} collective-permute-done((bf16[16,128,128]{2,1,0:T(8,128)(2,1)}, bf16[16,128,128]{2,1,0:T(8,128)(2,1)S(1)}, u32[]{:S(2)}, u32[]{:S(2)}) %collective-permute-start.1) | collective-permute-done | bytes 524320 | tf_op jit(solution)/shard_map/ppermute | solution.py:176
  53.0 0.0 copy-start.2
  53.0 11.1 %collective-permute-done.2.refs_3_ = bf16[16,128,128]{2,1,0:T(8,128)(2,1)S(1)} collective-permute-done((bf16[16,128,128]{2,1,0:T(8,128)(2,1)}, bf16[16,128,128]{2,1,0:T(8,128)(2,1)S(1)}, u32[]{:S(2)}, u32[]{:S(2)}) %collective-permute-start.2) | collective-permute-done | bytes 524320 | tf_op jit(solution)/shard_map/ppermute | solution.py:176
  64.0 0.0 copy-start.3
  64.0 0.0 all-to-all-done.1.refs_4_
  64.0 0.0 copy-start
  64.0 0.0 copy-done.1
  64.0 0.0 copy-done.2
  64.1 0.8 copy-done.3
  64.8 0.2 copy-done
  65.1 3.0 %contract.1 = f32[96,128]{1,0:T(8,128)} custom-call(f32[16,128,128]{2,1,0:T(8,128)} %bitcast.13, bf16[16,128,128]{2,1,0:T(8,128)(2,1)} %copy-done.1, bf16[16,128,128]{2,1,0:T(8,128)(2,1)} %copy-done.2, bf16[16,128,128]{2,1,0:T(8,128)(2,1)} %copy-done.3, bf16[16,128,128]{2,1,0:T(8,128)(2,1)} %copy-done), custom_call_target="tpu_custom_call" | custom-call | tf_op jit(solution)/shard_map/contract/pallas_call | solution.py:182
  68.1 0.8 reshape.54
  68.9 15.2 %all_to_all.26 = f32[32,3,128]{2,1,0:T(4,128)S(1)} all-to-all(f32[32,3,128]{2,1,0:T(4,128)S(1)} %reshape.54), channel_id=1, replica_groups=mesh['row'=8,'zh'=4,'y'=4,'zl'=4] {'row','y'}, dimensions={0} | all-to-all | bytes 98304 | tf_op jit(solution)/shard_map/all_to_all | solution.py:113
  84.1 23.6 %all_to_all.27 = f32[16,3,128]{2,1,0:T(4,128)S(1)} all-to-all(f32[16,3,128]{2,1,0:T(4,128)S(1)} %broadcast_in_dim.6), channel_id=1, replica_groups=mesh['row'=8,'zh'=4,'y'=4,'zl'=4] {'zh','zl'}, dimensions={0} | all-to-all | bytes 49152 | tf_op jit(solution)/shard_map/all_to_all | solution.py:113
  107.8 12.3 %all_to_all.28 = f32[32,3,128]{2,1,0:T(4,128)S(1)} all-to-all(f32[32,3,128]{2,1,0:T(4,128)S(1)} %broadcast_in_dim.7), channel_id=1, replica_groups=mesh['row'=8,'zh'=4,'y'=4,'zl'=4] {'row','y'}, dimensions={0} | all-to-all | bytes 98304 | tf_op jit(solution)/shard_map/all_to_all | solution.py:113
  120.2 0.1 fusion
  120.2 0.6 maximum_maximum_fusion
  (6 shorter events, 0.1 us)
Async XLA Ops:
  20.0 44.0 %all-to-all-start.1 = ((bf16[16,128,128]{2,1,0:T(8,128)(2,1)}), bf16[16,128,128]{2,1,0:T(8,128)(2,1)S(1)}, u32[]{:S(2)}, u32[]{:S(2)}) async-start(bf16[16,128,128]{2,1,0:T(8,128)(2,1)} %get-tuple-element.16), calls=%async_computation.1 | async-start | bytes 1048576 | tf_op jit(solution)/shard_map/all_to_all | solution.py:113
  35.7 15.2 %collective-permute-start = (bf16[16,128,128]{2,1,0:T(8,128)(2,1)}, bf16[16,128,128]{2,1,0:T(8,128)(2,1)S(1)}, u32[]{:S(2)}, u32[]{:S(2)}) collective-permute-start(bf16[16,128,128]{2,1,0:T(8,128)(2,1)} %bitcast.22), channel_id=1, source_target_pairs={{0,4},{4,8},{8,12},{12,0},{1,5},{5,9},{9,13},{13,1},{2,6},{6,10},{... | collective-permute-start | bytes 1572872 | tf_op jit(solution)/shard_map/ppermute | solution.py:176
  38.5 14.4 %collective-permute-start.1 = (bf16[16,128,128]{2,1,0:T(8,128)(2,1)}, bf16[16,128,128]{2,1,0:T(8,128)(2,1)S(1)}, u32[]{:S(2)}, u32[]{:S(2)}) collective-permute-start(bf16[16,128,128]{2,1,0:T(8,128)(2,1)} %bitcast.21), channel_id=1, source_target_pairs={{0,12},{4,0},{8,4},{12,8},{1,13},{5,1},{9,5},{13,9},{2,14},{6,2},{... | collective-permute-start | bytes 1572872 | tf_op jit(solution)/shard_map/ppermute | solution.py:176
  42.3 21.8 %collective-permute-start.2 = (bf16[16,128,128]{2,1,0:T(8,128)(2,1)}, bf16[16,128,128]{2,1,0:T(8,128)(2,1)S(1)}, u32[]{:S(2)}, u32[]{:S(2)}) collective-permute-start(bf16[16,128,128]{2,1,0:T(8,128)(2,1)} %bitcast.20), channel_id=1, source_target_pairs={{0,8},{4,12},{8,0},{12,4},{1,9},{5,13},{9,1},{13,5},{2,10},{6,14},... | collective-permute-start | bytes 1572872 | tf_op jit(solution)/shard_map/ppermute | solution.py:176
  50.9 13.1 %copy-start.1 = (bf16[16,128,128]{2,1,0:T(8,128)(2,1)}, bf16[16,128,128]{2,1,0:T(8,128)(2,1)S(1)}, u32[]{:S(2)}) copy-start(bf16[16,128,128]{2,1,0:T(8,128)(2,1)S(1)} %collective-permute-done.refs_1_) | copy-start | bytes 1572868
  53.0 11.1 %copy-start.2 = (bf16[16,128,128]{2,1,0:T(8,128)(2,1)}, bf16[16,128,128]{2,1,0:T(8,128)(2,1)S(1)}, u32[]{:S(2)}) copy-start(bf16[16,128,128]{2,1,0:T(8,128)(2,1)S(1)} %collective-permute-done.1.refs_2_) | copy-start | bytes 1572868
  64.0 0.8 copy-start.3
  64.0 1.0 copy-start

commit v3 on v1

v3 whole, which is shorter than its diff:
```python
import jax
import jax.numpy as jnp
from jax import lax
from jax.experimental import pallas as pl
from jax.experimental.pallas import tpu as pltpu
from jax.sharding import Mesh
from jax.sharding import PartitionSpec as P

TILE = 64
HALF = TILE // 2
LANES = 2 * TILE
CHUNK = 16
GROUP = 4
COL_LAYER = ("zh", "y", "zl")
Z = ("zh", "zl")
ROW_Y = ("row", "y")
FAR = (0, 8, 4, 12)
NEAR = (0, 1, 15, 2)
VMEM = pl.BlockSpec(memory_space=pltpu.VMEM)
ANY = pl.BlockSpec(memory_space=pl.ANY)


def lane_swapped(x):
    return pltpu.roll(x, TILE, axis=1)


def window_kernel(cols, p_ref, rows_ref, turned_ref, split, natural):
    local_rows, slots = cols.shape
    lane = lax.broadcasted_iota(jnp.int32, (HALF, LANES), 1)
    panel = lax.broadcasted_iota(jnp.int32, (8, slots), 0)
    slot = lax.broadcasted_iota(jnp.int32, (8, slots), 1)
    stacked = []
    for t in range(local_rows):
        chosen = jnp.zeros((8, slots), jnp.float32)
        for s in range(slots):
            chosen = jnp.where((slot == s) & (panel == cols[t, s]), 1.0, chosen)
        sums = jnp.dot(chosen.astype(jnp.bfloat16), p_ref[t], preferred_element_type=jnp.float32)
        for k in range(HALF):
            split[t, k] = sums[:, k * LANES : (k + 1) * LANES]
        first, second = split[t, :, 0, :], split[t, :, 1, :]
        even = jnp.where(lane < TILE, first, lane_swapped(second))
        odd = jnp.where(lane < TILE, lane_swapped(first), second)
        natural[t, pl.ds(0, HALF, stride=2)] = even
        natural[t, pl.ds(1, HALF, stride=2)] = odd
        stacked += [even, odd]
    rows = natural[...].astype(jnp.bfloat16)
    for r in range(rows_ref.shape[0]):
        rows_ref[r] = rows
    turned_ref[0] = jnp.concatenate(stacked, axis=0).T.astype(jnp.bfloat16)


def unfold_kernel(count, a_ref, out_ref, split):
    first = pl.program_id(0) * CHUNK
    tiles = a_ref[...].astype(jnp.float32)
    slot = first + lax.broadcasted_iota(jnp.int32, tiles.shape, 0)
    tiles = jnp.where(slot < count[0], tiles, 0.0)
    for k in range(HALF):
        split[k] = tiles[:, k * LANES : (k + 1) * LANES]
    for i in range(CHUNK):
        x = split[:, i, :]
        out_ref[i] = jnp.concatenate([x, lane_swapped(x)], axis=0).astype(jnp.bfloat16)


def product_kernel(rows, cols, count, a_ref, w_hbm, out_hbm, window, total, rounded, w_sem, sems):
    step = pl.program_id(0)
    first = step * CHUNK
    w_copy = pltpu.make_async_copy(w_hbm, window, w_sem)

    @pl.when(step == 0)
    def _():
        w_copy.start()
        total[...] = jnp.zeros_like(total)
        w_copy.wait()

    def place(row):
        f = row & (TILE - 1)
        block = (((f >> 2) & 3) * 4 + (f & 3)) * 4 + (f >> 4)
        return block * 2 + (row >> 6)

    @pl.when(first < count[0])
    def _():
        for g in range(0, CHUNK, GROUP):
            parts = [
                jnp.dot(
                    a_ref[i, :, :TILE],
                    window[cols[first + i]],
                    preferred_element_type=jnp.float32,
                )
                for i in range(g, g + GROUP)
            ]
            for i in range(g, g + GROUP):
                total[place(rows[first + i])] += parts[i - g]

    @pl.when(step == pl.num_programs(0) - 1)
    def _():
        copies = []
        peers, size = out_hbm.shape[0], out_hbm.shape[1]
        for y in range(peers):

            def store(turn, carry, y=y):
                rounded[y, turn] = total[y * size + turn].astype(jnp.bfloat16)
                return carry

            lax.fori_loop(0, size, store, 0, unroll=8)
            copies.append(pltpu.make_async_copy(rounded.at[y], out_hbm.at[y], sems.at[y]))
            copies[-1].start()
        for copy in copies:
            copy.wait()


def contract_kernel(own_z, p_hbm, *refs):
    *w_hbm, out_ref, p_buf, w_buf, p_sems, w_sems = refs
    copies = []
    for near, w in enumerate(w_hbm):
        zl = (own_z[0] - NEAR[near]) & 3
        source = p_hbm.at[:, pl.ds(zl * 4, 4)]
        copies.append(
            (
                pltpu.make_async_copy(source, p_buf.at[near], p_sems.at[near]),
                pltpu.make_async_copy(w, w_buf.at[near], w_sems.at[near]),
            )
        )
        for copy in copies[-1]:
            copy.start()
    galerkin = jnp.zeros((LANES, LANES), jnp.float32)
    for near in range(len(w_hbm)):
        for copy in copies[near]:
            copy.wait()
        for far in range(len(FAR)):
            zh = ((own_z[0] - NEAR[near] - FAR[far]) >> 2) & 3
            block = sum(
                p_buf[near, y, zh].astype(jnp.float32) for y in range(p_buf.shape[1])
            )
            high = block.astype(jnp.bfloat16)
            low = (block - high.astype(jnp.float32)).astype(jnp.bfloat16)
            w = w_buf[near, far]
            galerkin += jnp.dot(w, high, preferred_element_type=jnp.float32)
            galerkin += jnp.dot(w, low, preferred_element_type=jnp.float32)
    out_ref[:, 0, :] = galerkin[:HALF]
    out_ref[:, 1, :] = galerkin[HALF:TILE]
    corner = galerkin[TILE:]
    lane = lax.broadcasted_iota(jnp.int32, (HALF, LANES), 1)
    out_ref[:, 2, :] = jnp.where(lane < TILE, lane_swapped(corner[:HALF]), corner[HALF:])


def exchanged(x, axes):
    return lax.all_to_all(x, axes, 0, 0, tiled=True)


def moved_along_z(x, distance):
    depth = lax.axis_size(Z)
    return lax.ppermute(x, Z, [(z, (z + distance) % depth) for z in range(depth)])


def summed_over_all(x):
    peers, depth = lax.axis_size(ROW_Y), lax.axis_size(Z)
    piece = jnp.sum(exchanged(x, ROW_Y), axis=0)
    piece = jnp.sum(exchanged(jnp.broadcast_to(piece, (depth, *piece.shape)), Z), axis=0)
    return exchanged(jnp.broadcast_to(piece, (peers, *piece.shape)), ROW_Y)


def coarse_blocks(a_tiles, a_rows, a_cols, a_count, p_tiles, p_cols):
    local_rows, _, slots, area = p_tiles.shape
    total_slots = a_tiles.shape[2]
    n_row, n_y = lax.axis_size("row"), lax.axis_size("y")
    count = a_count.reshape(1)
    own_rows, own_turned = pl.pallas_call(
        window_kernel,
        out_shape=(
            jax.ShapeDtypeStruct((n_row, local_rows, TILE, LANES), jnp.bfloat16),
            jax.ShapeDtypeStruct((1, LANES, LANES), jnp.bfloat16),
        ),
        grid_spec=pltpu.PrefetchScalarGridSpec(
            num_scalar_prefetch=1,
            in_specs=[VMEM],
            out_specs=[VMEM, VMEM],
            scratch_shapes=[
                pltpu.VMEM((local_rows, HALF, 8, LANES), jnp.float32),
                pltpu.VMEM((local_rows, TILE, LANES), jnp.float32),
            ],
        ),
        name="window",
    )(p_cols.reshape(local_rows, slots), p_tiles.reshape(local_rows, slots, area))
    column_window = exchanged(own_rows, "row").reshape(n_row * local_rows, TILE, LANES)
    unfolded = pl.pallas_call(
        unfold_kernel,
        out_shape=jax.ShapeDtypeStruct((total_slots, TILE, LANES), jnp.bfloat16),
        grid_spec=pltpu.PrefetchScalarGridSpec(
            num_scalar_prefetch=1,
            grid=(total_slots // CHUNK,),
            in_specs=[pl.BlockSpec((CHUNK, area), lambda i, *_: (i, 0))],
            out_specs=pl.BlockSpec((CHUNK, TILE, LANES), lambda i, *_: (i, 0, 0)),
            scratch_shapes=[pltpu.VMEM((HALF, CHUNK, LANES), jnp.float32)],
        ),
        name="unfold",
    )(count, a_tiles.reshape(total_slots, area))
    depth = lax.axis_size(Z)
    places = depth * local_rows
    product = pl.pallas_call(
        product_kernel,
        out_shape=jax.ShapeDtypeStruct((n_y, places, TILE, LANES), jnp.bfloat16),
        grid_spec=pltpu.PrefetchScalarGridSpec(
            num_scalar_prefetch=3,
            grid=(total_slots // CHUNK,),
            in_specs=[pl.BlockSpec((CHUNK, TILE, LANES), lambda i, *_: (i, 0, 0)), ANY],
            out_specs=ANY,
            scratch_shapes=[
                pltpu.VMEM((n_row * local_rows, TILE, LANES), jnp.bfloat16),
                pltpu.VMEM((n_y * places, TILE, LANES), jnp.float32),
                pltpu.VMEM((n_y, places, TILE, LANES), jnp.bfloat16),
                pltpu.SemaphoreType.DMA,
                pltpu.SemaphoreType.DMA((n_y,)),
            ],
        ),
        name="product",
    )(
        a_rows.reshape(total_slots),
        a_cols.reshape(total_slots),
        count,
        unfolded,
        column_window,
    )
    gathered = exchanged(product.reshape(n_y, depth, LANES, LANES), "y")
    far = [own_turned]
    for distance in FAR[1:]:
        far.append(moved_along_z(own_turned, distance))
    pieces = [jnp.concatenate(far, axis=0)]
    for distance in NEAR[1:]:
        pieces.append(moved_along_z(pieces[0], distance))
    galerkin = pl.pallas_call(
        contract_kernel,
        out_shape=jax.ShapeDtypeStruct((HALF, 3, LANES), jnp.float32),
        grid_spec=pltpu.PrefetchScalarGridSpec(
            num_scalar_prefetch=1,
            in_specs=[ANY] * (1 + len(NEAR)),
            out_specs=VMEM,
            scratch_shapes=[
                pltpu.VMEM((len(NEAR), n_y, len(FAR), LANES, LANES), jnp.bfloat16),
                pltpu.VMEM((len(NEAR), len(FAR), LANES, LANES), jnp.bfloat16),
                pltpu.SemaphoreType.DMA((len(NEAR),)),
                pltpu.SemaphoreType.DMA((len(NEAR),)),
            ],
        ),
        name="contract",
    )(lax.axis_index(Z).reshape(1), gathered, *pieces)
    total = summed_over_all(galerkin)
    corner = jnp.concatenate([total[:, 2, :TILE], total[:, 2, TILE:]], axis=0)
    upper = jnp.concatenate([total[:, 0], total[:, 1]], axis=0)
    return jnp.concatenate([upper, corner], axis=1)


def solution(mesh):
    torus = Mesh(
        mesh.devices.reshape(mesh.shape["row"], 4, 4, mesh.shape["layer"]),
        ("row", "zh", "y", "zl"),
    )
    in_specs = (
        P("row", COL_LAYER, None, None),
        P("row", COL_LAYER, None),
        P("row", COL_LAYER, None),
        P("row", COL_LAYER),
        P("row", COL_LAYER, None, None),
        P("row", COL_LAYER, None),
    )
    return jax.shard_map(coarse_blocks, mesh=torus, in_specs=in_specs, out_specs=P(), check_vma=False)
```

time: 143 us -> 124 us (0.87)
  blocking collectives: 113 us -> 46.9 us
  starting transfers between devices: 10.2 us -> 43.9 us
  Pallas kernels: 10.5 us -> 19 us
  waiting for transfers between devices: 5.84 us -> 9.24 us
    all_to_all x5 -> x3, blocking collectives: 113 us -> 46.9 us  [exchanged(): return lax.all_to_all(x, axes, 0, 0, tiled=True)]
    ppermute x0 -> x6, starting transfers between devices: none -> 30.2 us  [moved_along_z(): lax.ppermute(x, Z, [(z, (z + distance) % depth) for z in range(depth)])]
    ppermute x0 -> x6, waiting for transfers between devices: none -> 9.23 us  [moved_along_z(): lax.ppermute(x, Z, [(z, (z + distance) % depth) for z in range(depth)])]
    pallas_call x3 -> x4, Pallas kernels: 10.5 us -> 19 us  [the longest x1 7.49 us: coarse_blocks(): pl.pallas_call(product_kernel, out_shape=jax.ShapeDtypeStruct((n_y, place...]
    all_to_all x1 -> x2, waiting for transfers between devices: 5.84 us -> 0.01 us  [exchanged(): return lax.all_to_all(x, axes, 0, 0, tiled=True)]
    all_to_all x1 -> x2, starting transfers between devices: 10.2 us -> 13.8 us  [exchanged(): return lax.all_to_all(x, axes, 0, 0, tiled=True)]
  transfers between devices with their start and end apart: 1 -> 8, of which waited for: 1 -> 3; matrix products, arithmetic and copies ran while one was open for 0% -> 0% of each run, Pallas kernels for 0% -> 5%
where the time goes in v3:
time: 124 us; the launch traced here: 123 us
  blocking collectives  46.9 us (38%)
  starting transfers between devices  43.9 us (35%)
  Pallas kernels  19 us (15%)
  waiting for transfers between devices  9.24 us (7%)
  local copies, waits for them, and re-layouts  2.26 us (2%)
    all_to_all x3, blocking collectives, exchanged(): return lax.all_to_all(x, axes, 0, 0, tiled=True)  46.9 us
    ppermute x6, starting transfers between devices, moved_along_z(): lax.ppermute(x, Z, [(z, (z + distance) % depth) for z in range(depth)])  30.2 us
    all_to_all x2, starting transfers between devices, exchanged(): return lax.all_to_all(x, axes, 0, 0, tiled=True)  13.8 us
    ppermute x6, waiting for transfers between devices, moved_along_z(): lax.ppermute(x, Z, [(z, (z + distance) % depth) for z in range(depth)])  9.23 us
    pallas_call x1, Pallas kernels, coarse_blocks(): pl.pallas_call(product_kernel, out_shape=jax.ShapeDtypeStruct((n_y, place...  7.49 us
    pallas_call x1, Pallas kernels, coarse_blocks(): pl.pallas_call(unfold_kernel, out_shape=jax.ShapeDtypeStruct((total_slots...  6.25 us
    pallas_call x1, Pallas kernels, coarse_blocks(): pl.pallas_call(contract_kernel, out_shape=jax.ShapeDtypeStruct((HALF, 3,...  2.75 us
    pallas_call x1, Pallas kernels, coarse_blocks(): pl.pallas_call(window_kernel, out_shape=(jax.ShapeDtypeStruct((n_row, loc...  2.54 us
  transfers between devices with their start and end apart: 8, of which 3 were waited for; matrix products, arithmetic and copies ran while one was open for 0% of the time, Pallas kernels for 5%

profile of v3, /device:TPU:1, one launch (start us, length us, event | category | flops | bytes accessed | tf_op | source)
XLA Modules:
  0.0 122.9 jit_solution(14309277623043318219)
XLA Ops:
  0.0 2.5 %window.1 = (bf16[8,2,64,128]{3,2,1,0:T(8,128)(2,1)}, bf16[1,128,128]{2,1,0:T(8,128)(2,1)}) custom-call(s32[2,4]{1,0:T(2,128)} %bitcast.27, bf16[2,4,4096]{2,1,0:T(4,128)(2,1)} %bitcast.22), custom_call_target="tpu_custom_call" | custom-call | tf_op jit(solution)/shard_map/window/pallas_call | solution.py:167
  2.5 10.2 %all-to-all-start = ((bf16[8,2,64,128]{3,2,1,0:T(8,128)(2,1)}), bf16[8,2,64,128]{3,2,1,0:T(8,128)(2,1)S(1)}, u32[]{:S(2)}, u32[]{:S(2)}) async-start(bf16[8,2,64,128]{3,2,1,0:T(8,128)(2,1)} %get-tuple-element.7), calls=%async_computation | async-start | bytes 524288 | tf_op jit(solution)/shard_map/all_to_all | solution.py:147
  13.3 6.3 %unfold.1.a_ref = bf16[128,64,128]{2,1,0:T(8,128)(2,1)} custom-call(s32[1]{0:T(128)} %bitcast.17.count, bf16[128,4096]{1,0:T(8,128)(2,1)} %bitcast.20), custom_call_target="tpu_custom_call" | custom-call | tf_op jit(solution)/shard_map/unfold/pallas_call | solution.py:185
  19.6 0.0 all-to-all-done
  19.6 0.7 copy-done.1
  20.3 7.5 %product.1 = bf16[4,32,64,128]{3,2,1,0:T(8,128)(2,1)} custom-call(s32[128]{0:T(128)} %bitcast.28, s32[128]{0:T(128)} %bitcast.29, s32[1]{0:T(128)} %bitcast.18.count, bf16[128,64,128]{2,1,0:T(8,128)(2,1)} %unfold.1.a_ref, bf16[16,64,128]{2,1,0:T(8,128)(2,1)} %bitcast.21), custom_call_target="tpu_custom_call" | custom-call | tf_op jit(solution)/shard_map/product/pallas_call | solution.py:199
  27.8 0.0 copy-start.6
  27.8 3.6 %all-to-all-start.1 = ((bf16[4,16,128,128]{3,2,1,0:T(8,128)(2,1)}), bf16[4,16,128,128]{3,2,1,0:T(8,128)(2,1)S(1)}, u32[]{:S(2)}, u32[]{:S(2)}) async-start(bf16[4,16,128,128]{3,2,1,0:T(8,128)(2,1)} %bitcast.19), calls=%async_computation.1 | async-start | bytes 4194304 | tf_op jit(solution)/shard_map/all_to_all | solution.py:147
  31.4 0.0 copy-done.6
  31.5 12.2 %collective-permute-start = (bf16[1,128,128]{2,1,0:T(8,128)(2,1)S(1)}, bf16[1,128,128]{2,1,0:T(8,128)(2,1)S(1)}, u32[]{:S(2)}, u32[]{:S(2)}) collective-permute-start(bf16[1,128,128]{2,1,0:T(8,128)(2,1)S(1)} %copy-done.6), channel_id=1, source_target_pairs={{0,32},{1,33},{2,34},{3,35},{16,48},{17,49},{18,50},{19,51},{32,0}... | collective-permute-start | bytes 98312 | tf_op jit(solution)/shard_map/ppermute | solution.py:152
  43.6 3.7 %collective-permute-start.1 = (bf16[1,128,128]{2,1,0:T(8,128)(2,1)S(1)}, bf16[1,128,128]{2,1,0:T(8,128)(2,1)S(1)}, u32[]{:S(2)}, u32[]{:S(2)}) collective-permute-start(bf16[1,128,128]{2,1,0:T(8,128)(2,1)S(1)} %copy-done.6), channel_id=1, source_target_pairs={{0,16},{1,17},{2,18},{3,19},{16,32},{17,33},{18,34},{19,35},{32,48... | collective-permute-start | bytes 98312 | tf_op jit(solution)/shard_map/ppermute | solution.py:152
  47.3 5.5 %collective-permute-start.2 = (bf16[1,128,128]{2,1,0:T(8,128)(2,1)S(1)}, bf16[1,128,128]{2,1,0:T(8,128)(2,1)S(1)}, u32[]{:S(2)}, u32[]{:S(2)}) collective-permute-start(bf16[1,128,128]{2,1,0:T(8,128)(2,1)S(1)} %copy-done.6), channel_id=1, source_target_pairs={{0,48},{1,49},{2,50},{3,51},{16,0},{17,1},{18,2},{19,3},{32,16},{3... | collective-permute-start | bytes 98312 | tf_op jit(solution)/shard_map/ppermute | solution.py:152
  52.9 0.0 collective-permute-done
  52.9 0.0 collective-permute-done.1
  52.9 3.0 %collective-permute-done.2 = bf16[1,128,128]{2,1,0:T(8,128)(2,1)S(1)} collective-permute-done((bf16[1,128,128]{2,1,0:T(8,128)(2,1)S(1)}, bf16[1,128,128]{2,1,0:T(8,128)(2,1)S(1)}, u32[]{:S(2)}, u32[]{:S(2)}) %collective-permute-start.2) | collective-permute-done | bytes 32800 | tf_op jit(solution)/shard_map/ppermute | solution.py:152
  55.9 3.4 %collective-permute-start.3 = (bf16[4,128,128]{2,1,0:T(8,128)(2,1)S(1)}, bf16[4,128,128]{2,1,0:T(8,128)(2,1)S(1)}, u32[]{:S(2)}, u32[]{:S(2)}) collective-permute-start(bf16[4,128,128]{2,1,0:T(8,128)(2,1)S(1)} %constant_dynamic-update-slice_fusion.refs_0_), channel_id=1, source_target_pairs={{0,1},{1,2},{2,3},{3,16},{16,17},{17,18},{18,19},{19,32},{32,33},{... | collective-permute-start | bytes 393224 | tf_op jit(solution)/shard_map/ppermute | solution.py:152
  59.3 3.1 %collective-permute-start.4 = (bf16[4,128,128]{2,1,0:T(8,128)(2,1)S(1)}, bf16[4,128,128]{2,1,0:T(8,128)(2,1)S(1)}, u32[]{:S(2)}, u32[]{:S(2)}) collective-permute-start(bf16[4,128,128]{2,1,0:T(8,128)(2,1)S(1)} %constant_dynamic-update-slice_fusion.refs_0_), channel_id=1, source_target_pairs={{0,51},{1,0},{2,1},{3,2},{16,3},{17,16},{18,17},{19,18},{32,19},{3... | collective-permute-start | bytes 393224 | tf_op jit(solution)/shard_map/ppermute | solution.py:152
  62.4 2.3 %collective-permute-start.5 = (bf16[4,128,128]{2,1,0:T(8,128)(2,1)S(1)}, bf16[4,128,128]{2,1,0:T(8,128)(2,1)S(1)}, u32[]{:S(2)}, u32[]{:S(2)}) collective-permute-start(bf16[4,128,128]{2,1,0:T(8,128)(2,1)S(1)} %constant_dynamic-update-slice_fusion.refs_0_), channel_id=1, source_target_pairs={{0,2},{1,3},{2,16},{3,17},{16,18},{17,19},{18,32},{19,33},{32,34},... | collective-permute-start | bytes 393224 | tf_op jit(solution)/shard_map/ppermute | solution.py:152
  64.8 0.0 collective-permute-done.3.refs_1_
  64.8 0.5 collective-permute-done.4.refs_2_
  65.3 5.7 %collective-permute-done.5.refs_3_ = bf16[4,128,128]{2,1,0:T(8,128)(2,1)S(1)} collective-permute-done((bf16[4,128,128]{2,1,0:T(8,128)(2,1)S(1)}, bf16[4,128,128]{2,1,0:T(8,128)(2,1)S(1)}, u32[]{:S(2)}, u32[]{:S(2)}) %collective-permute-start.5) | collective-permute-done | bytes 131104 | tf_op jit(solution)/shard_map/ppermute | solution.py:152
  71.0 0.0 all-to-all-done.1.p_hbm
  71.0 0.0 copy-done.3
  71.0 0.0 copy-done.4
  71.0 0.6 copy-done.5
  71.7 0.7 copy-done
  72.4 2.7 %contract.1 = f32[32,3,128]{2,1,0:T(4,128)} custom-call(s32[1]{0:T(128)} %bitcast.own_z, bf16[4,16,128,128]{3,2,1,0:T(8,128)(2,1)} %copy-done, bf16[4,128,128]{2,1,0:T(8,128)(2,1)} %copy-done.2, bf16[4,128,128]{2,1,0:T(8,128)(2,1)} %copy-done.3, bf16[4,128,128]{2,1,0:T(8,128)(2,1)} %copy-done.4, bf16[4,128,128]{2,1,0:T(8,128)(2,1)} %copy-done.5), custom_call_target="tpu_custom_call" | custom-call | tf_op jit(solution)/shard_map/contract/pallas_call | solution.py:230
  75.1 18.9 %all_to_all.25 = f32[32,3,128]{2,1,0:T(4,128)S(1)} all-to-all(f32[32,3,128]{2,1,0:T(4,128)} %contract.1), channel_id=1, replica_groups=mesh['row'=8,'zh'=4,'y'=4,'zl'=4] {'row','y'}, dimensions={0} | all-to-all | bytes 98304 | tf_op jit(solution)/shard_map/all_to_all | solution.py:147
  94.1 15.6 %all_to_all.26 = f32[16,3,128]{2,1,0:T(4,128)S(1)} all-to-all(f32[16,3,128]{2,1,0:T(4,128)S(1)} %broadcast_in_dim.6), channel_id=1, replica_groups=mesh['row'=8,'zh'=4,'y'=4,'zl'=4] {'zh','zl'}, dimensions={0} | all-to-all | bytes 49152 | tf_op jit(solution)/shard_map/all_to_all | solution.py:147
  109.8 12.3 %all_to_all.27 = f32[32,3,128]{2,1,0:T(4,128)S(1)} all-to-all(f32[32,3,128]{2,1,0:T(4,128)S(1)} %broadcast_in_dim.7), channel_id=1, replica_groups=mesh['row'=8,'zh'=4,'y'=4,'zl'=4] {'row','y'}, dimensions={0} | all-to-all | bytes 98304 | tf_op jit(solution)/shard_map/all_to_all | solution.py:147
  122.1 0.1 fusion.1
  122.2 0.6 maximum_maximum_fusion
  (16 shorter events, 0.2 us)
Async XLA Ops:
  2.5 17.1 %all-to-all-start = ((bf16[8,2,64,128]{3,2,1,0:T(8,128)(2,1)}), bf16[8,2,64,128]{3,2,1,0:T(8,128)(2,1)S(1)}, u32[]{:S(2)}, u32[]{:S(2)}) async-start(bf16[8,2,64,128]{3,2,1,0:T(8,128)(2,1)} %get-tuple-element.7), calls=%async_computation | async-start | bytes 524288 | tf_op jit(solution)/shard_map/all_to_all | solution.py:147
  19.6 0.7 copy-start.1
  27.8 3.6 %copy-start.6 = (bf16[1,128,128]{2,1,0:T(8,128)(2,1)S(1)}, bf16[1,128,128]{2,1,0:T(8,128)(2,1)}, u32[]{:S(2)}) copy-start(bf16[1,128,128]{2,1,0:T(8,128)(2,1)} %get-tuple-element.8) | copy-start | bytes 98308
  27.8 43.2 %all-to-all-start.1 = ((bf16[4,16,128,128]{3,2,1,0:T(8,128)(2,1)}), bf16[4,16,128,128]{3,2,1,0:T(8,128)(2,1)S(1)}, u32[]{:S(2)}, u32[]{:S(2)}) async-start(bf16[4,16,128,128]{3,2,1,0:T(8,128)(2,1)} %bitcast.19), calls=%async_computation.1 | async-start | bytes 4194304 | tf_op jit(solution)/shard_map/all_to_all | solution.py:147
  31.5 21.4 %collective-permute-start = (bf16[1,128,128]{2,1,0:T(8,128)(2,1)S(1)}, bf16[1,128,128]{2,1,0:T(8,128)(2,1)S(1)}, u32[]{:S(2)}, u32[]{:S(2)}) collective-permute-start(bf16[1,128,128]{2,1,0:T(8,128)(2,1)S(1)} %copy-done.6), channel_id=1, source_target_pairs={{0,32},{1,33},{2,34},{3,35},{16,48},{17,49},{18,50},{19,51},{32,0}... | collective-permute-start | bytes 98312 | tf_op jit(solution)/shard_map/ppermute | solution.py:152
  43.6 9.2 %collective-permute-start.1 = (bf16[1,128,128]{2,1,0:T(8,128)(2,1)S(1)}, bf16[1,128,128]{2,1,0:T(8,128)(2,1)S(1)}, u32[]{:S(2)}, u32[]{:S(2)}) collective-permute-start(bf16[1,128,128]{2,1,0:T(8,128)(2,1)S(1)} %copy-done.6), channel_id=1, source_target_pairs={{0,16},{1,17},{2,18},{3,19},{16,32},{17,33},{18,34},{19,35},{32,48... | collective-permute-start | bytes 98312 | tf_op jit(solution)/shard_map/ppermute | solution.py:152
  47.3 8.6 %collective-permute-start.2 = (bf16[1,128,128]{2,1,0:T(8,128)(2,1)S(1)}, bf16[1,128,128]{2,1,0:T(8,128)(2,1)S(1)}, u32[]{:S(2)}, u32[]{:S(2)}) collective-permute-start(bf16[1,128,128]{2,1,0:T(8,128)(2,1)S(1)} %copy-done.6), channel_id=1, source_target_pairs={{0,48},{1,49},{2,50},{3,51},{16,0},{17,1},{18,2},{19,3},{32,16},{3... | collective-permute-start | bytes 98312 | tf_op jit(solution)/shard_map/ppermute | solution.py:152
  55.9 15.1 %copy-start.2 = (bf16[4,128,128]{2,1,0:T(8,128)(2,1)}, bf16[4,128,128]{2,1,0:T(8,128)(2,1)S(1)}, u32[]{:S(2)}) copy-start(bf16[4,128,128]{2,1,0:T(8,128)(2,1)S(1)} %constant_dynamic-update-slice_fusion.refs_0_) | copy-start | bytes 393220
  55.9 8.8 %collective-permute-start.3 = (bf16[4,128,128]{2,1,0:T(8,128)(2,1)S(1)}, bf16[4,128,128]{2,1,0:T(8,128)(2,1)S(1)}, u32[]{:S(2)}, u32[]{:S(2)}) collective-permute-start(bf16[4,128,128]{2,1,0:T(8,128)(2,1)S(1)} %constant_dynamic-update-slice_fusion.refs_0_), channel_id=1, source_target_pairs={{0,1},{1,2},{2,3},{3,16},{16,17},{17,18},{18,19},{19,32},{32,33},{... | collective-permute-start | bytes 393224 | tf_op jit(solution)/shard_map/ppermute | solution.py:152
  59.3 6.0 %collective-permute-start.4 = (bf16[4,128,128]{2,1,0:T(8,128)(2,1)S(1)}, bf16[4,128,128]{2,1,0:T(8,128)(2,1)S(1)}, u32[]{:S(2)}, u32[]{:S(2)}) collective-permute-start(bf16[4,128,128]{2,1,0:T(8,128)(2,1)S(1)} %constant_dynamic-update-slice_fusion.refs_0_), channel_id=1, source_target_pairs={{0,51},{1,0},{2,1},{3,2},{16,3},{17,16},{18,17},{19,18},{32,19},{3... | collective-permute-start | bytes 393224 | tf_op jit(solution)/shard_map/ppermute | solution.py:152
  62.4 8.6 %collective-permute-start.5 = (bf16[4,128,128]{2,1,0:T(8,128)(2,1)S(1)}, bf16[4,128,128]{2,1,0:T(8,128)(2,1)S(1)}, u32[]{:S(2)}, u32[]{:S(2)}) collective-permute-start(bf16[4,128,128]{2,1,0:T(8,128)(2,1)S(1)} %constant_dynamic-update-slice_fusion.refs_0_), channel_id=1, source_target_pairs={{0,2},{1,3},{2,16},{3,17},{16,18},{17,19},{18,32},{19,33},{32,34},... | collective-permute-start | bytes 393224 | tf_op jit(solution)/shard_map/ppermute | solution.py:152
  64.8 6.3 %copy-start.3 = (bf16[4,128,128]{2,1,0:T(8,128)(2,1)}, bf16[4,128,128]{2,1,0:T(8,128)(2,1)S(1)}, u32[]{:S(2)}) copy-start(bf16[4,128,128]{2,1,0:T(8,128)(2,1)S(1)} %collective-permute-done.3.refs_1_) | copy-start | bytes 393220
  65.3 5.7 %copy-start.4 = (bf16[4,128,128]{2,1,0:T(8,128)(2,1)}, bf16[4,128,128]{2,1,0:T(8,128)(2,1)S(1)}, u32[]{:S(2)}) copy-start(bf16[4,128,128]{2,1,0:T(8,128)(2,1)S(1)} %collective-permute-done.4.refs_2_) | copy-start | bytes 393220
  71.0 0.7 copy-start.5
  71.0 1.4 %copy-start = (bf16[4,16,128,128]{3,2,1,0:T(8,128)(2,1)}, bf16[4,16,128,128]{3,2,1,0:T(8,128)(2,1)S(1)}, u32[]{:S(2)}) copy-start(bf16[4,16,128,128]{3,2,1,0:T(8,128)(2,1)S(1)} %all-to-all-done.1.p_hbm) | copy-start | bytes 6291460

commit v4 on v2

v4 whole, which is shorter than its diff:
```python
import jax
import jax.numpy as jnp
from jax import lax
from jax.experimental import pallas as pl
from jax.experimental.pallas import tpu as pltpu
from jax.sharding import Mesh
from jax.sharding import PartitionSpec as P

TILE = 64
HALF = TILE // 2
LANES = 2 * TILE
CHUNK = 16
GROUP = 4
COL_LAYER = ("zh", "y", "zl")
Z = ("zh", "zl")
ROW_Y = ("row", "y")
PARTS = 4
VMEM = pl.BlockSpec(memory_space=pltpu.VMEM)
ANY = pl.BlockSpec(memory_space=pl.ANY)
HBM = pl.BlockSpec(memory_space=pltpu.HBM)


def lane_swapped(x):
    return pltpu.roll(x, TILE, axis=1)


def window_kernel(cols, p_ref, rows_ref, turned_ref, split, natural):
    local_rows, slots = cols.shape
    lane = lax.broadcasted_iota(jnp.int32, (HALF, LANES), 1)
    panel = lax.broadcasted_iota(jnp.int32, (8, slots), 0)
    slot = lax.broadcasted_iota(jnp.int32, (8, slots), 1)
    stacked = []
    for t in range(local_rows):
        chosen = jnp.zeros((8, slots), jnp.float32)
        for s in range(slots):
            chosen = jnp.where((slot == s) & (panel == cols[t, s]), 1.0, chosen)
        sums = jnp.dot(chosen.astype(jnp.bfloat16), p_ref[t], preferred_element_type=jnp.float32)
        for k in range(HALF):
            split[t, k] = sums[:, k * LANES : (k + 1) * LANES]
        first, second = split[t, :, 0, :], split[t, :, 1, :]
        even = jnp.where(lane < TILE, first, lane_swapped(second))
        odd = jnp.where(lane < TILE, lane_swapped(first), second)
        natural[t, pl.ds(0, HALF, stride=2)] = even
        natural[t, pl.ds(1, HALF, stride=2)] = odd
        stacked += [even, odd]
    rows = natural[...].astype(jnp.bfloat16)
    for r in range(rows_ref.shape[0]):
        rows_ref[r] = rows
    turned = jnp.concatenate(stacked, axis=0).T.astype(jnp.bfloat16)
    for z in range(turned_ref.shape[0]):
        turned_ref[z] = turned


def product_kernel(rows, cols, count, own_y, a_hbm, w_hbm, *refs):
    *out_hbm, tiles_in, window, split, total, rounded, in_sems, out_sems = refs
    live = count[0]
    in_copies = [
        pltpu.make_async_copy(a_hbm, tiles_in, in_sems.at[0]),
        pltpu.make_async_copy(w_hbm, window, in_sems.at[1]),
    ]
    for copy in in_copies:
        copy.start()
    total[...] = jnp.zeros_like(total)
    for copy in in_copies:
        copy.wait()

    def place(row):
        f = row & (TILE - 1)
        z = ((f >> 4) << 2) | (f & 3)
        distance = ((f >> 2) - own_y[0]) & 3
        return (distance * 16 + z) * 2 + (row >> 6)

    def chunk(turn, carry):
        first = pl.multiple_of(turn * CHUNK, CHUNK)
        tiles = tiles_in[pl.ds(first, CHUNK), :].astype(jnp.float32)
        slot = first + lax.broadcasted_iota(jnp.int32, tiles.shape, 0)
        tiles = jnp.where(slot < live, tiles, 0.0)
        for k in range(HALF):
            split[k] = tiles[:, k * LANES : (k + 1) * LANES]
        for g in range(0, CHUNK, GROUP):
            parts = []
            for i in range(g, g + GROUP):
                x = split[:, i, :]
                tile = jnp.concatenate([x, lane_swapped(x)], axis=0).astype(jnp.bfloat16)
                parts.append(
                    jnp.dot(
                        tile[:, :TILE], window[cols[first + i]], preferred_element_type=jnp.float32
                    )
                )
            for i in range(g, g + GROUP):
                total[place(rows[first + i])] += parts[i - g]
        return carry

    lax.fori_loop(0, (live + CHUNK - 1) // CHUNK, chunk, 0)
    size = out_hbm[0].shape[0]
    out_copies = [pltpu.make_async_copy(total.at[pl.ds(0, size)], out_hbm[0], out_sems.at[0])]
    out_copies[0].start()
    for distance in range(1, len(out_hbm)):

        def store(turn, carry, distance=distance):
            rounded[distance - 1, turn] = total[distance * size + turn].astype(jnp.bfloat16)
            return carry

        lax.fori_loop(0, size, store, 0, unroll=8)
        copy = pltpu.make_async_copy(
            rounded.at[distance - 1], out_hbm[distance], out_sems.at[distance]
        )
        copy.start()
        out_copies.append(copy)
    for copy in out_copies:
        copy.wait()


def contract_kernel(own_hbm, *refs):
    *p_hbm, w_hbm, out_ref, own_buf, p_buf, w_buf, sems = refs
    pieces, parts = w_hbm.shape[0], sems.shape[0]
    size = pieces // parts
    copies = []
    for part in range(parts):
        there = pl.ds(part * size, size)
        pairs = [(own_hbm.at[there], own_buf.at[there]), (w_hbm.at[there], w_buf.at[there])]
        pairs += [(p.at[there], p_buf.at[i, there]) for i, p in enumerate(p_hbm)]
        copies.append(
            [pltpu.make_async_copy(*pair, sems.at[part, i]) for i, pair in enumerate(pairs)]
        )
        for copy in copies[-1]:
            copy.start()
    galerkin = jnp.zeros((LANES, LANES), jnp.float32)
    for part in range(parts):
        for copy in copies[part]:
            copy.wait()
        for z in range(part * size, (part + 1) * size):
            block = own_buf[z]
            for i in range(len(p_hbm)):
                block += p_buf[i, z].astype(jnp.float32)
            high = block.astype(jnp.bfloat16)
            low = (block - high.astype(jnp.float32)).astype(jnp.bfloat16)
            galerkin += jnp.dot(w_buf[z], high, preferred_element_type=jnp.float32)
            galerkin += jnp.dot(w_buf[z], low, preferred_element_type=jnp.float32)
    out_ref[:, 0, :] = galerkin[:HALF]
    out_ref[:, 1, :] = galerkin[HALF:TILE]
    corner = galerkin[TILE:]
    lane = lax.broadcasted_iota(jnp.int32, (HALF, LANES), 1)
    out_ref[:, 2, :] = jnp.where(lane < TILE, lane_swapped(corner[:HALF]), corner[HALF:])


def exchanged(x, axes):
    return lax.all_to_all(x, axes, 0, 0, tiled=True)


def summed_over_all(x):
    peers, depth = lax.axis_size(ROW_Y), lax.axis_size(Z)
    piece = jnp.sum(exchanged(x, ROW_Y), axis=0)
    piece = jnp.sum(exchanged(jnp.broadcast_to(piece, (depth, *piece.shape)), Z), axis=0)
    return exchanged(jnp.broadcast_to(piece, (peers, *piece.shape)), ROW_Y)


def coarse_blocks(a_tiles, a_rows, a_cols, a_count, p_tiles, p_cols):
    local_rows, _, slots, area = p_tiles.shape
    total_slots = a_tiles.shape[2]
    n_row, n_y = lax.axis_size("row"), lax.axis_size("y")
    depth = lax.axis_size(Z)
    places = depth * local_rows
    own_rows, own_turned = pl.pallas_call(
        window_kernel,
        out_shape=(
            jax.ShapeDtypeStruct((n_row, local_rows, TILE, LANES), jnp.bfloat16),
            jax.ShapeDtypeStruct((depth, LANES, LANES), jnp.bfloat16),
        ),
        grid_spec=pltpu.PrefetchScalarGridSpec(
            num_scalar_prefetch=1,
            in_specs=[VMEM],
            out_specs=[VMEM, VMEM],
            scratch_shapes=[
                pltpu.VMEM((local_rows, HALF, 8, LANES), jnp.float32),
                pltpu.VMEM((local_rows, TILE, LANES), jnp.float32),
            ],
        ),
        name="window",
    )(p_cols.reshape(local_rows, slots), p_tiles.reshape(local_rows, slots, area))
    column_window = exchanged(own_rows, "row").reshape(n_row * local_rows, TILE, LANES)
    turned = exchanged(own_turned, Z)
    products = pl.pallas_call(
        product_kernel,
        out_shape=[
            jax.ShapeDtypeStruct((places, TILE, LANES), jnp.bfloat16 if distance else jnp.float32)
            for distance in range(n_y)
        ],
        grid_spec=pltpu.PrefetchScalarGridSpec(
            num_scalar_prefetch=4,
            in_specs=[HBM, ANY],
            out_specs=[ANY] + [HBM] * (n_y - 1),
            scratch_shapes=[
                pltpu.VMEM((total_slots, area), jnp.bfloat16),
                pltpu.VMEM((n_row * local_rows, TILE, LANES), jnp.bfloat16),
                pltpu.VMEM((HALF, CHUNK, LANES), jnp.float32),
                pltpu.VMEM((n_y * places, TILE, LANES), jnp.float32),
                pltpu.VMEM((n_y - 1, places, TILE, LANES), jnp.bfloat16),
                pltpu.SemaphoreType.DMA((2,)),
                pltpu.SemaphoreType.DMA((n_y,)),
            ],
        ),
        compiler_params=pltpu.CompilerParams(vmem_limit_bytes=16 << 20),
        name="product",
    )(
        a_rows.reshape(total_slots),
        a_cols.reshape(total_slots),
        a_count.reshape(1),
        lax.axis_index("y").reshape(1),
        a_tiles.reshape(total_slots, area),
        column_window,
    )
    gathered = [products[0].reshape(depth, LANES, LANES)]
    for distance in range(1, n_y):
        gathered.append(
            lax.ppermute(
                products[distance].reshape(depth, LANES, LANES),
                "y",
                [(y, (y + distance) % n_y) for y in range(n_y)],
            )
        )
    galerkin = pl.pallas_call(
        contract_kernel,
        out_shape=jax.ShapeDtypeStruct((HALF, 3, LANES), jnp.float32),
        in_specs=[ANY] * (n_y + 1),
        out_specs=VMEM,
        scratch_shapes=[
            pltpu.VMEM((depth, LANES, LANES), jnp.float32),
            pltpu.VMEM((n_y - 1, depth, LANES, LANES), jnp.bfloat16),
            pltpu.VMEM((depth, LANES, LANES), jnp.bfloat16),
            pltpu.SemaphoreType.DMA((PARTS, n_y + 1)),
        ],
        compiler_params=pltpu.CompilerParams(vmem_limit_bytes=8 << 20),
        name="contract",
    )(*gathered, turned)
    total = summed_over_all(galerkin)
    corner = jnp.concatenate([total[:, 2, :TILE], total[:, 2, TILE:]], axis=0)
    upper = jnp.concatenate([total[:, 0], total[:, 1]], axis=0)
    return jnp.concatenate([upper, corner], axis=1)


def solution(mesh):
    torus = Mesh(
        mesh.devices.reshape(mesh.shape["row"], 4, 4, mesh.shape["layer"]),
        ("row", "zh", "y", "zl"),
    )
    in_specs = (
        P("row", COL_LAYER, None, None),
        P("row", COL_LAYER, None),
        P("row", COL_LAYER, None),
        P("row", COL_LAYER),
        P("row", COL_LAYER, None, None),
        P("row", COL_LAYER, None),
    )
    return jax.shard_map(
        coarse_blocks, mesh=torus, in_specs=in_specs, out_specs=P(), check_vma=False
    )
```

time: 122 us -> 119 us (0.975)
  blocking collectives: 68.5 us -> 66.8 us
  Pallas kernels: 10.8 us -> 9.28 us
  starting transfers between devices: 20 us -> 21.3 us
    pallas_call x1, Pallas kernels: 5.09 us -> 2.5 us  [coarse_blocks(): pl.pallas_call(product_kernel, out_shape=[jax.ShapeDtypeStruct((places, T...]
    all_to_all x4, blocking collectives: 68.5 us -> 66.8 us  [exchanged(): return lax.all_to_all(x, axes, 0, 0, tiled=True)]
  transfers between devices with their start and end apart: 4 -> 4, of which waited for: 3 -> 3; matrix products, arithmetic and copies ran while one was open for 0% -> 0% of each run, Pallas kernels for 4% -> 2%
where the time goes in v4:
time: 119 us
  blocking collectives  66.8 us (56%)
  starting transfers between devices  21.3 us (18%)
  waiting for transfers between devices  19 us (16%)
  Pallas kernels  9.28 us (8%)
    all_to_all x4, blocking collectives, exchanged(): return lax.all_to_all(x, axes, 0, 0, tiled=True)  66.8 us
    ppermute x3, waiting for transfers between devices, coarse_blocks(): lax.ppermute(products[distance].reshape(depth, LANES, LANES), 'y', [(y, (...  19 us
    ppermute x3, starting transfers between devices, coarse_blocks(): lax.ppermute(products[distance].reshape(depth, LANES, LANES), 'y', [(y, (...  10.7 us
    all_to_all x1, starting transfers between devices, exchanged(): return lax.all_to_all(x, axes, 0, 0, tiled=True)  10.6 us
    pallas_call x1, Pallas kernels, coarse_blocks(): pl.pallas_call(contract_kernel, out_shape=jax.ShapeDtypeStruct((HALF, 3,...  3.92 us
    pallas_call x1, Pallas kernels, coarse_blocks(): pl.pallas_call(window_kernel, out_shape=(jax.ShapeDtypeStruct((n_row, loc...  2.86 us
    pallas_call x1, Pallas kernels, coarse_blocks(): pl.pallas_call(product_kernel, out_shape=[jax.ShapeDtypeStruct((places, T...  2.5 us
  transfers between devices with their start and end apart: 4, of which 3 were waited for; matrix products, arithmetic and copies ran while one was open for 0% of the time, Pallas kernels for 2%

profile of v4, /device:TPU:1, one launch (start us, length us, event | category | flops | bytes accessed | tf_op | source)
XLA Modules:
  0.0 118.6 jit_solution(3507871463037722643)
XLA Ops:
  0.0 0.0 copy-start
  0.0 2.9 %window.1 = (bf16[8,2,64,128]{3,2,1,0:T(8,128)(2,1)}, bf16[16,128,128]{2,1,0:T(8,128)(2,1)}) custom-call(s32[2,4]{1,0:T(2,128)} %bitcast.34, bf16[2,4,4096]{2,1,0:T(4,128)(2,1)} %bitcast.29), custom_call_target="tpu_custom_call" | custom-call | tf_op jit(solution)/shard_map/window/pallas_call | solution.py:164
  2.9 16.6 %all_to_all.25 = bf16[8,2,64,128]{3,2,1,0:T(8,128)(2,1)S(1)} all-to-all(bf16[8,2,64,128]{3,2,1,0:T(8,128)(2,1)} %get-tuple-element.11), channel_id=1, replica_groups=mesh['row'=8,'zh'=4,'y'=4,'zl'=4] {'row'}, dimensions={0} | all-to-all | bytes 524288 | tf_op jit(solution)/shard_map/all_to_all | solution.py:148
  19.5 10.6 %all-to-all-start.1 = ((bf16[16,128,128]{2,1,0:T(8,128)(2,1)}), bf16[16,128,128]{2,1,0:T(8,128)(2,1)S(1)}, u32[]{:S(2)}, u32[]{:S(2)}) async-start(bf16[16,128,128]{2,1,0:T(8,128)(2,1)} %get-tuple-element.16), calls=%async_computation.1 | async-start | bytes 1048576 | tf_op jit(solution)/shard_map/all_to_all | solution.py:148
  30.7 0.0 copy-start.1
  30.7 0.0 copy-start.2
  30.7 0.0 copy-done
  30.7 0.6 copy-done.1
  31.4 0.0 copy-done.2
  31.4 2.5 %product.1 = (f32[32,64,128]{2,1,0:T(8,128)S(1)}, bf16[32,64,128]{2,1,0:T(8,128)(2,1)S(1)}, bf16[32,64,128]{2,1,0:T(8,128)(2,1)S(1)}, bf16[32,64,128]{2,1,0:T(8,128)(2,1)S(1)}) custom-call(s32[128]{0:T(128)S(1)} %bitcast.24, s32[128]{0:T(128)S(1)} %bitcast.25, s32[1]{0:T(128)} %bitcast.20.count, s32[1]{0:T(128)} %bitcast.3.own_y, ...), custom_call_target="tpu_custom_call" | custom-call | tf_op jit(solution)/shard_map/product/pallas_call | solution.py:183
  33.9 2.8 %collective-permute-start = (bf16[16,128,128]{2,1,0:T(8,128)(2,1)S(1)}, bf16[16,128,128]{2,1,0:T(8,128)(2,1)S(1)}, u32[]{:S(2)}, u32[]{:S(2)}) collective-permute-start(bf16[16,128,128]{2,1,0:T(8,128)(2,1)S(1)} %bitcast.28), channel_id=1, source_target_pairs={{0,4},{4,8},{8,12},{12,0},{1,5},{5,9},{9,13},{13,1},{2,6},{6,10},{... | collective-permute-start | bytes 1572872 | tf_op jit(solution)/shard_map/ppermute | solution.py:216
  36.7 4.9 %collective-permute-start.1 = (bf16[16,128,128]{2,1,0:T(8,128)(2,1)S(1)}, bf16[16,128,128]{2,1,0:T(8,128)(2,1)S(1)}, u32[]{:S(2)}, u32[]{:S(2)}) collective-permute-start(bf16[16,128,128]{2,1,0:T(8,128)(2,1)S(1)} %bitcast.27), channel_id=1, source_target_pairs={{0,8},{4,12},{8,0},{12,4},{1,9},{5,13},{9,1},{13,5},{2,10},{6,14},... | collective-permute-start | bytes 1572872 | tf_op jit(solution)/shard_map/ppermute | solution.py:216
  41.6 3.0 %collective-permute-start.2 = (bf16[16,128,128]{2,1,0:T(8,128)(2,1)S(1)}, bf16[16,128,128]{2,1,0:T(8,128)(2,1)S(1)}, u32[]{:S(2)}, u32[]{:S(2)}) collective-permute-start(bf16[16,128,128]{2,1,0:T(8,128)(2,1)S(1)} %bitcast.26), channel_id=1, source_target_pairs={{0,12},{4,0},{8,4},{12,8},{1,13},{5,1},{9,5},{13,9},{2,14},{6,2},{... | collective-permute-start | bytes 1572872 | tf_op jit(solution)/shard_map/ppermute | solution.py:216
  44.6 4.3 %collective-permute-done.refs_0_ = bf16[16,128,128]{2,1,0:T(8,128)(2,1)S(1)} collective-permute-done((bf16[16,128,128]{2,1,0:T(8,128)(2,1)S(1)}, bf16[16,128,128]{2,1,0:T(8,128)(2,1)S(1)}, u32[]{:S(2)}, u32[]{:S(2)}) %collective-permute-start) | collective-permute-done | bytes 524320 | tf_op jit(solution)/shard_map/ppermute | solution.py:216
  48.9 13.1 %collective-permute-done.1.refs_1_ = bf16[16,128,128]{2,1,0:T(8,128)(2,1)S(1)} collective-permute-done((bf16[16,128,128]{2,1,0:T(8,128)(2,1)S(1)}, bf16[16,128,128]{2,1,0:T(8,128)(2,1)S(1)}, u32[]{:S(2)}, u32[]{:S(2)}) %collective-permute-start.1) | collective-permute-done | bytes 524320 | tf_op jit(solution)/shard_map/ppermute | solution.py:216
  62.0 1.6 %collective-permute-done.2.refs_2_ = bf16[16,128,128]{2,1,0:T(8,128)(2,1)S(1)} collective-permute-done((bf16[16,128,128]{2,1,0:T(8,128)(2,1)S(1)}, bf16[16,128,128]{2,1,0:T(8,128)(2,1)S(1)}, u32[]{:S(2)}, u32[]{:S(2)}) %collective-permute-start.2) | collective-permute-done | bytes 524320 | tf_op jit(solution)/shard_map/ppermute | solution.py:216
  63.6 0.0 all-to-all-done.1.refs_3_
  63.6 3.9 %contract.1 = f32[32,3,128]{2,1,0:T(4,128)S(1)} custom-call(f32[16,128,128]{2,1,0:T(8,128)S(1)} %bitcast.21, bf16[16,128,128]{2,1,0:T(8,128)(2,1)S(1)} %collective-permute-done.refs_0_, bf16[16,128,128]{2,1,0:T(8,128)(2,1)S(1)} %collective-permute-done.1.refs_1_, bf16[16,128,128]{2,1,0:T(8,128)(2,1)S(1)} %collective-permute-done.2.refs_2_, ...), custom_call_target="tpu_custom_call" | custom-call | tf_op jit(solution)/shard_map/contract/pallas_call | solution.py:222
  67.5 13.8 %all_to_all.26 = f32[32,3,128]{2,1,0:T(4,128)S(1)} all-to-all(f32[32,3,128]{2,1,0:T(4,128)S(1)} %contract.1), channel_id=1, replica_groups=mesh['row'=8,'zh'=4,'y'=4,'zl'=4] {'row','y'}, dimensions={0} | all-to-all | bytes 98304 | tf_op jit(solution)/shard_map/all_to_all | solution.py:148
  81.4 24.0 %all_to_all.27 = f32[16,3,128]{2,1,0:T(4,128)S(1)} all-to-all(f32[16,3,128]{2,1,0:T(4,128)S(1)} %broadcast_in_dim.6), channel_id=1, replica_groups=mesh['row'=8,'zh'=4,'y'=4,'zl'=4] {'zh','zl'}, dimensions={0} | all-to-all | bytes 49152 | tf_op jit(solution)/shard_map/all_to_all | solution.py:148
  105.4 12.3 %all_to_all.28 = f32[32,3,128]{2,1,0:T(4,128)S(1)} all-to-all(f32[32,3,128]{2,1,0:T(4,128)S(1)} %broadcast_in_dim.7), channel_id=1, replica_groups=mesh['row'=8,'zh'=4,'y'=4,'zl'=4] {'row','y'}, dimensions={0} | all-to-all | bytes 98304 | tf_op jit(solution)/shard_map/all_to_all | solution.py:148
  117.8 0.1 fusion.1
  117.9 0.6 maximum_maximum_fusion
  (5 shorter events, 0.1 us)
Async XLA Ops:
  0.0 30.7 %copy-start = (bf16[1,1,128,4096]{3,2,1,0:T(8,128)(2,1)S(1)}, bf16[1,1,128,4096]{3,2,1,0:T(8,128)(2,1)}, u32[]{:S(2)}) copy-start(bf16[1,1,128,4096]{3,2,1,0:T(8,128)(2,1)} %param.6) | copy-start | bytes 3145732
  19.5 44.1 %all-to-all-start.1 = ((bf16[16,128,128]{2,1,0:T(8,128)(2,1)}), bf16[16,128,128]{2,1,0:T(8,128)(2,1)S(1)}, u32[]{:S(2)}, u32[]{:S(2)}) async-start(bf16[16,128,128]{2,1,0:T(8,128)(2,1)} %get-tuple-element.16), calls=%async_computation.1 | async-start | bytes 1048576 | tf_op jit(solution)/shard_map/all_to_all | solution.py:148
  30.7 0.7 copy-start.1
  30.7 0.7 copy-start.2
  33.9 15.0 %collective-permute-start = (bf16[16,128,128]{2,1,0:T(8,128)(2,1)S(1)}, bf16[16,128,128]{2,1,0:T(8,128)(2,1)S(1)}, u32[]{:S(2)}, u32[]{:S(2)}) collective-permute-start(bf16[16,128,128]{2,1,0:T(8,128)(2,1)S(1)} %bitcast.28), channel_id=1, source_target_pairs={{0,4},{4,8},{8,12},{12,0},{1,5},{5,9},{9,13},{13,1},{2,6},{6,10},{... | collective-permute-start | bytes 1572872 | tf_op jit(solution)/shard_map/ppermute | solution.py:216
  36.7 25.3 %collective-permute-start.1 = (bf16[16,128,128]{2,1,0:T(8,128)(2,1)S(1)}, bf16[16,128,128]{2,1,0:T(8,128)(2,1)S(1)}, u32[]{:S(2)}, u32[]{:S(2)}) collective-permute-start(bf16[16,128,128]{2,1,0:T(8,128)(2,1)S(1)} %bitcast.27), channel_id=1, source_target_pairs={{0,8},{4,12},{8,0},{12,4},{1,9},{5,13},{9,1},{13,5},{2,10},{6,14},... | collective-permute-start | bytes 1572872 | tf_op jit(solution)/shard_map/ppermute | solution.py:216
  41.6 22.0 %collective-permute-start.2 = (bf16[16,128,128]{2,1,0:T(8,128)(2,1)S(1)}, bf16[16,128,128]{2,1,0:T(8,128)(2,1)S(1)}, u32[]{:S(2)}, u32[]{:S(2)}) collective-permute-start(bf16[16,128,128]{2,1,0:T(8,128)(2,1)S(1)} %bitcast.26), channel_id=1, source_target_pairs={{0,12},{4,0},{8,4},{12,8},{1,13},{5,1},{9,5},{13,9},{2,14},{6,2},{... | collective-permute-start | bytes 1572872 | tf_op jit(solution)/shard_map/ppermute | solution.py:216

commit v5 on v4

--- a/solution.py
+++ b/solution.py
@@ -14,10 +14,8 @@
 COL_LAYER = ("zh", "y", "zl")
 Z = ("zh", "zl")
 ROW_Y = ("row", "y")
-PARTS = 4
 VMEM = pl.BlockSpec(memory_space=pltpu.VMEM)
 ANY = pl.BlockSpec(memory_space=pl.ANY)
-HBM = pl.BlockSpec(memory_space=pltpu.HBM)
 
 
 def lane_swapped(x):
@@ -51,18 +49,13 @@
         turned_ref[z] = turned
 
 
-def product_kernel(rows, cols, count, own_y, a_hbm, w_hbm, *refs):
-    *out_hbm, tiles_in, window, split, total, rounded, in_sems, out_sems = refs
+def product_kernel(rows, cols, count, own_y, a_hbm, window, *refs):
+    *out_hbm, tiles_in, split, total, rounded, in_sem, out_sems = refs
     live = count[0]
-    in_copies = [
-        pltpu.make_async_copy(a_hbm, tiles_in, in_sems.at[0]),
-        pltpu.make_async_copy(w_hbm, window, in_sems.at[1]),
-    ]
-    for copy in in_copies:
-        copy.start()
+    in_copy = pltpu.make_async_copy(a_hbm, tiles_in, in_sem)
+    in_copy.start()
     total[...] = jnp.zeros_like(total)
-    for copy in in_copies:
-        copy.wait()
+    in_copy.wait()
 
     def place(row):
         f = row & (TILE - 1)
@@ -111,37 +104,26 @@
         copy.wait()
 
 
-def contract_kernel(own_hbm, *refs):
-    *p_hbm, w_hbm, out_ref, own_buf, p_buf, w_buf, sems = refs
-    pieces, parts = w_hbm.shape[0], sems.shape[0]
-    size = pieces // parts
-    copies = []
-    for part in range(parts):
-        there = pl.ds(part * size, size)
-        pairs = [(own_hbm.at[there], own_buf.at[there]), (w_hbm.at[there], w_buf.at[there])]
-        pairs += [(p.at[there], p_buf.at[i, there]) for i, p in enumerate(p_hbm)]
-        copies.append(
-            [pltpu.make_async_copy(*pair, sems.at[part, i]) for i, pair in enumerate(pairs)]
-        )
-        for copy in copies[-1]:
-            copy.start()
+def contract_kernel(own_ref, *refs):
+    *p_refs, w_ref, out_ref = refs
     galerkin = jnp.zeros((LANES, LANES), jnp.float32)
-    for part in range(parts):
-        for copy in copies[part]:
-            copy.wait()
-        for z in range(part * size, (part + 1) * size):
-            block = own_buf[z]
-            for i in range(len(p_hbm)):
-                block += p_buf[i, z].astype(jnp.float32)
-            high = block.astype(jnp.bfloat16)
-            low = (block - high.astype(jnp.float32)).astype(jnp.bfloat16)
-            galerkin += jnp.dot(w_buf[z], high, preferred_element_type=jnp.float32)
-            galerkin += jnp.dot(w_buf[z], low, preferred_element_type=jnp.float32)
+    for z in range(w_ref.shape[0]):
+        block = own_ref[z]
+        for p_ref in p_refs:
+            block += p_ref[z].astype(jnp.float32)
+        high = block.astype(jnp.bfloat16)
+        low = (block - high.astype(jnp.float32)).astype(jnp.bfloat16)
+        galerkin += jnp.dot(w_ref[z], high, preferred_element_type=jnp.float32)
+        galerkin += jnp.dot(w_ref[z], low, preferred_element_type=jnp.float32)
     out_ref[:, 0, :] = galerkin[:HALF]
     out_ref[:, 1, :] = galerkin[HALF:TILE]
     corner = galerkin[TILE:]
     lane = lax.broadcasted_iota(jnp.int32, (HALF, LANES), 1)
     out_ref[:, 2, :] = jnp.where(lane < TILE, lane_swapped(corner[:HALF]), corner[HALF:])
+
+
+def in_vmem(x):
+    return pltpu.with_memory_space_constraint(x, pltpu.VMEM)
 
 
 def exchanged(x, axes):
@@ -183,24 +165,24 @@
     products = pl.pallas_call(
         product_kernel,
         out_shape=[
-            jax.ShapeDtypeStruct((places, TILE, LANES), jnp.bfloat16 if distance else jnp.float32)
+            jax.ShapeDtypeStruct(
+                (places, TILE, LANES), jnp.bfloat16 if distance else jnp.float32
+            )
             for distance in range(n_y)
         ],
         grid_spec=pltpu.PrefetchScalarGridSpec(
             num_scalar_prefetch=4,
-            in_specs=[HBM, ANY],
-            out_specs=[ANY] + [HBM] * (n_y - 1),
+            in_specs=[ANY, VMEM],
+            out_specs=[ANY] * n_y,
             scratch_shapes=[
                 pltpu.VMEM((total_slots, area), jnp.bfloat16),
-                pltpu.VMEM((n_row * local_rows, TILE, LANES), jnp.bfloat16),
                 pltpu.VMEM((HALF, CHUNK, LANES), jnp.float32),
                 pltpu.VMEM((n_y * places, TILE, LANES), jnp.float32),
                 pltpu.VMEM((n_y - 1, places, TILE, LANES), jnp.bfloat16),
-                pltpu.SemaphoreType.DMA((2,)),
+                pltpu.SemaphoreType.DMA,
                 pltpu.SemaphoreType.DMA((n_y,)),
             ],
         ),
-        compiler_params=pltpu.CompilerParams(vmem_limit_bytes=16 << 20),
         name="product",
     )(
         a_rows.reshape(total_slots),
@@ -208,7 +190,7 @@
         a_count.reshape(1),
         lax.axis_index("y").reshape(1),
         a_tiles.reshape(total_slots, area),
-        column_window,
+        in_vmem(column_window),
     )
     gathered = [products[0].reshape(depth, LANES, LANES)]
     for distance in range(1, n_y):
@@ -222,17 +204,11 @@
     galerkin = pl.pallas_call(
         contract_kernel,
         out_shape=jax.ShapeDtypeStruct((HALF, 3, LANES), jnp.float32),
-        in_specs=[ANY] * (n_y + 1),
+        in_specs=[VMEM] * (n_y + 1),
         out_specs=VMEM,
-        scratch_shapes=[
-            pltpu.VMEM((depth, LANES, LANES), jnp.float32),
-            pltpu.VMEM((n_y - 1, depth, LANES, LANES), jnp.bfloat16),
-            pltpu.VMEM((depth, LANES, LANES), jnp.bfloat16),
-            pltpu.SemaphoreType.DMA((PARTS, n_y + 1)),
-        ],
         compiler_params=pltpu.CompilerParams(vmem_limit_bytes=8 << 20),
         name="contract",
-    )(*gathered, turned)
+    )(*[in_vmem(x) for x in (*gathered, turned)])
     total = summed_over_all(galerkin)
     corner = jnp.concatenate([total[:, 2, :TILE], total[:, 2, TILE:]], axis=0)
     upper = jnp.concatenate([total[:, 0], total[:, 1]], axis=0)
@@ -252,6 +228,4 @@
         P("row", COL_LAYER, None, None),
         P("row", COL_LAYER, None),
     )
-    return jax.shard_map(
-        coarse_blocks, mesh=torus, in_specs=in_specs, out_specs=P(), check_vma=False
-    )
+    return jax.shard_map(coarse_blocks, mesh=torus, in_specs=in_specs, out_specs=P(), check_vma=False)

time: 119 us -> 118 us (level)
  Pallas kernels: 9.28 us -> 7.82 us
    pallas_call x1, Pallas kernels: 3.92 us -> 0.55 us  [coarse_blocks(): pl.pallas_call(contract_kernel, out_shape=jax.ShapeDtypeStruct((HALF, 3,...]
    pallas_call x1, Pallas kernels: 2.5 us -> 4.54 us  [coarse_blocks(): pl.pallas_call(product_kernel, out_shape=[jax.ShapeDtypeStruct((places, T...]
  transfers between devices with their start and end apart: 4 -> 4, of which waited for: 3 -> 3; matrix products, arithmetic and copies ran while one was open for 0% -> 0% of each run, Pallas kernels for 2% -> 4%
where the time goes in v5:
time: 118 us
  blocking collectives  66.7 us (57%)
  starting transfers between devices  21.3 us (18%)
  waiting for transfers between devices  19.3 us (16%)
  Pallas kernels  7.82 us (7%)
  local copies, waits for them, and re-layouts  1.37 us (1%)
    all_to_all x4, blocking collectives, exchanged(): return lax.all_to_all(x, axes, 0, 0, tiled=True)  66.7 us
    ppermute x3, waiting for transfers between devices, coarse_blocks(): lax.ppermute(products[distance].reshape(depth, LANES, LANES), 'y', [(y, (...  19.3 us
    ppermute x3, starting transfers between devices, coarse_blocks(): lax.ppermute(products[distance].reshape(depth, LANES, LANES), 'y', [(y, (...  10.7 us
    all_to_all x1, starting transfers between devices, exchanged(): return lax.all_to_all(x, axes, 0, 0, tiled=True)  10.6 us
    pallas_call x1, Pallas kernels, coarse_blocks(): pl.pallas_call(product_kernel, out_shape=[jax.ShapeDtypeStruct((places, T...  4.54 us
    pallas_call x1, Pallas kernels, coarse_blocks(): pl.pallas_call(window_kernel, out_shape=(jax.ShapeDtypeStruct((n_row, loc...  2.73 us
  transfers between devices with their start and end apart: 4, of which 3 were waited for; matrix products, arithmetic and copies ran while one was open for 0% of the time, Pallas kernels for 4%

profile of v5, /device:TPU:1, one launch (start us, length us, event | category | flops | bytes accessed | tf_op | source)
XLA Modules:
  0.0 117.8 jit_solution(959699021841973254)
XLA Ops:
  0.0 2.7 %window.1 = (bf16[8,2,64,128]{3,2,1,0:T(8,128)(2,1)}, bf16[16,128,128]{2,1,0:T(8,128)(2,1)}) custom-call(s32[2,4]{1,0:T(2,128)} %bitcast.29, bf16[2,4,4096]{2,1,0:T(4,128)(2,1)} %bitcast.24), custom_call_target="tpu_custom_call" | custom-call | tf_op jit(solution)/shard_map/window/pallas_call | solution.py:146
  2.7 16.6 %all_to_all.25 = bf16[8,2,64,128]{3,2,1,0:T(8,128)(2,1)S(1)} all-to-all(bf16[8,2,64,128]{3,2,1,0:T(8,128)(2,1)} %get-tuple-element.11), channel_id=1, replica_groups=mesh['row'=8,'zh'=4,'y'=4,'zl'=4] {'row'}, dimensions={0} | all-to-all | bytes 524288 | tf_op jit(solution)/shard_map/all_to_all | solution.py:130
  19.3 10.6 %all-to-all-start.1 = ((bf16[16,128,128]{2,1,0:T(8,128)(2,1)}), bf16[16,128,128]{2,1,0:T(8,128)(2,1)S(1)}, u32[]{:S(2)}, u32[]{:S(2)}) async-start(bf16[16,128,128]{2,1,0:T(8,128)(2,1)} %get-tuple-element.16), calls=%async_computation.1 | async-start | bytes 1048576 | tf_op jit(solution)/shard_map/all_to_all | solution.py:130
  30.6 4.5 %product.1 = (f32[32,64,128]{2,1,0:T(8,128)}, bf16[32,64,128]{2,1,0:T(8,128)(2,1)}, bf16[32,64,128]{2,1,0:T(8,128)(2,1)}, bf16[32,64,128]{2,1,0:T(8,128)(2,1)}) custom-call(s32[128]{0:T(128)} %bitcast.30, s32[128]{0:T(128)} %bitcast.31, s32[1]{0:T(128)} %bitcast.20.count, s32[1]{0:T(128)} %bitcast.3.own_y, bf16[128,4096]{1,0:T(8,128)(2,1)} %bitcast.23, ...), custom_call_target="tpu_custom_call" | custom-call | tf_op jit(solution)/shard_map/product/pallas_call | solution.py:165
  35.1 2.8 %collective-permute-start = (bf16[16,128,128]{2,1,0:T(8,128)(2,1)}, bf16[16,128,128]{2,1,0:T(8,128)(2,1)S(1)}, u32[]{:S(2)}, u32[]{:S(2)}) collective-permute-start(bf16[16,128,128]{2,1,0:T(8,128)(2,1)} %bitcast.34), channel_id=1, source_target_pairs={{0,4},{4,8},{8,12},{12,0},{1,5},{5,9},{9,13},{13,1},{2,6},{6,10},{... | collective-permute-start | bytes 1572872 | tf_op jit(solution)/shard_map/ppermute | solution.py:198
  37.9 4.9 %collective-permute-start.1 = (bf16[16,128,128]{2,1,0:T(8,128)(2,1)}, bf16[16,128,128]{2,1,0:T(8,128)(2,1)S(1)}, u32[]{:S(2)}, u32[]{:S(2)}) collective-permute-start(bf16[16,128,128]{2,1,0:T(8,128)(2,1)} %bitcast.33), channel_id=1, source_target_pairs={{0,8},{4,12},{8,0},{12,4},{1,9},{5,13},{9,1},{13,5},{2,10},{6,14},... | collective-permute-start | bytes 1572872 | tf_op jit(solution)/shard_map/ppermute | solution.py:198
  42.9 3.0 %collective-permute-start.2 = (bf16[16,128,128]{2,1,0:T(8,128)(2,1)}, bf16[16,128,128]{2,1,0:T(8,128)(2,1)S(1)}, u32[]{:S(2)}, u32[]{:S(2)}) collective-permute-start(bf16[16,128,128]{2,1,0:T(8,128)(2,1)} %bitcast.32), channel_id=1, source_target_pairs={{0,12},{4,0},{8,4},{12,8},{1,13},{5,1},{9,5},{13,9},{2,14},{6,2},{... | collective-permute-start | bytes 1572872 | tf_op jit(solution)/shard_map/ppermute | solution.py:198
  45.8 4.5 %collective-permute-done.refs_0_ = bf16[16,128,128]{2,1,0:T(8,128)(2,1)S(1)} collective-permute-done((bf16[16,128,128]{2,1,0:T(8,128)(2,1)}, bf16[16,128,128]{2,1,0:T(8,128)(2,1)S(1)}, u32[]{:S(2)}, u32[]{:S(2)}) %collective-permute-start) | collective-permute-done | bytes 524320 | tf_op jit(solution)/shard_map/ppermute | solution.py:198
  50.3 13.1 %collective-permute-done.1.refs_1_ = bf16[16,128,128]{2,1,0:T(8,128)(2,1)S(1)} collective-permute-done((bf16[16,128,128]{2,1,0:T(8,128)(2,1)}, bf16[16,128,128]{2,1,0:T(8,128)(2,1)S(1)}, u32[]{:S(2)}, u32[]{:S(2)}) %collective-permute-start.1) | collective-permute-done | bytes 524320 | tf_op jit(solution)/shard_map/ppermute | solution.py:198
  63.4 1.7 %collective-permute-done.2.refs_2_ = bf16[16,128,128]{2,1,0:T(8,128)(2,1)S(1)} collective-permute-done((bf16[16,128,128]{2,1,0:T(8,128)(2,1)}, bf16[16,128,128]{2,1,0:T(8,128)(2,1)S(1)}, u32[]{:S(2)}, u32[]{:S(2)}) %collective-permute-start.2) | collective-permute-done | bytes 524320 | tf_op jit(solution)/shard_map/ppermute | solution.py:198
  65.2 0.0 all-to-all-done.1.refs_3_
  65.2 0.0 copy-start
  65.2 1.2 %copy-done = f32[32,64,128]{2,1,0:T(8,128)S(1)} copy-done((f32[32,64,128]{2,1,0:T(8,128)S(1)}, f32[32,64,128]{2,1,0:T(8,128)}, u32[]{:S(2)}) %copy-start) | copy-done | bytes 1048600
  66.4 0.5 contract.1
  66.9 13.7 %all_to_all.26 = f32[32,3,128]{2,1,0:T(4,128)S(1)} all-to-all(f32[32,3,128]{2,1,0:T(4,128)S(1)} %contract.1), channel_id=1, replica_groups=mesh['row'=8,'zh'=4,'y'=4,'zl'=4] {'row','y'}, dimensions={0} | all-to-all | bytes 98304 | tf_op jit(solution)/shard_map/all_to_all | solution.py:130
  80.7 24.0 %all_to_all.27 = f32[16,3,128]{2,1,0:T(4,128)S(1)} all-to-all(f32[16,3,128]{2,1,0:T(4,128)S(1)} %broadcast_in_dim.6), channel_id=1, replica_groups=mesh['row'=8,'zh'=4,'y'=4,'zl'=4] {'zh','zl'}, dimensions={0} | all-to-all | bytes 49152 | tf_op jit(solution)/shard_map/all_to_all | solution.py:130
  104.7 12.3 %all_to_all.28 = f32[32,3,128]{2,1,0:T(4,128)S(1)} all-to-all(f32[32,3,128]{2,1,0:T(4,128)S(1)} %broadcast_in_dim.7), channel_id=1, replica_groups=mesh['row'=8,'zh'=4,'y'=4,'zl'=4] {'row','y'}, dimensions={0} | all-to-all | bytes 98304 | tf_op jit(solution)/shard_map/all_to_all | solution.py:130
  117.1 0.1 fusion.1
  117.2 0.6 maximum_maximum_fusion
  (5 shorter events, 0.1 us)
Async XLA Ops:
  19.3 45.8 %all-to-all-start.1 = ((bf16[16,128,128]{2,1,0:T(8,128)(2,1)}), bf16[16,128,128]{2,1,0:T(8,128)(2,1)S(1)}, u32[]{:S(2)}, u32[]{:S(2)}) async-start(bf16[16,128,128]{2,1,0:T(8,128)(2,1)} %get-tuple-element.16), calls=%async_computation.1 | async-start | bytes 1048576 | tf_op jit(solution)/shard_map/all_to_all | solution.py:130
  35.1 15.2 %collective-permute-start = (bf16[16,128,128]{2,1,0:T(8,128)(2,1)}, bf16[16,128,128]{2,1,0:T(8,128)(2,1)S(1)}, u32[]{:S(2)}, u32[]{:S(2)}) collective-permute-start(bf16[16,128,128]{2,1,0:T(8,128)(2,1)} %bitcast.34), channel_id=1, source_target_pairs={{0,4},{4,8},{8,12},{12,0},{1,5},{5,9},{9,13},{13,1},{2,6},{6,10},{... | collective-permute-start | bytes 1572872 | tf_op jit(solution)/shard_map/ppermute | solution.py:198
  37.9 25.5 %collective-permute-start.1 = (bf16[16,128,128]{2,1,0:T(8,128)(2,1)}, bf16[16,128,128]{2,1,0:T(8,128)(2,1)S(1)}, u32[]{:S(2)}, u32[]{:S(2)}) collective-permute-start(bf16[16,128,128]{2,1,0:T(8,128)(2,1)} %bitcast.33), channel_id=1, source_target_pairs={{0,8},{4,12},{8,0},{12,4},{1,9},{5,13},{9,1},{13,5},{2,10},{6,14},... | collective-permute-start | bytes 1572872 | tf_op jit(solution)/shard_map/ppermute | solution.py:198
  42.9 22.3 %collective-permute-start.2 = (bf16[16,128,128]{2,1,0:T(8,128)(2,1)}, bf16[16,128,128]{2,1,0:T(8,128)(2,1)S(1)}, u32[]{:S(2)}, u32[]{:S(2)}) collective-permute-start(bf16[16,128,128]{2,1,0:T(8,128)(2,1)} %bitcast.32), channel_id=1, source_target_pairs={{0,12},{4,0},{8,4},{12,8},{1,13},{5,1},{9,5},{13,9},{2,14},{6,2},{... | collective-permute-start | bytes 1572872 | tf_op jit(solution)/shard_map/ppermute | solution.py:198
  65.2 1.2 %copy-start = (f32[32,64,128]{2,1,0:T(8,128)S(1)}, f32[32,64,128]{2,1,0:T(8,128)}, u32[]{:S(2)}) copy-start(f32[32,64,128]{2,1,0:T(8,128)} %get-tuple-element.12) | copy-start | bytes 3145732

commit v6 on v5

--- a/solution.py
+++ b/solution.py
@@ -11,6 +11,7 @@
 LANES = 2 * TILE
 CHUNK = 16
 GROUP = 4
+NEAR = (0, 1, 2, 15)
 COL_LAYER = ("zh", "y", "zl")
 Z = ("zh", "zl")
 ROW_Y = ("row", "y")
@@ -49,42 +50,41 @@
         turned_ref[z] = turned
 
 
-def product_kernel(rows, cols, count, own_y, a_hbm, window, *refs):
-    *out_hbm, tiles_in, split, total, rounded, in_sem, out_sems = refs
-    live = count[0]
-    in_copy = pltpu.make_async_copy(a_hbm, tiles_in, in_sem)
-    in_copy.start()
-    total[...] = jnp.zeros_like(total)
-    in_copy.wait()
-
-    def place(row):
-        f = row & (TILE - 1)
-        z = ((f >> 4) << 2) | (f & 3)
-        distance = ((f >> 2) - own_y[0]) & 3
-        return (distance * 16 + z) * 2 + (row >> 6)
-
+def unfold_kernel(tiles, out_ref, split):
     def chunk(turn, carry):
         first = pl.multiple_of(turn * CHUNK, CHUNK)
-        tiles = tiles_in[pl.ds(first, CHUNK), :].astype(jnp.float32)
-        slot = first + lax.broadcasted_iota(jnp.int32, tiles.shape, 0)
-        tiles = jnp.where(slot < live, tiles, 0.0)
+        some = tiles[pl.ds(first, CHUNK), :].astype(jnp.float32)
         for k in range(HALF):
-            split[k] = tiles[:, k * LANES : (k + 1) * LANES]
+            split[k] = some[:, k * LANES : (k + 1) * LANES]
+        for i in range(CHUNK):
+            x = split[:, i, :]
+            out_ref[first + i] = jnp.concatenate([x, lane_swapped(x)], axis=0).astype(jnp.bfloat16)
+        return carry
+
+    lax.fori_loop(0, tiles.shape[0] // CHUNK, chunk, 0)
+
+
+def product_kernel(slots, tiles, window, *refs):
+    *out_hbm, total, rounded, out_sems = refs
+    total[...] = jnp.zeros_like(total)
+
+    def chunk(turn, carry):
+        first = turn * CHUNK
         for g in range(0, CHUNK, GROUP):
-            parts = []
-            for i in range(g, g + GROUP):
-                x = split[:, i, :]
-                tile = jnp.concatenate([x, lane_swapped(x)], axis=0).astype(jnp.bfloat16)
-                parts.append(
-                    jnp.dot(
-                        tile[:, :TILE], window[cols[first + i]], preferred_element_type=jnp.float32
-                    )
+            held = [slots[first + i] for i in range(g, g + GROUP)]
+            parts = [
+                jnp.dot(
+                    tiles[first + g + i, :, :TILE],
+                    window[held[i] & 15],
+                    preferred_element_type=jnp.float32,
                 )
-            for i in range(g, g + GROUP):
-                total[place(rows[first + i])] += parts[i - g]
+                for i in range(GROUP)
+            ]
+            for i in range(GROUP):
+                total[held[i] >> 4] += parts[i]
         return carry
 
-    lax.fori_loop(0, (live + CHUNK - 1) // CHUNK, chunk, 0)
+    lax.fori_loop(0, tiles.shape[0] // CHUNK, chunk, 0)
     size = out_hbm[0].shape[0]
     out_copies = [pltpu.make_async_copy(total.at[pl.ds(0, size)], out_hbm[0], out_sems.at[0])]
     out_copies[0].start()
@@ -104,17 +104,17 @@
         copy.wait()
 
 
-def contract_kernel(own_ref, *refs):
-    *p_refs, w_ref, out_ref = refs
+def contract_kernel(*refs):
+    p_refs, (*w_refs, out_ref) = refs[:4], refs[4:]
     galerkin = jnp.zeros((LANES, LANES), jnp.float32)
-    for z in range(w_ref.shape[0]):
-        block = own_ref[z]
-        for p_ref in p_refs:
-            block += p_ref[z].astype(jnp.float32)
-        high = block.astype(jnp.bfloat16)
-        low = (block - high.astype(jnp.float32)).astype(jnp.bfloat16)
-        galerkin += jnp.dot(w_ref[z], high, preferred_element_type=jnp.float32)
-        galerkin += jnp.dot(w_ref[z], low, preferred_element_type=jnp.float32)
+    for near, w_ref in enumerate(w_refs):
+        for zh in range(w_ref.shape[0]):
+            piece = near * w_ref.shape[0] + zh
+            block = sum(p_ref[piece].astype(jnp.float32) for p_ref in p_refs)
+            high = block.astype(jnp.bfloat16)
+            low = (block - high.astype(jnp.float32)).astype(jnp.bfloat16)
+            galerkin += jnp.dot(w_ref[zh], high, preferred_element_type=jnp.float32)
+            galerkin += jnp.dot(w_ref[zh], low, preferred_element_type=jnp.float32)
     out_ref[:, 0, :] = galerkin[:HALF]
     out_ref[:, 1, :] = galerkin[HALF:TILE]
     corner = galerkin[TILE:]
@@ -130,6 +130,11 @@
     return lax.all_to_all(x, axes, 0, 0, tiled=True)
 
 
+def moved(x, axes, distance):
+    peers = lax.axis_size(axes)
+    return lax.ppermute(x, axes, [(i, (i + distance) % peers) for i in range(peers)])
+
+
 def summed_over_all(x):
     peers, depth = lax.axis_size(ROW_Y), lax.axis_size(Z)
     piece = jnp.sum(exchanged(x, ROW_Y), axis=0)
@@ -137,17 +142,28 @@
     return exchanged(jnp.broadcast_to(piece, (peers, *piece.shape)), ROW_Y)
 
 
+def slot_table(a_rows, a_cols, a_count):
+    rows, cols = a_rows.reshape(-1), a_cols.reshape(-1)
+    f = rows % TILE
+    zh, y, zl = f // 16, f // 4 % 4, f % 4
+    y_distance = (y - lax.axis_index("y")) % 4
+    z_distance = (lax.axis_index("zl") - zl) % 4
+    place = ((y_distance * 4 + z_distance) * 4 + zh) * 2 + rows // TILE
+    live = jnp.arange(rows.shape[0], dtype=jnp.int32) < a_count.reshape(())
+    return jnp.where(live, place, 128) * 16 + cols
+
+
 def coarse_blocks(a_tiles, a_rows, a_cols, a_count, p_tiles, p_cols):
     local_rows, _, slots, area = p_tiles.shape
     total_slots = a_tiles.shape[2]
     n_row, n_y = lax.axis_size("row"), lax.axis_size("y")
-    depth = lax.axis_size(Z)
-    places = depth * local_rows
+    n_zh, n_zl = lax.axis_size("zh"), lax.axis_size("zl")
+    places = n_zh * n_zl * local_rows
     own_rows, own_turned = pl.pallas_call(
         window_kernel,
         out_shape=(
             jax.ShapeDtypeStruct((n_row, local_rows, TILE, LANES), jnp.bfloat16),
-            jax.ShapeDtypeStruct((depth, LANES, LANES), jnp.bfloat16),
+            jax.ShapeDtypeStruct((n_zh, LANES, LANES), jnp.bfloat16),
         ),
         grid_spec=pltpu.PrefetchScalarGridSpec(
             num_scalar_prefetch=1,
@@ -161,7 +177,16 @@
         name="window",
     )(p_cols.reshape(local_rows, slots), p_tiles.reshape(local_rows, slots, area))
     column_window = exchanged(own_rows, "row").reshape(n_row * local_rows, TILE, LANES)
-    turned = exchanged(own_turned, Z)
+    unfolded = pl.pallas_call(
+        unfold_kernel,
+        out_shape=jax.ShapeDtypeStruct((total_slots, TILE, LANES), jnp.bfloat16),
+        in_specs=[VMEM],
+        out_specs=VMEM,
+        scratch_shapes=[pltpu.VMEM((HALF, CHUNK, LANES), jnp.float32)],
+        compiler_params=pltpu.CompilerParams(vmem_limit_bytes=8 << 20),
+        name="unfold",
+    )(in_vmem(a_tiles.reshape(total_slots, area)))
+    pieces = [exchanged(own_turned, "zh")]
     products = pl.pallas_call(
         product_kernel,
         out_shape=[
@@ -171,44 +196,30 @@
             for distance in range(n_y)
         ],
         grid_spec=pltpu.PrefetchScalarGridSpec(
-            num_scalar_prefetch=4,
-            in_specs=[ANY, VMEM],
+            num_scalar_prefetch=1,
+            in_specs=[VMEM, VMEM],
             out_specs=[ANY] * n_y,
             scratch_shapes=[
-                pltpu.VMEM((total_slots, area), jnp.bfloat16),
-                pltpu.VMEM((HALF, CHUNK, LANES), jnp.float32),
-                pltpu.VMEM((n_y * places, TILE, LANES), jnp.float32),
+                pltpu.VMEM((n_y * places + 1, TILE, LANES), jnp.float32),
                 pltpu.VMEM((n_y - 1, places, TILE, LANES), jnp.bfloat16),
-                pltpu.SemaphoreType.DMA,
                 pltpu.SemaphoreType.DMA((n_y,)),
             ],
         ),
         name="product",
-    )(
-        a_rows.reshape(total_slots),
-        a_cols.reshape(total_slots),
-        a_count.reshape(1),
-        lax.axis_index("y").reshape(1),
-        a_tiles.reshape(total_slots, area),
-        in_vmem(column_window),
-    )
-    gathered = [products[0].reshape(depth, LANES, LANES)]
+    )(slot_table(a_rows, a_cols, a_count), in_vmem(unfolded), in_vmem(column_window))
+    gathered = [products[0].reshape(-1, LANES, LANES)]
     for distance in range(1, n_y):
-        gathered.append(
-            lax.ppermute(
-                products[distance].reshape(depth, LANES, LANES),
-                "y",
-                [(y, (y + distance) % n_y) for y in range(n_y)],
-            )
-        )
+        gathered.append(moved(products[distance].reshape(-1, LANES, LANES), "y", distance))
+    for distance in NEAR[1:]:
+        pieces.append(moved(pieces[0], Z, distance))
     galerkin = pl.pallas_call(
         contract_kernel,
         out_shape=jax.ShapeDtypeStruct((HALF, 3, LANES), jnp.float32),
-        in_specs=[VMEM] * (n_y + 1),
+        in_specs=[VMEM] * (n_y + n_zl),
         out_specs=VMEM,
         compiler_params=pltpu.CompilerParams(vmem_limit_bytes=8 << 20),
         name="contract",
-    )(*[in_vmem(x) for x in (*gathered, turned)])
+    )(*[in_vmem(x) for x in (*gathered, *pieces)])
     total = summed_over_all(galerkin)
     corner = jnp.concatenate([total[:, 2, :TILE], total[:, 2, TILE:]], axis=0)
     upper = jnp.concatenate([total[:, 0], total[:, 1]], axis=0)

time: 118 us -> 117 us (level)
  starting transfers between devices: 21.3 us -> 40.7 us
  blocking collectives: 66.7 us -> 48.9 us
  waiting for transfers between devices: 19.3 us -> 12.7 us
  Pallas kernels: 7.82 us -> 9.57 us
  local copies, waits for them, and re-layouts: 1.37 us -> 2.6 us
    all_to_all x4 -> x3, blocking collectives: 66.7 us -> 48.9 us  [exchanged(): return lax.all_to_all(x, axes, 0, 0, tiled=True)]
    all_to_all x1 -> x2, starting transfers between devices: 10.6 us -> 20.6 us  [exchanged(): return lax.all_to_all(x, axes, 0, 0, tiled=True)]
    ppermute x3 -> x6, waiting for transfers between devices: 19.3 us -> 9.87 us  [moved(): lax.ppermute(x, axes, [(i, (i + distance) % peers) for i in range(peers)])]
    ppermute x3 -> x6, starting transfers between devices: 10.7 us -> 20.1 us  [moved(): lax.ppermute(x, axes, [(i, (i + distance) % peers) for i in range(peers)])]
    all_to_all x1 -> x2, waiting for transfers between devices: 0.01 us -> 2.82 us  [exchanged(): return lax.all_to_all(x, axes, 0, 0, tiled=True)]
    pallas_call x0 -> x1, Pallas kernels: none -> 1.79 us  [coarse_blocks(): pl.pallas_call(unfold_kernel, out_shape=jax.ShapeDtypeStruct((total_slots...]
    unnamed x2 -> x8, local copies, waits for them, and re-layouts: 1.23 us -> 2.45 us
  transfers between devices with their start and end apart: 4 -> 8, of which waited for: 3 -> 6; matrix products, arithmetic and copies ran while one was open for 0% -> 0% of each run, Pallas kernels for 4% -> 5%
where the time goes in v6:
time: 117 us; the launch traced here: 116 us
  blocking collectives  48.9 us (42%)
  starting transfers between devices  40.7 us (35%)
  waiting for transfers between devices  12.7 us (11%)
  Pallas kernels  9.57 us (8%)
  local copies, waits for them, and re-layouts  2.6 us (2%)
  other arithmetic  1.29 us (1%)
    all_to_all x3, blocking collectives, exchanged(): return lax.all_to_all(x, axes, 0, 0, tiled=True)  48.9 us
    all_to_all x2, starting transfers between devices, exchanged(): return lax.all_to_all(x, axes, 0, 0, tiled=True)  20.6 us
    ppermute x6, starting transfers between devices, moved(): lax.ppermute(x, axes, [(i, (i + distance) % peers) for i in range(peers)])  20.1 us
    ppermute x6, waiting for transfers between devices, moved(): lax.ppermute(x, axes, [(i, (i + distance) % peers) for i in range(peers)])  9.87 us
    pallas_call x1, Pallas kernels, coarse_blocks(): pl.pallas_call(product_kernel, out_shape=[jax.ShapeDtypeStruct((places, T...  4.51 us
    all_to_all x2, waiting for transfers between devices, exchanged(): return lax.all_to_all(x, axes, 0, 0, tiled=True)  2.82 us
    pallas_call x1, Pallas kernels, coarse_blocks(): pl.pallas_call(window_kernel, out_shape=(jax.ShapeDtypeStruct((n_row, loc...  2.72 us
    unnamed x8, local copies, waits for them, and re-layouts  2.45 us
  transfers between devices with their start and end apart: 8, of which 6 were waited for; matrix products, arithmetic and copies ran while one was open for 0% of the time, Pallas kernels for 5%

profile of v6, /device:TPU:1, one launch (start us, length us, event | category | flops | bytes accessed | tf_op | source)
XLA Modules:
  0.0 116.5 jit_solution(16369285463205695572)
XLA Ops:
  0.0 0.0 copy-start.3
  0.0 2.7 %window.1 = (bf16[8,2,64,128]{3,2,1,0:T(8,128)(2,1)}, bf16[4,128,128]{2,1,0:T(8,128)(2,1)}) custom-call(s32[2,4]{1,0:T(2,128)} %bitcast.41, bf16[2,4,4096]{2,1,0:T(4,128)(2,1)} %bitcast.36), custom_call_target="tpu_custom_call" | custom-call | tf_op jit(solution)/shard_map/window/pallas_call | solution.py:162
  2.7 10.1 %all-to-all-start = ((bf16[8,2,64,128]{3,2,1,0:T(8,128)(2,1)}), bf16[8,2,64,128]{3,2,1,0:T(8,128)(2,1)S(1)}, u32[]{:S(2)}, u32[]{:S(2)}) async-start(bf16[8,2,64,128]{3,2,1,0:T(8,128)(2,1)} %get-tuple-element.11), calls=%async_computation | async-start | bytes 524288 | tf_op jit(solution)/shard_map/all_to_all | solution.py:130
  13.5 0.0 copy-start
  13.5 1.2 %copy-done = bf16[1,1,128,4096]{3,2,1,0:T(8,128)(2,1)S(1)} copy-done((bf16[1,1,128,4096]{3,2,1,0:T(8,128)(2,1)S(1)}, bf16[1,1,128,4096]{3,2,1,0:T(8,128)(2,1)}, u32[]{:S(2)}) %copy-start) | copy-done | bytes 1048600
  14.8 1.8 %unfold.1.tiles = bf16[128,64,128]{2,1,0:T(8,128)(2,1)S(1)} custom-call(bf16[128,4096]{1,0:T(8,128)(2,1)S(1)} %bitcast.33), custom_call_target="tpu_custom_call" | custom-call | tf_op jit(solution)/shard_map/unfold/pallas_call | solution.py:180
  16.5 2.8 %all-to-all-done = bf16[8,2,64,128]{3,2,1,0:T(8,128)(2,1)S(1)} async-done(((bf16[8,2,64,128]{3,2,1,0:T(8,128)(2,1)}), bf16[8,2,64,128]{3,2,1,0:T(8,128)(2,1)S(1)}, u32[]{:S(2)}, u32[]{:S(2)}) %all-to-all-start) | async-done | bytes 262176 | tf_op jit(solution)/shard_map/all_to_all | solution.py:130
  19.4 10.4 %all-to-all-start.1 = ((bf16[4,128,128]{2,1,0:T(8,128)(2,1)}), bf16[4,128,128]{2,1,0:T(8,128)(2,1)S(1)}, u32[]{:S(2)}, u32[]{:S(2)}) async-start(bf16[4,128,128]{2,1,0:T(8,128)(2,1)} %get-tuple-element.16), calls=%async_computation.1 | async-start | bytes 262144 | tf_op jit(solution)/shard_map/all_to_all | solution.py:130
  29.8 0.0 copy-done.3
  29.8 0.0 copy-done.2
  29.8 0.6 fusion.2.slots
  30.4 4.5 %product.1 = (f32[32,64,128]{2,1,0:T(8,128)}, bf16[32,64,128]{2,1,0:T(8,128)(2,1)}, bf16[32,64,128]{2,1,0:T(8,128)(2,1)}, bf16[32,64,128]{2,1,0:T(8,128)(2,1)}) custom-call(s32[128]{0:T(128)} %fusion.2.slots, bf16[128,64,128]{2,1,0:T(8,128)(2,1)S(1)} %unfold.1.tiles, bf16[16,64,128]{2,1,0:T(8,128)(2,1)S(1)} %bitcast.35), custom_call_target="tpu_custom_call" | custom-call | tf_op jit(solution)/shard_map/product/pallas_call | solution.py:190
  34.9 3.2 %collective-permute-start = (bf16[16,128,128]{2,1,0:T(8,128)(2,1)}, bf16[16,128,128]{2,1,0:T(8,128)(2,1)S(1)}, u32[]{:S(2)}, u32[]{:S(2)}) collective-permute-start(bf16[16,128,128]{2,1,0:T(8,128)(2,1)} %bitcast.44), channel_id=1, source_target_pairs={{0,4},{4,8},{8,12},{12,0},{1,5},{5,9},{9,13},{13,1},{2,6},{6,10},{... | collective-permute-start | bytes 1572872 | tf_op jit(solution)/shard_map/ppermute | solution.py:135
  38.1 4.5 %collective-permute-start.1 = (bf16[16,128,128]{2,1,0:T(8,128)(2,1)}, bf16[16,128,128]{2,1,0:T(8,128)(2,1)S(1)}, u32[]{:S(2)}, u32[]{:S(2)}) collective-permute-start(bf16[16,128,128]{2,1,0:T(8,128)(2,1)} %bitcast.43), channel_id=1, source_target_pairs={{0,8},{4,12},{8,0},{12,4},{1,9},{5,13},{9,1},{13,5},{2,10},{6,14},... | collective-permute-start | bytes 1572872 | tf_op jit(solution)/shard_map/ppermute | solution.py:135
  42.6 3.0 %collective-permute-start.2 = (bf16[16,128,128]{2,1,0:T(8,128)(2,1)}, bf16[16,128,128]{2,1,0:T(8,128)(2,1)S(1)}, u32[]{:S(2)}, u32[]{:S(2)}) collective-permute-start(bf16[16,128,128]{2,1,0:T(8,128)(2,1)} %bitcast.42), channel_id=1, source_target_pairs={{0,12},{4,0},{8,4},{12,8},{1,13},{5,1},{9,5},{13,9},{2,14},{6,2},{... | collective-permute-start | bytes 1572872 | tf_op jit(solution)/shard_map/ppermute | solution.py:135
  45.6 0.0 all-to-all-done.1.refs_4_
  45.6 2.7 %collective-permute-start.3 = (bf16[4,128,128]{2,1,0:T(8,128)(2,1)S(1)}, bf16[4,128,128]{2,1,0:T(8,128)(2,1)S(1)}, u32[]{:S(2)}, u32[]{:S(2)}) collective-permute-start(bf16[4,128,128]{2,1,0:T(8,128)(2,1)S(1)} %all-to-all-done.1.refs_4_), channel_id=1, source_target_pairs={{0,1},{1,2},{2,3},{3,16},{16,17},{17,18},{18,19},{19,32},{32,33},{... | collective-permute-start | bytes 393224 | tf_op jit(solution)/shard_map/ppermute | solution.py:135
  48.3 3.1 %collective-permute-start.4 = (bf16[4,128,128]{2,1,0:T(8,128)(2,1)S(1)}, bf16[4,128,128]{2,1,0:T(8,128)(2,1)S(1)}, u32[]{:S(2)}, u32[]{:S(2)}) collective-permute-start(bf16[4,128,128]{2,1,0:T(8,128)(2,1)S(1)} %all-to-all-done.1.refs_4_), channel_id=1, source_target_pairs={{0,2},{1,3},{2,16},{3,17},{16,18},{17,19},{18,32},{19,33},{32,34},... | collective-permute-start | bytes 393224 | tf_op jit(solution)/shard_map/ppermute | solution.py:135
  51.4 2.5 %collective-permute-done.3.refs_5_ = bf16[4,128,128]{2,1,0:T(8,128)(2,1)S(1)} collective-permute-done((bf16[4,128,128]{2,1,0:T(8,128)(2,1)S(1)}, bf16[4,128,128]{2,1,0:T(8,128)(2,1)S(1)}, u32[]{:S(2)}, u32[]{:S(2)}) %collective-permute-start.3) | collective-permute-done | bytes 131104 | tf_op jit(solution)/shard_map/ppermute | solution.py:135
  53.9 3.6 %collective-permute-start.5 = (bf16[4,128,128]{2,1,0:T(8,128)(2,1)S(1)}, bf16[4,128,128]{2,1,0:T(8,128)(2,1)S(1)}, u32[]{:S(2)}, u32[]{:S(2)}) collective-permute-start(bf16[4,128,128]{2,1,0:T(8,128)(2,1)S(1)} %all-to-all-done.1.refs_4_), channel_id=1, source_target_pairs={{0,51},{1,0},{2,1},{3,2},{16,3},{17,16},{18,17},{19,18},{32,19},{3... | collective-permute-start | bytes 393224 | tf_op jit(solution)/shard_map/ppermute | solution.py:135
  57.6 1.2 %collective-permute-done.4.refs_6_ = bf16[4,128,128]{2,1,0:T(8,128)(2,1)S(1)} collective-permute-done((bf16[4,128,128]{2,1,0:T(8,128)(2,1)S(1)}, bf16[4,128,128]{2,1,0:T(8,128)(2,1)S(1)}, u32[]{:S(2)}, u32[]{:S(2)}) %collective-permute-start.4) | collective-permute-done | bytes 131104 | tf_op jit(solution)/shard_map/ppermute | solution.py:135
  58.8 1.1 collective-permute-done.5.refs_7_
  60.0 0.0 collective-permute-done.refs_1_
  60.0 2.8 %collective-permute-done.1.refs_2_ = bf16[16,128,128]{2,1,0:T(8,128)(2,1)S(1)} collective-permute-done((bf16[16,128,128]{2,1,0:T(8,128)(2,1)}, bf16[16,128,128]{2,1,0:T(8,128)(2,1)S(1)}, u32[]{:S(2)}, u32[]{:S(2)}) %collective-permute-start.1) | collective-permute-done | bytes 524320 | tf_op jit(solution)/shard_map/ppermute | solution.py:135
  62.8 2.1 %collective-permute-done.2.refs_3_ = bf16[16,128,128]{2,1,0:T(8,128)(2,1)S(1)} collective-permute-done((bf16[16,128,128]{2,1,0:T(8,128)(2,1)}, bf16[16,128,128]{2,1,0:T(8,128)(2,1)S(1)}, u32[]{:S(2)}, u32[]{:S(2)}) %collective-permute-start.2) | collective-permute-done | bytes 524320 | tf_op jit(solution)/shard_map/ppermute | solution.py:135
  64.9 1.2 %copy-done.1 = f32[32,64,128]{2,1,0:T(8,128)S(1)} copy-done((f32[32,64,128]{2,1,0:T(8,128)S(1)}, f32[32,64,128]{2,1,0:T(8,128)}, u32[]{:S(2)}) %copy-start.1) | copy-done | bytes 1048600
  66.2 0.5 contract.1
  66.7 13.7 %all_to_all.25 = f32[32,3,128]{2,1,0:T(4,128)S(1)} all-to-all(f32[32,3,128]{2,1,0:T(4,128)S(1)} %contract.1), channel_id=1, replica_groups=mesh['row'=8,'zh'=4,'y'=4,'zl'=4] {'row','y'}, dimensions={0} | all-to-all | bytes 98304 | tf_op jit(solution)/shard_map/all_to_all | solution.py:130
  80.5 22.9 %all_to_all.26 = f32[16,3,128]{2,1,0:T(4,128)S(1)} all-to-all(f32[16,3,128]{2,1,0:T(4,128)S(1)} %broadcast_in_dim.11), channel_id=1, replica_groups=mesh['row'=8,'zh'=4,'y'=4,'zl'=4] {'zh','zl'}, dimensions={0} | all-to-all | bytes 49152 | tf_op jit(solution)/shard_map/all_to_all | solution.py:130
  103.4 12.3 %all_to_all.27 = f32[32,3,128]{2,1,0:T(4,128)S(1)} all-to-all(f32[32,3,128]{2,1,0:T(4,128)S(1)} %broadcast_in_dim.12), channel_id=1, replica_groups=mesh['row'=8,'zh'=4,'y'=4,'zl'=4] {'row','y'}, dimensions={0} | all-to-all | bytes 98304 | tf_op jit(solution)/shard_map/all_to_all | solution.py:130
  115.7 0.1 fusion.10
  115.8 0.6 maximum_maximum_fusion
  (7 shorter events, 0.1 us)
Async XLA Ops:
  0.0 29.8 %copy-start.3 = (s32[1,1,128]{2,1,0:T(1,128)S(1)}, s32[1,1,128]{2,1,0:T(1,128)}, u32[]{:S(2)}) copy-start(s32[1,1,128]{2,1,0:T(1,128)} %param.7) | copy-start | bytes 1540
  0.0 29.8 %copy-start.2 = (s32[1,1,128]{2,1,0:T(1,128)S(1)}, s32[1,1,128]{2,1,0:T(1,128)}, u32[]{:S(2)}) copy-start(s32[1,1,128]{2,1,0:T(1,128)} %param.8) | copy-start | bytes 1540
  2.7 16.6 %all-to-all-start = ((bf16[8,2,64,128]{3,2,1,0:T(8,128)(2,1)}), bf16[8,2,64,128]{3,2,1,0:T(8,128)(2,1)S(1)}, u32[]{:S(2)}, u32[]{:S(2)}) async-start(bf16[8,2,64,128]{3,2,1,0:T(8,128)(2,1)} %get-tuple-element.11), calls=%async_computation | async-start | bytes 524288 | tf_op jit(solution)/shard_map/all_to_all | solution.py:130
  13.5 1.2 %copy-start = (bf16[1,1,128,4096]{3,2,1,0:T(8,128)(2,1)S(1)}, bf16[1,1,128,4096]{3,2,1,0:T(8,128)(2,1)}, u32[]{:S(2)}) copy-start(bf16[1,1,128,4096]{3,2,1,0:T(8,128)(2,1)} %param.6) | copy-start | bytes 3145732
  19.4 26.3 %all-to-all-start.1 = ((bf16[4,128,128]{2,1,0:T(8,128)(2,1)}), bf16[4,128,128]{2,1,0:T(8,128)(2,1)S(1)}, u32[]{:S(2)}, u32[]{:S(2)}) async-start(bf16[4,128,128]{2,1,0:T(8,128)(2,1)} %get-tuple-element.16), calls=%async_computation.1 | async-start | bytes 262144 | tf_op jit(solution)/shard_map/all_to_all | solution.py:130
  34.9 25.1 %collective-permute-start = (bf16[16,128,128]{2,1,0:T(8,128)(2,1)}, bf16[16,128,128]{2,1,0:T(8,128)(2,1)S(1)}, u32[]{:S(2)}, u32[]{:S(2)}) collective-permute-start(bf16[16,128,128]{2,1,0:T(8,128)(2,1)} %bitcast.44), channel_id=1, source_target_pairs={{0,4},{4,8},{8,12},{12,0},{1,5},{5,9},{9,13},{13,1},{2,6},{6,10},{... | collective-permute-start | bytes 1572872 | tf_op jit(solution)/shard_map/ppermute | solution.py:135
  38.1 24.7 %collective-permute-start.1 = (bf16[16,128,128]{2,1,0:T(8,128)(2,1)}, bf16[16,128,128]{2,1,0:T(8,128)(2,1)S(1)}, u32[]{:S(2)}, u32[]{:S(2)}) collective-permute-start(bf16[16,128,128]{2,1,0:T(8,128)(2,1)} %bitcast.43), channel_id=1, source_target_pairs={{0,8},{4,12},{8,0},{12,4},{1,9},{5,13},{9,1},{13,5},{2,10},{6,14},... | collective-permute-start | bytes 1572872 | tf_op jit(solution)/shard_map/ppermute | solution.py:135
  42.6 22.3 %collective-permute-start.2 = (bf16[16,128,128]{2,1,0:T(8,128)(2,1)}, bf16[16,128,128]{2,1,0:T(8,128)(2,1)S(1)}, u32[]{:S(2)}, u32[]{:S(2)}) collective-permute-start(bf16[16,128,128]{2,1,0:T(8,128)(2,1)} %bitcast.42), channel_id=1, source_target_pairs={{0,12},{4,0},{8,4},{12,8},{1,13},{5,1},{9,5},{13,9},{2,14},{6,2},{... | collective-permute-start | bytes 1572872 | tf_op jit(solution)/shard_map/ppermute | solution.py:135
  45.6 8.3 %collective-permute-start.3 = (bf16[4,128,128]{2,1,0:T(8,128)(2,1)S(1)}, bf16[4,128,128]{2,1,0:T(8,128)(2,1)S(1)}, u32[]{:S(2)}, u32[]{:S(2)}) collective-permute-start(bf16[4,128,128]{2,1,0:T(8,128)(2,1)S(1)} %all-to-all-done.1.refs_4_), channel_id=1, source_target_pairs={{0,1},{1,2},{2,3},{3,16},{16,17},{17,18},{18,19},{19,32},{32,33},{... | collective-permute-start | bytes 393224 | tf_op jit(solution)/shard_map/ppermute | solution.py:135
  48.3 10.5 %collective-permute-start.4 = (bf16[4,128,128]{2,1,0:T(8,128)(2,1)S(1)}, bf16[4,128,128]{2,1,0:T(8,128)(2,1)S(1)}, u32[]{:S(2)}, u32[]{:S(2)}) collective-permute-start(bf16[4,128,128]{2,1,0:T(8,128)(2,1)S(1)} %all-to-all-done.1.refs_4_), channel_id=1, source_target_pairs={{0,2},{1,3},{2,16},{3,17},{16,18},{17,19},{18,32},{19,33},{32,34},... | collective-permute-start | bytes 393224 | tf_op jit(solution)/shard_map/ppermute | solution.py:135
  53.9 6.0 %collective-permute-start.5 = (bf16[4,128,128]{2,1,0:T(8,128)(2,1)S(1)}, bf16[4,128,128]{2,1,0:T(8,128)(2,1)S(1)}, u32[]{:S(2)}, u32[]{:S(2)}) collective-permute-start(bf16[4,128,128]{2,1,0:T(8,128)(2,1)S(1)} %all-to-all-done.1.refs_4_), channel_id=1, source_target_pairs={{0,51},{1,0},{2,1},{3,2},{16,3},{17,16},{18,17},{19,18},{32,19},{3... | collective-permute-start | bytes 393224 | tf_op jit(solution)/shard_map/ppermute | solution.py:135
  64.9 1.2 %copy-start.1 = (f32[32,64,128]{2,1,0:T(8,128)S(1)}, f32[32,64,128]{2,1,0:T(8,128)}, u32[]{:S(2)}) copy-start(f32[32,64,128]{2,1,0:T(8,128)} %get-tuple-element.12) | copy-start | bytes 3145732

commit v7 on v6

--- a/solution.py
+++ b/solution.py
@@ -104,13 +104,23 @@
         copy.wait()
 
 
-def contract_kernel(*refs):
-    p_refs, (*w_refs, out_ref) = refs[:4], refs[4:]
+def contract_kernel(own_hbm, *refs):
+    *in_refs, out_ref, own, sems = refs
+    w_refs, p_refs = in_refs[: sems.shape[0]], in_refs[sems.shape[0] :]
+    size = own.shape[0] // len(w_refs)
+    copies = []
+    for near in range(len(w_refs)):
+        there = pl.ds(near * size, size)
+        copies.append(pltpu.make_async_copy(own_hbm.at[there], own.at[there], sems.at[near]))
+        copies[-1].start()
     galerkin = jnp.zeros((LANES, LANES), jnp.float32)
     for near, w_ref in enumerate(w_refs):
-        for zh in range(w_ref.shape[0]):
-            piece = near * w_ref.shape[0] + zh
-            block = sum(p_ref[piece].astype(jnp.float32) for p_ref in p_refs)
+        copies[near].wait()
+        for zh in range(size):
+            piece = near * size + zh
+            block = own[piece]
+            for p_ref in p_refs:
+                block += p_ref[piece].astype(jnp.float32)
             high = block.astype(jnp.bfloat16)
             low = (block - high.astype(jnp.float32)).astype(jnp.bfloat16)
             galerkin += jnp.dot(w_ref[zh], high, preferred_element_type=jnp.float32)
@@ -207,7 +217,7 @@
         ),
         name="product",
     )(slot_table(a_rows, a_cols, a_count), in_vmem(unfolded), in_vmem(column_window))
-    gathered = [products[0].reshape(-1, LANES, LANES)]
+    own, gathered = products[0].reshape(-1, LANES, LANES), []
     for distance in range(1, n_y):
         gathered.append(moved(products[distance].reshape(-1, LANES, LANES), "y", distance))
     for distance in NEAR[1:]:
@@ -215,11 +225,18 @@
     galerkin = pl.pallas_call(
         contract_kernel,
         out_shape=jax.ShapeDtypeStruct((HALF, 3, LANES), jnp.float32),
-        in_specs=[VMEM] * (n_y + n_zl),
+        in_specs=[ANY] + [VMEM] * (n_y - 1 + n_zl),
         out_specs=VMEM,
+        scratch_shapes=[
+            pltpu.VMEM((n_zh * n_zl, LANES, LANES), jnp.float32),
+            pltpu.SemaphoreType.DMA((n_zl,)),
+        ],
         compiler_params=pltpu.CompilerParams(vmem_limit_bytes=8 << 20),
         name="contract",
-    )(*[in_vmem(x) for x in (*gathered, *pieces)])
+    )(
+        pltpu.with_memory_space_constraint(own, pltpu.HBM),
+        *[in_vmem(x) for x in (*pieces, *gathered)],
+    )
     total = summed_over_all(galerkin)
     corner = jnp.concatenate([total[:, 2, :TILE], total[:, 2, TILE:]], axis=0)
     upper = jnp.concatenate([total[:, 0], total[:, 1]], axis=0)

time: 117 us -> 117 us (level)
  Pallas kernels: 9.57 us -> 11 us
  local copies, waits for them, and re-layouts: 2.6 us -> 1.37 us
    pallas_call x1, Pallas kernels: 0.55 us -> 1.93 us  [coarse_blocks(): pl.pallas_call(contract_kernel, out_shape=jax.ShapeDtypeStruct((HALF, 3,...]
    unnamed x8 -> x6, local copies, waits for them, and re-layouts: 2.45 us -> 1.23 us
where the time goes in v7:
time: 117 us
  blocking collectives  48.9 us (42%)
  starting transfers between devices  40.7 us (35%)
  waiting for transfers between devices  12.7 us (11%)
  Pallas kernels  11 us (9%)
  local copies, waits for them, and re-layouts  1.37 us (1%)
  other arithmetic  1.25 us (1%)
    all_to_all x3, blocking collectives, exchanged(): return lax.all_to_all(x, axes, 0, 0, tiled=True)  48.9 us
    all_to_all x2, starting transfers between devices, exchanged(): return lax.all_to_all(x, axes, 0, 0, tiled=True)  20.6 us
    ppermute x6, starting transfers between devices, moved(): lax.ppermute(x, axes, [(i, (i + distance) % peers) for i in range(peers)])  20.1 us
    ppermute x6, waiting for transfers between devices, moved(): lax.ppermute(x, axes, [(i, (i + distance) % peers) for i in range(peers)])  9.87 us
    pallas_call x1, Pallas kernels, coarse_blocks(): pl.pallas_call(product_kernel, out_shape=[jax.ShapeDtypeStruct((places, T...  4.51 us
    all_to_all x2, waiting for transfers between devices, exchanged(): return lax.all_to_all(x, axes, 0, 0, tiled=True)  2.82 us
    pallas_call x1, Pallas kernels, coarse_blocks(): pl.pallas_call(window_kernel, out_shape=(jax.ShapeDtypeStruct((n_row, loc...  2.72 us
  transfers between devices with their start and end apart: 8, of which 6 were waited for; matrix products, arithmetic and copies ran while one was open for 0% of the time, Pallas kernels for 5%

profile of v7, /device:TPU:1, one launch (start us, length us, event | category | flops | bytes accessed | tf_op | source)
XLA Modules:
  0.0 116.6 jit_solution(14896833079657368059)
XLA Ops:
  0.0 0.0 copy-start.2
  0.0 0.0 copy-start.1
  0.0 2.7 %window.1 = (bf16[8,2,64,128]{3,2,1,0:T(8,128)(2,1)}, bf16[4,128,128]{2,1,0:T(8,128)(2,1)}) custom-call(s32[2,4]{1,0:T(2,128)} %bitcast.41, bf16[2,4,4096]{2,1,0:T(4,128)(2,1)} %bitcast.36), custom_call_target="tpu_custom_call" | custom-call | tf_op jit(solution)/shard_map/window/pallas_call | solution.py:172
  2.7 10.1 %all-to-all-start = ((bf16[8,2,64,128]{3,2,1,0:T(8,128)(2,1)}), bf16[8,2,64,128]{3,2,1,0:T(8,128)(2,1)S(1)}, u32[]{:S(2)}, u32[]{:S(2)}) async-start(bf16[8,2,64,128]{3,2,1,0:T(8,128)(2,1)} %get-tuple-element.11), calls=%async_computation | async-start | bytes 524288 | tf_op jit(solution)/shard_map/all_to_all | solution.py:140
  13.5 0.0 copy-start
  13.5 1.2 %copy-done = bf16[1,1,128,4096]{3,2,1,0:T(8,128)(2,1)S(1)} copy-done((bf16[1,1,128,4096]{3,2,1,0:T(8,128)(2,1)S(1)}, bf16[1,1,128,4096]{3,2,1,0:T(8,128)(2,1)}, u32[]{:S(2)}) %copy-start) | copy-done | bytes 1048600
  14.8 1.8 %unfold.1.tiles = bf16[128,64,128]{2,1,0:T(8,128)(2,1)S(1)} custom-call(bf16[128,4096]{1,0:T(8,128)(2,1)S(1)} %bitcast.33), custom_call_target="tpu_custom_call" | custom-call | tf_op jit(solution)/shard_map/unfold/pallas_call | solution.py:190
  16.6 2.8 %all-to-all-done = bf16[8,2,64,128]{3,2,1,0:T(8,128)(2,1)S(1)} async-done(((bf16[8,2,64,128]{3,2,1,0:T(8,128)(2,1)}), bf16[8,2,64,128]{3,2,1,0:T(8,128)(2,1)S(1)}, u32[]{:S(2)}, u32[]{:S(2)}) %all-to-all-start) | async-done | bytes 262176 | tf_op jit(solution)/shard_map/all_to_all | solution.py:140
  19.4 10.4 %all-to-all-start.1 = ((bf16[4,128,128]{2,1,0:T(8,128)(2,1)}), bf16[4,128,128]{2,1,0:T(8,128)(2,1)S(1)}, u32[]{:S(2)}, u32[]{:S(2)}) async-start(bf16[4,128,128]{2,1,0:T(8,128)(2,1)} %get-tuple-element.13), calls=%async_computation.1 | async-start | bytes 262144 | tf_op jit(solution)/shard_map/all_to_all | solution.py:140
  29.8 0.0 copy-done.2
  29.8 0.0 copy-done.1
  29.8 0.5 fusion.2.slots
  30.3 4.5 %product.1 = (f32[32,64,128]{2,1,0:T(8,128)}, bf16[32,64,128]{2,1,0:T(8,128)(2,1)}, bf16[32,64,128]{2,1,0:T(8,128)(2,1)}, bf16[32,64,128]{2,1,0:T(8,128)(2,1)}) custom-call(s32[128]{0:T(128)} %fusion.2.slots, bf16[128,64,128]{2,1,0:T(8,128)(2,1)S(1)} %unfold.1.tiles, bf16[16,64,128]{2,1,0:T(8,128)(2,1)S(1)} %bitcast.34), custom_call_target="tpu_custom_call" | custom-call | tf_op jit(solution)/shard_map/product/pallas_call | solution.py:200
  34.9 3.2 %collective-permute-start.3 = (bf16[16,128,128]{2,1,0:T(8,128)(2,1)}, bf16[16,128,128]{2,1,0:T(8,128)(2,1)S(1)}, u32[]{:S(2)}, u32[]{:S(2)}) collective-permute-start(bf16[16,128,128]{2,1,0:T(8,128)(2,1)} %bitcast.44), channel_id=1, source_target_pairs={{0,4},{4,8},{8,12},{12,0},{1,5},{5,9},{9,13},{13,1},{2,6},{6,10},{... | collective-permute-start | bytes 1572872 | tf_op jit(solution)/shard_map/ppermute | solution.py:145
  38.1 4.5 %collective-permute-start.4 = (bf16[16,128,128]{2,1,0:T(8,128)(2,1)}, bf16[16,128,128]{2,1,0:T(8,128)(2,1)S(1)}, u32[]{:S(2)}, u32[]{:S(2)}) collective-permute-start(bf16[16,128,128]{2,1,0:T(8,128)(2,1)} %bitcast.43), channel_id=1, source_target_pairs={{0,8},{4,12},{8,0},{12,4},{1,9},{5,13},{9,1},{13,5},{2,10},{6,14},... | collective-permute-start | bytes 1572872 | tf_op jit(solution)/shard_map/ppermute | solution.py:145
  42.6 3.0 %collective-permute-start.5 = (bf16[16,128,128]{2,1,0:T(8,128)(2,1)}, bf16[16,128,128]{2,1,0:T(8,128)(2,1)S(1)}, u32[]{:S(2)}, u32[]{:S(2)}) collective-permute-start(bf16[16,128,128]{2,1,0:T(8,128)(2,1)} %bitcast.42), channel_id=1, source_target_pairs={{0,12},{4,0},{8,4},{12,8},{1,13},{5,1},{9,5},{13,9},{2,14},{6,2},{... | collective-permute-start | bytes 1572872 | tf_op jit(solution)/shard_map/ppermute | solution.py:145
  45.6 0.0 all-to-all-done.1.refs_0_
  45.6 2.7 %collective-permute-start = (bf16[4,128,128]{2,1,0:T(8,128)(2,1)S(1)}, bf16[4,128,128]{2,1,0:T(8,128)(2,1)S(1)}, u32[]{:S(2)}, u32[]{:S(2)}) collective-permute-start(bf16[4,128,128]{2,1,0:T(8,128)(2,1)S(1)} %all-to-all-done.1.refs_0_), channel_id=1, source_target_pairs={{0,1},{1,2},{2,3},{3,16},{16,17},{17,18},{18,19},{19,32},{32,33},{... | collective-permute-start | bytes 393224 | tf_op jit(solution)/shard_map/ppermute | solution.py:145
  48.3 3.1 %collective-permute-start.1 = (bf16[4,128,128]{2,1,0:T(8,128)(2,1)S(1)}, bf16[4,128,128]{2,1,0:T(8,128)(2,1)S(1)}, u32[]{:S(2)}, u32[]{:S(2)}) collective-permute-start(bf16[4,128,128]{2,1,0:T(8,128)(2,1)S(1)} %all-to-all-done.1.refs_0_), channel_id=1, source_target_pairs={{0,2},{1,3},{2,16},{3,17},{16,18},{17,19},{18,32},{19,33},{32,34},... | collective-permute-start | bytes 393224 | tf_op jit(solution)/shard_map/ppermute | solution.py:145
  51.4 2.5 %collective-permute-done.refs_1_ = bf16[4,128,128]{2,1,0:T(8,128)(2,1)S(1)} collective-permute-done((bf16[4,128,128]{2,1,0:T(8,128)(2,1)S(1)}, bf16[4,128,128]{2,1,0:T(8,128)(2,1)S(1)}, u32[]{:S(2)}, u32[]{:S(2)}) %collective-permute-start) | collective-permute-done | bytes 131104 | tf_op jit(solution)/shard_map/ppermute | solution.py:145
  53.9 3.6 %collective-permute-start.2 = (bf16[4,128,128]{2,1,0:T(8,128)(2,1)S(1)}, bf16[4,128,128]{2,1,0:T(8,128)(2,1)S(1)}, u32[]{:S(2)}, u32[]{:S(2)}) collective-permute-start(bf16[4,128,128]{2,1,0:T(8,128)(2,1)S(1)} %all-to-all-done.1.refs_0_), channel_id=1, source_target_pairs={{0,51},{1,0},{2,1},{3,2},{16,3},{17,16},{18,17},{19,18},{32,19},{3... | collective-permute-start | bytes 393224 | tf_op jit(solution)/shard_map/ppermute | solution.py:145
  57.6 1.2 %collective-permute-done.1.refs_2_ = bf16[4,128,128]{2,1,0:T(8,128)(2,1)S(1)} collective-permute-done((bf16[4,128,128]{2,1,0:T(8,128)(2,1)S(1)}, bf16[4,128,128]{2,1,0:T(8,128)(2,1)S(1)}, u32[]{:S(2)}, u32[]{:S(2)}) %collective-permute-start.1) | collective-permute-done | bytes 131104 | tf_op jit(solution)/shard_map/ppermute | solution.py:145
  58.8 1.1 collective-permute-done.2.refs_3_
  59.9 0.0 collective-permute-done.3.refs_4_
  59.9 2.8 %collective-permute-done.4.refs_5_ = bf16[16,128,128]{2,1,0:T(8,128)(2,1)S(1)} collective-permute-done((bf16[16,128,128]{2,1,0:T(8,128)(2,1)}, bf16[16,128,128]{2,1,0:T(8,128)(2,1)S(1)}, u32[]{:S(2)}, u32[]{:S(2)}) %collective-permute-start.4) | collective-permute-done | bytes 524320 | tf_op jit(solution)/shard_map/ppermute | solution.py:145
  62.8 2.1 %collective-permute-done.5.refs_6_ = bf16[16,128,128]{2,1,0:T(8,128)(2,1)S(1)} collective-permute-done((bf16[16,128,128]{2,1,0:T(8,128)(2,1)}, bf16[16,128,128]{2,1,0:T(8,128)(2,1)S(1)}, u32[]{:S(2)}, u32[]{:S(2)}) %collective-permute-start.5) | collective-permute-done | bytes 524320 | tf_op jit(solution)/shard_map/ppermute | solution.py:145
  64.9 1.9 %contract.1 = f32[32,3,128]{2,1,0:T(4,128)S(1)} custom-call(f32[16,128,128]{2,1,0:T(8,128)} %bitcast.35, bf16[4,128,128]{2,1,0:T(8,128)(2,1)S(1)} %all-to-all-done.1.refs_0_, bf16[4,128,128]{2,1,0:T(8,128)(2,1)S(1)} %collective-permute-done.refs_1_, bf16[4,128,128]{2,1,0:T(8,128)(2,1)S(1)} %collective-permute-done.1.refs_2_, ...), custom_call_target="tpu_custom_call" | custom-call | tf_op jit(solution)/shard_map/contract/pallas_call | solution.py:225
  66.9 13.7 %all_to_all.25 = f32[32,3,128]{2,1,0:T(4,128)S(1)} all-to-all(f32[32,3,128]{2,1,0:T(4,128)S(1)} %contract.1), channel_id=1, replica_groups=mesh['row'=8,'zh'=4,'y'=4,'zl'=4] {'row','y'}, dimensions={0} | all-to-all | bytes 98304 | tf_op jit(solution)/shard_map/all_to_all | solution.py:140
  80.6 22.8 %all_to_all.26 = f32[16,3,128]{2,1,0:T(4,128)S(1)} all-to-all(f32[16,3,128]{2,1,0:T(4,128)S(1)} %broadcast_in_dim.11), channel_id=1, replica_groups=mesh['row'=8,'zh'=4,'y'=4,'zl'=4] {'zh','zl'}, dimensions={0} | all-to-all | bytes 49152 | tf_op jit(solution)/shard_map/all_to_all | solution.py:140
  103.5 12.3 %all_to_all.27 = f32[32,3,128]{2,1,0:T(4,128)S(1)} all-to-all(f32[32,3,128]{2,1,0:T(4,128)S(1)} %broadcast_in_dim.12), channel_id=1, replica_groups=mesh['row'=8,'zh'=4,'y'=4,'zl'=4] {'row','y'}, dimensions={0} | all-to-all | bytes 98304 | tf_op jit(solution)/shard_map/all_to_all | solution.py:140
  115.9 0.1 fusion.10
  116.0 0.6 maximum_maximum_fusion
  (5 shorter events, 0.1 us)
Async XLA Ops:
  0.0 29.8 %copy-start.2 = (s32[1,1,128]{2,1,0:T(1,128)S(1)}, s32[1,1,128]{2,1,0:T(1,128)}, u32[]{:S(2)}) copy-start(s32[1,1,128]{2,1,0:T(1,128)} %param.7) | copy-start | bytes 1540
  0.0 29.8 %copy-start.1 = (s32[1,1,128]{2,1,0:T(1,128)S(1)}, s32[1,1,128]{2,1,0:T(1,128)}, u32[]{:S(2)}) copy-start(s32[1,1,128]{2,1,0:T(1,128)} %param.8) | copy-start | bytes 1540
  2.7 16.6 %all-to-all-start = ((bf16[8,2,64,128]{3,2,1,0:T(8,128)(2,1)}), bf16[8,2,64,128]{3,2,1,0:T(8,128)(2,1)S(1)}, u32[]{:S(2)}, u32[]{:S(2)}) async-start(bf16[8,2,64,128]{3,2,1,0:T(8,128)(2,1)} %get-tuple-element.11), calls=%async_computation | async-start | bytes 524288 | tf_op jit(solution)/shard_map/all_to_all | solution.py:140
  13.5 1.2 %copy-start = (bf16[1,1,128,4096]{3,2,1,0:T(8,128)(2,1)S(1)}, bf16[1,1,128,4096]{3,2,1,0:T(8,128)(2,1)}, u32[]{:S(2)}) copy-start(bf16[1,1,128,4096]{3,2,1,0:T(8,128)(2,1)} %param.6) | copy-start | bytes 3145732
  19.4 26.2 %all-to-all-start.1 = ((bf16[4,128,128]{2,1,0:T(8,128)(2,1)}), bf16[4,128,128]{2,1,0:T(8,128)(2,1)S(1)}, u32[]{:S(2)}, u32[]{:S(2)}) async-start(bf16[4,128,128]{2,1,0:T(8,128)(2,1)} %get-tuple-element.13), calls=%async_computation.1 | async-start | bytes 262144 | tf_op jit(solution)/shard_map/all_to_all | solution.py:140
  34.9 25.1 %collective-permute-start.3 = (bf16[16,128,128]{2,1,0:T(8,128)(2,1)}, bf16[16,128,128]{2,1,0:T(8,128)(2,1)S(1)}, u32[]{:S(2)}, u32[]{:S(2)}) collective-permute-start(bf16[16,128,128]{2,1,0:T(8,128)(2,1)} %bitcast.44), channel_id=1, source_target_pairs={{0,4},{4,8},{8,12},{12,0},{1,5},{5,9},{9,13},{13,1},{2,6},{6,10},{... | collective-permute-start | bytes 1572872 | tf_op jit(solution)/shard_map/ppermute | solution.py:145
  38.1 24.7 %collective-permute-start.4 = (bf16[16,128,128]{2,1,0:T(8,128)(2,1)}, bf16[16,128,128]{2,1,0:T(8,128)(2,1)S(1)}, u32[]{:S(2)}, u32[]{:S(2)}) collective-permute-start(bf16[16,128,128]{2,1,0:T(8,128)(2,1)} %bitcast.43), channel_id=1, source_target_pairs={{0,8},{4,12},{8,0},{12,4},{1,9},{5,13},{9,1},{13,5},{2,10},{6,14},... | collective-permute-start | bytes 1572872 | tf_op jit(solution)/shard_map/ppermute | solution.py:145
  42.6 22.3 %collective-permute-start.5 = (bf16[16,128,128]{2,1,0:T(8,128)(2,1)}, bf16[16,128,128]{2,1,0:T(8,128)(2,1)S(1)}, u32[]{:S(2)}, u32[]{:S(2)}) collective-permute-start(bf16[16,128,128]{2,1,0:T(8,128)(2,1)} %bitcast.42), channel_id=1, source_target_pairs={{0,12},{4,0},{8,4},{12,8},{1,13},{5,1},{9,5},{13,9},{2,14},{6,2},{... | collective-permute-start | bytes 1572872 | tf_op jit(solution)/shard_map/ppermute | solution.py:145
  45.6 8.3 %collective-permute-start = (bf16[4,128,128]{2,1,0:T(8,128)(2,1)S(1)}, bf16[4,128,128]{2,1,0:T(8,128)(2,1)S(1)}, u32[]{:S(2)}, u32[]{:S(2)}) collective-permute-start(bf16[4,128,128]{2,1,0:T(8,128)(2,1)S(1)} %all-to-all-done.1.refs_0_), channel_id=1, source_target_pairs={{0,1},{1,2},{2,3},{3,16},{16,17},{17,18},{18,19},{19,32},{32,33},{... | collective-permute-start | bytes 393224 | tf_op jit(solution)/shard_map/ppermute | solution.py:145
  48.3 10.5 %collective-permute-start.1 = (bf16[4,128,128]{2,1,0:T(8,128)(2,1)S(1)}, bf16[4,128,128]{2,1,0:T(8,128)(2,1)S(1)}, u32[]{:S(2)}, u32[]{:S(2)}) collective-permute-start(bf16[4,128,128]{2,1,0:T(8,128)(2,1)S(1)} %all-to-all-done.1.refs_0_), channel_id=1, source_target_pairs={{0,2},{1,3},{2,16},{3,17},{16,18},{17,19},{18,32},{19,33},{32,34},... | collective-permute-start | bytes 393224 | tf_op jit(solution)/shard_map/ppermute | solution.py:145
  53.9 6.0 %collective-permute-start.2 = (bf16[4,128,128]{2,1,0:T(8,128)(2,1)S(1)}, bf16[4,128,128]{2,1,0:T(8,128)(2,1)S(1)}, u32[]{:S(2)}, u32[]{:S(2)}) collective-permute-start(bf16[4,128,128]{2,1,0:T(8,128)(2,1)S(1)} %all-to-all-done.1.refs_0_), channel_id=1, source_target_pairs={{0,51},{1,0},{2,1},{3,2},{16,3},{17,16},{18,17},{19,18},{32,19},{3... | collective-permute-start | bytes 393224 | tf_op jit(solution)/shard_map/ppermute | solution.py:145

commit v8 on v6

--- a/solution.py
+++ b/solution.py
@@ -65,7 +65,7 @@
 
 
 def product_kernel(slots, tiles, window, *refs):
-    *out_hbm, total, rounded, out_sems = refs
+    own_ref, *out_hbm, total, rounded, out_sems = refs
     total[...] = jnp.zeros_like(total)
 
     def chunk(turn, carry):
@@ -85,27 +85,29 @@
         return carry
 
     lax.fori_loop(0, tiles.shape[0] // CHUNK, chunk, 0)
-    size = out_hbm[0].shape[0]
-    out_copies = [pltpu.make_async_copy(total.at[pl.ds(0, size)], out_hbm[0], out_sems.at[0])]
-    out_copies[0].start()
-    for distance in range(1, len(out_hbm)):
+    size = own_ref.shape[0]
+    copies = []
+    for distance, out in enumerate(out_hbm, 1):
 
         def store(turn, carry, distance=distance):
             rounded[distance - 1, turn] = total[distance * size + turn].astype(jnp.bfloat16)
             return carry
 
         lax.fori_loop(0, size, store, 0, unroll=8)
-        copy = pltpu.make_async_copy(
-            rounded.at[distance - 1], out_hbm[distance], out_sems.at[distance]
-        )
-        copy.start()
-        out_copies.append(copy)
-    for copy in out_copies:
+        copies.append(pltpu.make_async_copy(rounded.at[distance - 1], out, out_sems.at[distance - 1]))
+        copies[-1].start()
+
+    def keep(turn, carry):
+        own_ref[turn] = total[turn]
+        return carry
+
+    lax.fori_loop(0, size, keep, 0, unroll=8)
+    for copy in copies:
         copy.wait()
 
 
 def contract_kernel(*refs):
-    p_refs, (*w_refs, out_ref) = refs[:4], refs[4:]
+    w_refs, (*p_refs, out_ref) = refs[: len(NEAR)], refs[len(NEAR) :]
     galerkin = jnp.zeros((LANES, LANES), jnp.float32)
     for near, w_ref in enumerate(w_refs):
         for zh in range(w_ref.shape[0]):
@@ -189,25 +191,22 @@
     pieces = [exchanged(own_turned, "zh")]
     products = pl.pallas_call(
         product_kernel,
-        out_shape=[
-            jax.ShapeDtypeStruct(
-                (places, TILE, LANES), jnp.bfloat16 if distance else jnp.float32
-            )
-            for distance in range(n_y)
-        ],
+        out_shape=[jax.ShapeDtypeStruct((places, TILE, LANES), jnp.float32)]
+        + [pltpu.HBM((places, TILE, LANES), jnp.bfloat16)] * (n_y - 1),
         grid_spec=pltpu.PrefetchScalarGridSpec(
             num_scalar_prefetch=1,
             in_specs=[VMEM, VMEM],
-            out_specs=[ANY] * n_y,
+            out_specs=[VMEM] + [ANY] * (n_y - 1),
             scratch_shapes=[
                 pltpu.VMEM((n_y * places + 1, TILE, LANES), jnp.float32),
                 pltpu.VMEM((n_y - 1, places, TILE, LANES), jnp.bfloat16),
-                pltpu.SemaphoreType.DMA((n_y,)),
+                pltpu.SemaphoreType.DMA((n_y - 1,)),
             ],
         ),
+        compiler_params=pltpu.CompilerParams(vmem_limit_bytes=16 << 20),
         name="product",
     )(slot_table(a_rows, a_cols, a_count), in_vmem(unfolded), in_vmem(column_window))
-    gathered = [products[0].reshape(-1, LANES, LANES)]
+    own, gathered = products[0].reshape(-1, LANES, LANES), []
     for distance in range(1, n_y):
         gathered.append(moved(products[distance].reshape(-1, LANES, LANES), "y", distance))
     for distance in NEAR[1:]:
@@ -219,7 +218,9 @@
         out_specs=VMEM,
         compiler_params=pltpu.CompilerParams(vmem_limit_bytes=8 << 20),
         name="contract",
-    )(*[in_vmem(x) for x in (*gathered, *pieces)])
+    )(
+        *[in_vmem(x) for x in (*pieces, own, *gathered)],
+    )
     total = summed_over_all(galerkin)
     corner = jnp.concatenate([total[:, 2, :TILE], total[:, 2, TILE:]], axis=0)
     upper = jnp.concatenate([total[:, 0], total[:, 1]], axis=0)

time: 117 us -> 115 us (0.983)
  local copies, waits for them, and re-layouts: 2.6 us -> 1.37 us
    unnamed x8 -> x6, local copies, waits for them, and re-layouts: 2.45 us -> 1.23 us
where the time goes in v8:
time: 115 us; the launch traced here: 114 us
  blocking collectives  48.9 us (43%)
  starting transfers between devices  40.7 us (35%)
  waiting for transfers between devices  12.7 us (11%)
  Pallas kernels  9.12 us (8%)
  local copies, waits for them, and re-layouts  1.37 us (1%)
    all_to_all x3, blocking collectives, exchanged(): return lax.all_to_all(x, axes, 0, 0, tiled=True)  48.9 us
    all_to_all x2, starting transfers between devices, exchanged(): return lax.all_to_all(x, axes, 0, 0, tiled=True)  20.6 us
    ppermute x6, starting transfers between devices, moved(): lax.ppermute(x, axes, [(i, (i + distance) % peers) for i in range(peers)])  20.1 us
    ppermute x6, waiting for transfers between devices, moved(): lax.ppermute(x, axes, [(i, (i + distance) % peers) for i in range(peers)])  9.86 us
    pallas_call x1, Pallas kernels, coarse_blocks(): pl.pallas_call(product_kernel, out_shape=[jax.ShapeDtypeStruct((places, T...  4.08 us
    all_to_all x2, waiting for transfers between devices, exchanged(): return lax.all_to_all(x, axes, 0, 0, tiled=True)  2.82 us
    pallas_call x1, Pallas kernels, coarse_blocks(): pl.pallas_call(window_kernel, out_shape=(jax.ShapeDtypeStruct((n_row, loc...  2.7 us
  transfers between devices with their start and end apart: 8, of which 6 were waited for; matrix products, arithmetic and copies ran while one was open for 0% of the time, Pallas kernels for 5%

profile of v8, /device:TPU:1, one launch (start us, length us, event | category | flops | bytes accessed | tf_op | source)
XLA Modules:
  0.0 114.3 jit_solution(14676828308369829812)
XLA Ops:
  0.0 0.0 copy-start.2
  0.0 0.0 copy-start.1
  0.0 2.7 %window.1 = (bf16[8,2,64,128]{3,2,1,0:T(8,128)(2,1)}, bf16[4,128,128]{2,1,0:T(8,128)(2,1)}) custom-call(s32[2,4]{1,0:T(2,128)} %bitcast.41, bf16[2,4,4096]{2,1,0:T(4,128)(2,1)} %bitcast.36), custom_call_target="tpu_custom_call" | custom-call | tf_op jit(solution)/shard_map/window/pallas_call | solution.py:164
  2.7 10.1 %all-to-all-start.1 = ((bf16[8,2,64,128]{3,2,1,0:T(8,128)(2,1)}), bf16[8,2,64,128]{3,2,1,0:T(8,128)(2,1)S(1)}, u32[]{:S(2)}, u32[]{:S(2)}) async-start(bf16[8,2,64,128]{3,2,1,0:T(8,128)(2,1)} %get-tuple-element.12), calls=%async_computation.1 | async-start | bytes 524288 | tf_op jit(solution)/shard_map/all_to_all | solution.py:132
  13.5 0.0 copy-start
  13.5 1.2 %copy-done = bf16[1,1,128,4096]{3,2,1,0:T(8,128)(2,1)S(1)} copy-done((bf16[1,1,128,4096]{3,2,1,0:T(8,128)(2,1)S(1)}, bf16[1,1,128,4096]{3,2,1,0:T(8,128)(2,1)}, u32[]{:S(2)}) %copy-start) | copy-done | bytes 1048600
  14.7 1.8 %unfold.1.tiles = bf16[128,64,128]{2,1,0:T(8,128)(2,1)S(1)} custom-call(bf16[128,4096]{1,0:T(8,128)(2,1)S(1)} %bitcast.33), custom_call_target="tpu_custom_call" | custom-call | tf_op jit(solution)/shard_map/unfold/pallas_call | solution.py:182
  16.5 2.8 %all-to-all-done.1 = bf16[8,2,64,128]{3,2,1,0:T(8,128)(2,1)S(1)} async-done(((bf16[8,2,64,128]{3,2,1,0:T(8,128)(2,1)}), bf16[8,2,64,128]{3,2,1,0:T(8,128)(2,1)S(1)}, u32[]{:S(2)}, u32[]{:S(2)}) %all-to-all-start.1) | async-done | bytes 262176 | tf_op jit(solution)/shard_map/all_to_all | solution.py:132
  19.4 10.4 %all-to-all-start = ((bf16[4,128,128]{2,1,0:T(8,128)(2,1)}), bf16[4,128,128]{2,1,0:T(8,128)(2,1)S(1)}, u32[]{:S(2)}, u32[]{:S(2)}) async-start(bf16[4,128,128]{2,1,0:T(8,128)(2,1)} %get-tuple-element.11), calls=%async_computation | async-start | bytes 262144 | tf_op jit(solution)/shard_map/all_to_all | solution.py:132
  29.8 0.0 copy-done.2
  29.8 0.0 copy-done.1
  29.8 4.1 %product.1 = (f32[32,64,128]{2,1,0:T(8,128)S(1)}, bf16[32,64,128]{2,1,0:T(8,128)(2,1)}, bf16[32,64,128]{2,1,0:T(8,128)(2,1)}, bf16[32,64,128]{2,1,0:T(8,128)(2,1)}) custom-call(s32[128]{0:T(128)S(1)} %fusion.2.slots, bf16[128,64,128]{2,1,0:T(8,128)(2,1)S(1)} %unfold.1.tiles, bf16[16,64,128]{2,1,0:T(8,128)(2,1)S(1)} %bitcast.35), custom_call_target="tpu_custom_call" | custom-call | tf_op jit(solution)/shard_map/product/pallas_call | solution.py:192
  33.9 3.2 %collective-permute-start.3 = (bf16[16,128,128]{2,1,0:T(8,128)(2,1)}, bf16[16,128,128]{2,1,0:T(8,128)(2,1)S(1)}, u32[]{:S(2)}, u32[]{:S(2)}) collective-permute-start(bf16[16,128,128]{2,1,0:T(8,128)(2,1)} %bitcast.44), channel_id=1, source_target_pairs={{0,4},{4,8},{8,12},{12,0},{1,5},{5,9},{9,13},{13,1},{2,6},{6,10},{... | collective-permute-start | bytes 1572872 | tf_op jit(solution)/shard_map/ppermute | solution.py:137
  37.1 4.5 %collective-permute-start.4 = (bf16[16,128,128]{2,1,0:T(8,128)(2,1)}, bf16[16,128,128]{2,1,0:T(8,128)(2,1)S(1)}, u32[]{:S(2)}, u32[]{:S(2)}) collective-permute-start(bf16[16,128,128]{2,1,0:T(8,128)(2,1)} %bitcast.43), channel_id=1, source_target_pairs={{0,8},{4,12},{8,0},{12,4},{1,9},{5,13},{9,1},{13,5},{2,10},{6,14},... | collective-permute-start | bytes 1572872 | tf_op jit(solution)/shard_map/ppermute | solution.py:137
  41.6 3.0 %collective-permute-start.5 = (bf16[16,128,128]{2,1,0:T(8,128)(2,1)}, bf16[16,128,128]{2,1,0:T(8,128)(2,1)S(1)}, u32[]{:S(2)}, u32[]{:S(2)}) collective-permute-start(bf16[16,128,128]{2,1,0:T(8,128)(2,1)} %bitcast.42), channel_id=1, source_target_pairs={{0,12},{4,0},{8,4},{12,8},{1,13},{5,1},{9,5},{13,9},{2,14},{6,2},{... | collective-permute-start | bytes 1572872 | tf_op jit(solution)/shard_map/ppermute | solution.py:137
  44.6 0.0 all-to-all-done.refs_0_
  44.6 2.7 %collective-permute-start = (bf16[4,128,128]{2,1,0:T(8,128)(2,1)S(1)}, bf16[4,128,128]{2,1,0:T(8,128)(2,1)S(1)}, u32[]{:S(2)}, u32[]{:S(2)}) collective-permute-start(bf16[4,128,128]{2,1,0:T(8,128)(2,1)S(1)} %all-to-all-done.refs_0_), channel_id=1, source_target_pairs={{0,1},{1,2},{2,3},{3,16},{16,17},{17,18},{18,19},{19,32},{32,33},{... | collective-permute-start | bytes 393224 | tf_op jit(solution)/shard_map/ppermute | solution.py:137
  47.4 3.1 %collective-permute-start.1 = (bf16[4,128,128]{2,1,0:T(8,128)(2,1)S(1)}, bf16[4,128,128]{2,1,0:T(8,128)(2,1)S(1)}, u32[]{:S(2)}, u32[]{:S(2)}) collective-permute-start(bf16[4,128,128]{2,1,0:T(8,128)(2,1)S(1)} %all-to-all-done.refs_0_), channel_id=1, source_target_pairs={{0,2},{1,3},{2,16},{3,17},{16,18},{17,19},{18,32},{19,33},{32,34},... | collective-permute-start | bytes 393224 | tf_op jit(solution)/shard_map/ppermute | solution.py:137
  50.4 2.5 %collective-permute-done.refs_1_ = bf16[4,128,128]{2,1,0:T(8,128)(2,1)S(1)} collective-permute-done((bf16[4,128,128]{2,1,0:T(8,128)(2,1)S(1)}, bf16[4,128,128]{2,1,0:T(8,128)(2,1)S(1)}, u32[]{:S(2)}, u32[]{:S(2)}) %collective-permute-start) | collective-permute-done | bytes 131104 | tf_op jit(solution)/shard_map/ppermute | solution.py:137
  52.9 3.6 %collective-permute-start.2 = (bf16[4,128,128]{2,1,0:T(8,128)(2,1)S(1)}, bf16[4,128,128]{2,1,0:T(8,128)(2,1)S(1)}, u32[]{:S(2)}, u32[]{:S(2)}) collective-permute-start(bf16[4,128,128]{2,1,0:T(8,128)(2,1)S(1)} %all-to-all-done.refs_0_), channel_id=1, source_target_pairs={{0,51},{1,0},{2,1},{3,2},{16,3},{17,16},{18,17},{19,18},{32,19},{3... | collective-permute-start | bytes 393224 | tf_op jit(solution)/shard_map/ppermute | solution.py:137
  56.6 1.2 %collective-permute-done.1.refs_2_ = bf16[4,128,128]{2,1,0:T(8,128)(2,1)S(1)} collective-permute-done((bf16[4,128,128]{2,1,0:T(8,128)(2,1)S(1)}, bf16[4,128,128]{2,1,0:T(8,128)(2,1)S(1)}, u32[]{:S(2)}, u32[]{:S(2)}) %collective-permute-start.1) | collective-permute-done | bytes 131104 | tf_op jit(solution)/shard_map/ppermute | solution.py:137
  57.8 1.2 %collective-permute-done.2.refs_3_ = bf16[4,128,128]{2,1,0:T(8,128)(2,1)S(1)} collective-permute-done((bf16[4,128,128]{2,1,0:T(8,128)(2,1)S(1)}, bf16[4,128,128]{2,1,0:T(8,128)(2,1)S(1)}, u32[]{:S(2)}, u32[]{:S(2)}) %collective-permute-start.2) | collective-permute-done | bytes 131104 | tf_op jit(solution)/shard_map/ppermute | solution.py:137
  59.0 0.0 collective-permute-done.3.refs_5_
  59.0 2.8 %collective-permute-done.4.refs_6_ = bf16[16,128,128]{2,1,0:T(8,128)(2,1)S(1)} collective-permute-done((bf16[16,128,128]{2,1,0:T(8,128)(2,1)}, bf16[16,128,128]{2,1,0:T(8,128)(2,1)S(1)}, u32[]{:S(2)}, u32[]{:S(2)}) %collective-permute-start.4) | collective-permute-done | bytes 524320 | tf_op jit(solution)/shard_map/ppermute | solution.py:137
  61.8 2.1 %collective-permute-done.5.refs_7_ = bf16[16,128,128]{2,1,0:T(8,128)(2,1)S(1)} collective-permute-done((bf16[16,128,128]{2,1,0:T(8,128)(2,1)}, bf16[16,128,128]{2,1,0:T(8,128)(2,1)S(1)}, u32[]{:S(2)}, u32[]{:S(2)}) %collective-permute-start.5) | collective-permute-done | bytes 524320 | tf_op jit(solution)/shard_map/ppermute | solution.py:137
  63.9 0.6 contract.1
  64.5 13.7 %all_to_all.25 = f32[32,3,128]{2,1,0:T(4,128)S(1)} all-to-all(f32[32,3,128]{2,1,0:T(4,128)S(1)} %contract.1), channel_id=1, replica_groups=mesh['row'=8,'zh'=4,'y'=4,'zl'=4] {'row','y'}, dimensions={0} | all-to-all | bytes 98304 | tf_op jit(solution)/shard_map/all_to_all | solution.py:132
  78.3 22.9 %all_to_all.26 = f32[16,3,128]{2,1,0:T(4,128)S(1)} all-to-all(f32[16,3,128]{2,1,0:T(4,128)S(1)} %broadcast_in_dim.11), channel_id=1, replica_groups=mesh['row'=8,'zh'=4,'y'=4,'zl'=4] {'zh','zl'}, dimensions={0} | all-to-all | bytes 49152 | tf_op jit(solution)/shard_map/all_to_all | solution.py:132
  101.1 12.3 %all_to_all.27 = f32[32,3,128]{2,1,0:T(4,128)S(1)} all-to-all(f32[32,3,128]{2,1,0:T(4,128)S(1)} %broadcast_in_dim.12), channel_id=1, replica_groups=mesh['row'=8,'zh'=4,'y'=4,'zl'=4] {'row','y'}, dimensions={0} | all-to-all | bytes 98304 | tf_op jit(solution)/shard_map/all_to_all | solution.py:132
  113.5 0.1 fusion.10
  113.6 0.6 maximum_maximum_fusion
  (6 shorter events, 0.2 us)
Async XLA Ops:
  0.0 29.8 %copy-start.2 = (s32[1,1,128]{2,1,0:T(1,128)S(1)}, s32[1,1,128]{2,1,0:T(1,128)}, u32[]{:S(2)}) copy-start(s32[1,1,128]{2,1,0:T(1,128)} %param.7) | copy-start | bytes 1540
  0.0 29.8 %copy-start.1 = (s32[1,1,128]{2,1,0:T(1,128)S(1)}, s32[1,1,128]{2,1,0:T(1,128)}, u32[]{:S(2)}) copy-start(s32[1,1,128]{2,1,0:T(1,128)} %param.8) | copy-start | bytes 1540
  2.7 16.6 %all-to-all-start.1 = ((bf16[8,2,64,128]{3,2,1,0:T(8,128)(2,1)}), bf16[8,2,64,128]{3,2,1,0:T(8,128)(2,1)S(1)}, u32[]{:S(2)}, u32[]{:S(2)}) async-start(bf16[8,2,64,128]{3,2,1,0:T(8,128)(2,1)} %get-tuple-element.12), calls=%async_computation.1 | async-start | bytes 524288 | tf_op jit(solution)/shard_map/all_to_all | solution.py:132
  13.5 1.2 %copy-start = (bf16[1,1,128,4096]{3,2,1,0:T(8,128)(2,1)S(1)}, bf16[1,1,128,4096]{3,2,1,0:T(8,128)(2,1)}, u32[]{:S(2)}) copy-start(bf16[1,1,128,4096]{3,2,1,0:T(8,128)(2,1)} %param.6) | copy-start | bytes 3145732
  19.4 25.3 %all-to-all-start = ((bf16[4,128,128]{2,1,0:T(8,128)(2,1)}), bf16[4,128,128]{2,1,0:T(8,128)(2,1)S(1)}, u32[]{:S(2)}, u32[]{:S(2)}) async-start(bf16[4,128,128]{2,1,0:T(8,128)(2,1)} %get-tuple-element.11), calls=%async_computation | async-start | bytes 262144 | tf_op jit(solution)/shard_map/all_to_all | solution.py:132
  33.9 25.1 %collective-permute-start.3 = (bf16[16,128,128]{2,1,0:T(8,128)(2,1)}, bf16[16,128,128]{2,1,0:T(8,128)(2,1)S(1)}, u32[]{:S(2)}, u32[]{:S(2)}) collective-permute-start(bf16[16,128,128]{2,1,0:T(8,128)(2,1)} %bitcast.44), channel_id=1, source_target_pairs={{0,4},{4,8},{8,12},{12,0},{1,5},{5,9},{9,13},{13,1},{2,6},{6,10},{... | collective-permute-start | bytes 1572872 | tf_op jit(solution)/shard_map/ppermute | solution.py:137
  37.1 24.7 %collective-permute-start.4 = (bf16[16,128,128]{2,1,0:T(8,128)(2,1)}, bf16[16,128,128]{2,1,0:T(8,128)(2,1)S(1)}, u32[]{:S(2)}, u32[]{:S(2)}) collective-permute-start(bf16[16,128,128]{2,1,0:T(8,128)(2,1)} %bitcast.43), channel_id=1, source_target_pairs={{0,8},{4,12},{8,0},{12,4},{1,9},{5,13},{9,1},{13,5},{2,10},{6,14},... | collective-permute-start | bytes 1572872 | tf_op jit(solution)/shard_map/ppermute | solution.py:137
  41.6 22.3 %collective-permute-start.5 = (bf16[16,128,128]{2,1,0:T(8,128)(2,1)}, bf16[16,128,128]{2,1,0:T(8,128)(2,1)S(1)}, u32[]{:S(2)}, u32[]{:S(2)}) collective-permute-start(bf16[16,128,128]{2,1,0:T(8,128)(2,1)} %bitcast.42), channel_id=1, source_target_pairs={{0,12},{4,0},{8,4},{12,8},{1,13},{5,1},{9,5},{13,9},{2,14},{6,2},{... | collective-permute-start | bytes 1572872 | tf_op jit(solution)/shard_map/ppermute | solution.py:137
  44.6 8.3 %collective-permute-start = (bf16[4,128,128]{2,1,0:T(8,128)(2,1)S(1)}, bf16[4,128,128]{2,1,0:T(8,128)(2,1)S(1)}, u32[]{:S(2)}, u32[]{:S(2)}) collective-permute-start(bf16[4,128,128]{2,1,0:T(8,128)(2,1)S(1)} %all-to-all-done.refs_0_), channel_id=1, source_target_pairs={{0,1},{1,2},{2,3},{3,16},{16,17},{17,18},{18,19},{19,32},{32,33},{... | collective-permute-start | bytes 393224 | tf_op jit(solution)/shard_map/ppermute | solution.py:137
  47.4 10.5 %collective-permute-start.1 = (bf16[4,128,128]{2,1,0:T(8,128)(2,1)S(1)}, bf16[4,128,128]{2,1,0:T(8,128)(2,1)S(1)}, u32[]{:S(2)}, u32[]{:S(2)}) collective-permute-start(bf16[4,128,128]{2,1,0:T(8,128)(2,1)S(1)} %all-to-all-done.refs_0_), channel_id=1, source_target_pairs={{0,2},{1,3},{2,16},{3,17},{16,18},{17,19},{18,32},{19,33},{32,34},... | collective-permute-start | bytes 393224 | tf_op jit(solution)/shard_map/ppermute | solution.py:137
  52.9 6.0 %collective-permute-start.2 = (bf16[4,128,128]{2,1,0:T(8,128)(2,1)S(1)}, bf16[4,128,128]{2,1,0:T(8,128)(2,1)S(1)}, u32[]{:S(2)}, u32[]{:S(2)}) collective-permute-start(bf16[4,128,128]{2,1,0:T(8,128)(2,1)S(1)} %all-to-all-done.refs_0_), channel_id=1, source_target_pairs={{0,51},{1,0},{2,1},{3,2},{16,3},{17,16},{18,17},{19,18},{32,19},{3... | collective-permute-start | bytes 393224 | tf_op jit(solution)/shard_map/ppermute | solution.py:137

commit v9 on v8

--- a/solution.py
+++ b/solution.py
@@ -23,17 +23,14 @@
     return pltpu.roll(x, TILE, axis=1)
 
 
-def window_kernel(cols, p_ref, rows_ref, turned_ref, split, natural):
-    local_rows, slots = cols.shape
+def window_kernel(cols_ref, p_ref, rows_ref, turned_ref, split, natural):
+    local_rows, slots = cols_ref.shape
     lane = lax.broadcasted_iota(jnp.int32, (HALF, LANES), 1)
     panel = lax.broadcasted_iota(jnp.int32, (8, slots), 0)
-    slot = lax.broadcasted_iota(jnp.int32, (8, slots), 1)
     stacked = []
     for t in range(local_rows):
-        chosen = jnp.zeros((8, slots), jnp.float32)
-        for s in range(slots):
-            chosen = jnp.where((slot == s) & (panel == cols[t, s]), 1.0, chosen)
-        sums = jnp.dot(chosen.astype(jnp.bfloat16), p_ref[t], preferred_element_type=jnp.float32)
+        chosen = jnp.where(cols_ref[t : t + 1, :] == panel, 1.0, 0.0).astype(jnp.bfloat16)
+        sums = jnp.dot(chosen, p_ref[t], preferred_element_type=jnp.float32)
         for k in range(HALF):
             split[t, k] = sums[:, k * LANES : (k + 1) * LANES]
         first, second = split[t, :, 0, :], split[t, :, 1, :]
@@ -64,9 +61,12 @@
     lax.fori_loop(0, tiles.shape[0] // CHUNK, chunk, 0)
 
 
-def product_kernel(slots, tiles, window, *refs):
-    own_ref, *out_hbm, total, rounded, out_sems = refs
+def product_kernel(slots_hbm, tiles, window, *refs):
+    own_ref, *out_hbm, slots, total, rounded, slots_sem, out_sems = refs
+    slots_copy = pltpu.make_async_copy(slots_hbm, slots, slots_sem)
+    slots_copy.start()
     total[...] = jnp.zeros_like(total)
+    slots_copy.wait()
 
     def chunk(turn, carry):
         first = turn * CHUNK
@@ -167,15 +167,12 @@
             jax.ShapeDtypeStruct((n_row, local_rows, TILE, LANES), jnp.bfloat16),
             jax.ShapeDtypeStruct((n_zh, LANES, LANES), jnp.bfloat16),
         ),
-        grid_spec=pltpu.PrefetchScalarGridSpec(
-            num_scalar_prefetch=1,
-            in_specs=[VMEM],
-            out_specs=[VMEM, VMEM],
-            scratch_shapes=[
-                pltpu.VMEM((local_rows, HALF, 8, LANES), jnp.float32),
-                pltpu.VMEM((local_rows, TILE, LANES), jnp.float32),
-            ],
-        ),
+        in_specs=[VMEM, VMEM],
+        out_specs=[VMEM, VMEM],
+        scratch_shapes=[
+            pltpu.VMEM((local_rows, HALF, 8, LANES), jnp.float32),
+            pltpu.VMEM((local_rows, TILE, LANES), jnp.float32),
+        ],
         name="window",
     )(p_cols.reshape(local_rows, slots), p_tiles.reshape(local_rows, slots, area))
     column_window = exchanged(own_rows, "row").reshape(n_row * local_rows, TILE, LANES)
@@ -193,16 +190,15 @@
         product_kernel,
         out_shape=[jax.ShapeDtypeStruct((places, TILE, LANES), jnp.float32)]
         + [pltpu.HBM((places, TILE, LANES), jnp.bfloat16)] * (n_y - 1),
-        grid_spec=pltpu.PrefetchScalarGridSpec(
-            num_scalar_prefetch=1,
-            in_specs=[VMEM, VMEM],
-            out_specs=[VMEM] + [ANY] * (n_y - 1),
-            scratch_shapes=[
-                pltpu.VMEM((n_y * places + 1, TILE, LANES), jnp.float32),
-                pltpu.VMEM((n_y - 1, places, TILE, LANES), jnp.bfloat16),
-                pltpu.SemaphoreType.DMA((n_y - 1,)),
-            ],
-        ),
+        in_specs=[ANY, VMEM, VMEM],
+        out_specs=[VMEM] + [ANY] * (n_y - 1),
+        scratch_shapes=[
+            pltpu.SMEM((total_slots,), jnp.int32),
+            pltpu.VMEM((n_y * places + 1, TILE, LANES), jnp.float32),
+            pltpu.VMEM((n_y - 1, places, TILE, LANES), jnp.bfloat16),
+            pltpu.SemaphoreType.DMA,
+            pltpu.SemaphoreType.DMA((n_y - 1,)),
+        ],
         compiler_params=pltpu.CompilerParams(vmem_limit_bytes=16 << 20),
         name="product",
     )(slot_table(a_rows, a_cols, a_count), in_vmem(unfolded), in_vmem(column_window))

time: 115 us -> 114 us (level)
  no operation moved by 1% of the time
where the time goes in v9:
time: 114 us; the launch traced here: 113 us
  blocking collectives  48.9 us (43%)
  starting transfers between devices  40.7 us (36%)
  waiting for transfers between devices  12.7 us (11%)
  Pallas kernels  8.1 us (7%)
  local copies, waits for them, and re-layouts  1.37 us (1%)
    all_to_all x3, blocking collectives, exchanged(): return lax.all_to_all(x, axes, 0, 0, tiled=True)  48.9 us
    all_to_all x2, starting transfers between devices, exchanged(): return lax.all_to_all(x, axes, 0, 0, tiled=True)  20.6 us
    ppermute x6, starting transfers between devices, moved(): lax.ppermute(x, axes, [(i, (i + distance) % peers) for i in range(peers)])  20.1 us
    ppermute x6, waiting for transfers between devices, moved(): lax.ppermute(x, axes, [(i, (i + distance) % peers) for i in range(peers)])  9.86 us
    pallas_call x1, Pallas kernels, coarse_blocks(): pl.pallas_call(product_kernel, out_shape=[jax.ShapeDtypeStruct((places, T...  3.83 us
    all_to_all x2, waiting for transfers between devices, exchanged(): return lax.all_to_all(x, axes, 0, 0, tiled=True)  2.82 us
  transfers between devices with their start and end apart: 8, of which 6 were waited for; matrix products, arithmetic and copies ran while one was open for 0% of the time, Pallas kernels for 5%

profile of v9, /device:TPU:1, one launch (start us, length us, event | category | flops | bytes accessed | tf_op | source)
XLA Modules:
  0.0 113.2 jit_solution(1679432606512118147)
XLA Ops:
  0.0 0.0 copy-start.2
  0.0 0.0 copy-start.1
  0.0 1.9 %window.1 = (bf16[8,2,64,128]{3,2,1,0:T(8,128)(2,1)}, bf16[4,128,128]{2,1,0:T(8,128)(2,1)}) custom-call(s32[2,4]{1,0:T(2,128)} %bitcast.41, bf16[2,4,4096]{2,1,0:T(4,128)(2,1)} %bitcast.36), custom_call_target="tpu_custom_call" | custom-call | tf_op jit(solution)/shard_map/window/pallas_call | solution.py:164
  1.9 10.1 %all-to-all-start.1 = ((bf16[8,2,64,128]{3,2,1,0:T(8,128)(2,1)}), bf16[8,2,64,128]{3,2,1,0:T(8,128)(2,1)S(1)}, u32[]{:S(2)}, u32[]{:S(2)}) async-start(bf16[8,2,64,128]{3,2,1,0:T(8,128)(2,1)} %get-tuple-element.12), calls=%async_computation.1 | async-start | bytes 524288 | tf_op jit(solution)/shard_map/all_to_all | solution.py:132
  12.7 0.0 copy-start
  12.7 1.2 %copy-done = bf16[1,1,128,4096]{3,2,1,0:T(8,128)(2,1)S(1)} copy-done((bf16[1,1,128,4096]{3,2,1,0:T(8,128)(2,1)S(1)}, bf16[1,1,128,4096]{3,2,1,0:T(8,128)(2,1)}, u32[]{:S(2)}) %copy-start) | copy-done | bytes 1048600
  14.0 1.8 %unfold.1.tiles = bf16[128,64,128]{2,1,0:T(8,128)(2,1)S(1)} custom-call(bf16[128,4096]{1,0:T(8,128)(2,1)S(1)} %bitcast.33), custom_call_target="tpu_custom_call" | custom-call | tf_op jit(solution)/shard_map/unfold/pallas_call | solution.py:179
  15.8 2.8 %all-to-all-done.1 = bf16[8,2,64,128]{3,2,1,0:T(8,128)(2,1)S(1)} async-done(((bf16[8,2,64,128]{3,2,1,0:T(8,128)(2,1)}), bf16[8,2,64,128]{3,2,1,0:T(8,128)(2,1)S(1)}, u32[]{:S(2)}, u32[]{:S(2)}) %all-to-all-start.1) | async-done | bytes 262176 | tf_op jit(solution)/shard_map/all_to_all | solution.py:132
  18.6 10.4 %all-to-all-start = ((bf16[4,128,128]{2,1,0:T(8,128)(2,1)}), bf16[4,128,128]{2,1,0:T(8,128)(2,1)S(1)}, u32[]{:S(2)}, u32[]{:S(2)}) async-start(bf16[4,128,128]{2,1,0:T(8,128)(2,1)} %get-tuple-element.11), calls=%async_computation | async-start | bytes 262144 | tf_op jit(solution)/shard_map/all_to_all | solution.py:132
  29.0 0.0 copy-done.2
  29.0 0.0 copy-done.1
  29.0 3.8 %product.1 = (f32[32,64,128]{2,1,0:T(8,128)S(1)}, bf16[32,64,128]{2,1,0:T(8,128)(2,1)}, bf16[32,64,128]{2,1,0:T(8,128)(2,1)}, bf16[32,64,128]{2,1,0:T(8,128)(2,1)}) custom-call(s32[128]{0:T(128)S(1)} %fusion.2.slots_hbm, bf16[128,64,128]{2,1,0:T(8,128)(2,1)S(1)} %unfold.1.tiles, bf16[16,64,128]{2,1,0:T(8,128)(2,1)S(1)} %bitcast.35), custom_call_target="tpu_custom_call" | custom-call | tf_op jit(solution)/shard_map/product/pallas_call | solution.py:189
  32.9 3.2 %collective-permute-start.3 = (bf16[16,128,128]{2,1,0:T(8,128)(2,1)}, bf16[16,128,128]{2,1,0:T(8,128)(2,1)S(1)}, u32[]{:S(2)}, u32[]{:S(2)}) collective-permute-start(bf16[16,128,128]{2,1,0:T(8,128)(2,1)} %bitcast.44), channel_id=1, source_target_pairs={{0,4},{4,8},{8,12},{12,0},{1,5},{5,9},{9,13},{13,1},{2,6},{6,10},{... | collective-permute-start | bytes 1572872 | tf_op jit(solution)/shard_map/ppermute | solution.py:137
  36.1 4.5 %collective-permute-start.4 = (bf16[16,128,128]{2,1,0:T(8,128)(2,1)}, bf16[16,128,128]{2,1,0:T(8,128)(2,1)S(1)}, u32[]{:S(2)}, u32[]{:S(2)}) collective-permute-start(bf16[16,128,128]{2,1,0:T(8,128)(2,1)} %bitcast.43), channel_id=1, source_target_pairs={{0,8},{4,12},{8,0},{12,4},{1,9},{5,13},{9,1},{13,5},{2,10},{6,14},... | collective-permute-start | bytes 1572872 | tf_op jit(solution)/shard_map/ppermute | solution.py:137
  40.6 3.0 %collective-permute-start.5 = (bf16[16,128,128]{2,1,0:T(8,128)(2,1)}, bf16[16,128,128]{2,1,0:T(8,128)(2,1)S(1)}, u32[]{:S(2)}, u32[]{:S(2)}) collective-permute-start(bf16[16,128,128]{2,1,0:T(8,128)(2,1)} %bitcast.42), channel_id=1, source_target_pairs={{0,12},{4,0},{8,4},{12,8},{1,13},{5,1},{9,5},{13,9},{2,14},{6,2},{... | collective-permute-start | bytes 1572872 | tf_op jit(solution)/shard_map/ppermute | solution.py:137
  43.6 0.0 all-to-all-done.refs_0_
  43.6 2.7 %collective-permute-start = (bf16[4,128,128]{2,1,0:T(8,128)(2,1)S(1)}, bf16[4,128,128]{2,1,0:T(8,128)(2,1)S(1)}, u32[]{:S(2)}, u32[]{:S(2)}) collective-permute-start(bf16[4,128,128]{2,1,0:T(8,128)(2,1)S(1)} %all-to-all-done.refs_0_), channel_id=1, source_target_pairs={{0,1},{1,2},{2,3},{3,16},{16,17},{17,18},{18,19},{19,32},{32,33},{... | collective-permute-start | bytes 393224 | tf_op jit(solution)/shard_map/ppermute | solution.py:137
  46.3 3.1 %collective-permute-start.1 = (bf16[4,128,128]{2,1,0:T(8,128)(2,1)S(1)}, bf16[4,128,128]{2,1,0:T(8,128)(2,1)S(1)}, u32[]{:S(2)}, u32[]{:S(2)}) collective-permute-start(bf16[4,128,128]{2,1,0:T(8,128)(2,1)S(1)} %all-to-all-done.refs_0_), channel_id=1, source_target_pairs={{0,2},{1,3},{2,16},{3,17},{16,18},{17,19},{18,32},{19,33},{32,34},... | collective-permute-start | bytes 393224 | tf_op jit(solution)/shard_map/ppermute | solution.py:137
  49.4 2.5 %collective-permute-done.refs_1_ = bf16[4,128,128]{2,1,0:T(8,128)(2,1)S(1)} collective-permute-done((bf16[4,128,128]{2,1,0:T(8,128)(2,1)S(1)}, bf16[4,128,128]{2,1,0:T(8,128)(2,1)S(1)}, u32[]{:S(2)}, u32[]{:S(2)}) %collective-permute-start) | collective-permute-done | bytes 131104 | tf_op jit(solution)/shard_map/ppermute | solution.py:137
  51.9 3.6 %collective-permute-start.2 = (bf16[4,128,128]{2,1,0:T(8,128)(2,1)S(1)}, bf16[4,128,128]{2,1,0:T(8,128)(2,1)S(1)}, u32[]{:S(2)}, u32[]{:S(2)}) collective-permute-start(bf16[4,128,128]{2,1,0:T(8,128)(2,1)S(1)} %all-to-all-done.refs_0_), channel_id=1, source_target_pairs={{0,51},{1,0},{2,1},{3,2},{16,3},{17,16},{18,17},{19,18},{32,19},{3... | collective-permute-start | bytes 393224 | tf_op jit(solution)/shard_map/ppermute | solution.py:137
  55.6 1.2 %collective-permute-done.1.refs_2_ = bf16[4,128,128]{2,1,0:T(8,128)(2,1)S(1)} collective-permute-done((bf16[4,128,128]{2,1,0:T(8,128)(2,1)S(1)}, bf16[4,128,128]{2,1,0:T(8,128)(2,1)S(1)}, u32[]{:S(2)}, u32[]{:S(2)}) %collective-permute-start.1) | collective-permute-done | bytes 131104 | tf_op jit(solution)/shard_map/ppermute | solution.py:137
  56.8 1.1 %collective-permute-done.2.refs_3_ = bf16[4,128,128]{2,1,0:T(8,128)(2,1)S(1)} collective-permute-done((bf16[4,128,128]{2,1,0:T(8,128)(2,1)S(1)}, bf16[4,128,128]{2,1,0:T(8,128)(2,1)S(1)}, u32[]{:S(2)}, u32[]{:S(2)}) %collective-permute-start.2) | collective-permute-done | bytes 131104 | tf_op jit(solution)/shard_map/ppermute | solution.py:137
  57.9 0.0 collective-permute-done.3.refs_5_
  57.9 2.8 %collective-permute-done.4.refs_6_ = bf16[16,128,128]{2,1,0:T(8,128)(2,1)S(1)} collective-permute-done((bf16[16,128,128]{2,1,0:T(8,128)(2,1)}, bf16[16,128,128]{2,1,0:T(8,128)(2,1)S(1)}, u32[]{:S(2)}, u32[]{:S(2)}) %collective-permute-start.4) | collective-permute-done | bytes 524320 | tf_op jit(solution)/shard_map/ppermute | solution.py:137
  60.8 2.1 %collective-permute-done.5.refs_7_ = bf16[16,128,128]{2,1,0:T(8,128)(2,1)S(1)} collective-permute-done((bf16[16,128,128]{2,1,0:T(8,128)(2,1)}, bf16[16,128,128]{2,1,0:T(8,128)(2,1)S(1)}, u32[]{:S(2)}, u32[]{:S(2)}) %collective-permute-start.5) | collective-permute-done | bytes 524320 | tf_op jit(solution)/shard_map/ppermute | solution.py:137
  62.9 0.5 contract.1
  63.5 13.7 %all_to_all.25 = f32[32,3,128]{2,1,0:T(4,128)S(1)} all-to-all(f32[32,3,128]{2,1,0:T(4,128)S(1)} %contract.1), channel_id=1, replica_groups=mesh['row'=8,'zh'=4,'y'=4,'zl'=4] {'row','y'}, dimensions={0} | all-to-all | bytes 98304 | tf_op jit(solution)/shard_map/all_to_all | solution.py:132
  77.2 22.9 %all_to_all.26 = f32[16,3,128]{2,1,0:T(4,128)S(1)} all-to-all(f32[16,3,128]{2,1,0:T(4,128)S(1)} %broadcast_in_dim.11), channel_id=1, replica_groups=mesh['row'=8,'zh'=4,'y'=4,'zl'=4] {'zh','zl'}, dimensions={0} | all-to-all | bytes 49152 | tf_op jit(solution)/shard_map/all_to_all | solution.py:132
  100.1 12.3 %all_to_all.27 = f32[32,3,128]{2,1,0:T(4,128)S(1)} all-to-all(f32[32,3,128]{2,1,0:T(4,128)S(1)} %broadcast_in_dim.12), channel_id=1, replica_groups=mesh['row'=8,'zh'=4,'y'=4,'zl'=4] {'row','y'}, dimensions={0} | all-to-all | bytes 98304 | tf_op jit(solution)/shard_map/all_to_all | solution.py:132
  112.5 0.1 fusion.10
  112.6 0.6 maximum_maximum_fusion
  (6 shorter events, 0.2 us)
Async XLA Ops:
  0.0 29.0 %copy-start.2 = (s32[1,1,128]{2,1,0:T(1,128)S(1)}, s32[1,1,128]{2,1,0:T(1,128)}, u32[]{:S(2)}) copy-start(s32[1,1,128]{2,1,0:T(1,128)} %param.7) | copy-start | bytes 1540
  0.0 29.0 %copy-start.1 = (s32[1,1,128]{2,1,0:T(1,128)S(1)}, s32[1,1,128]{2,1,0:T(1,128)}, u32[]{:S(2)}) copy-start(s32[1,1,128]{2,1,0:T(1,128)} %param.8) | copy-start | bytes 1540
  1.9 16.6 %all-to-all-start.1 = ((bf16[8,2,64,128]{3,2,1,0:T(8,128)(2,1)}), bf16[8,2,64,128]{3,2,1,0:T(8,128)(2,1)S(1)}, u32[]{:S(2)}, u32[]{:S(2)}) async-start(bf16[8,2,64,128]{3,2,1,0:T(8,128)(2,1)} %get-tuple-element.12), calls=%async_computation.1 | async-start | bytes 524288 | tf_op jit(solution)/shard_map/all_to_all | solution.py:132
  12.7 1.2 %copy-start = (bf16[1,1,128,4096]{3,2,1,0:T(8,128)(2,1)S(1)}, bf16[1,1,128,4096]{3,2,1,0:T(8,128)(2,1)}, u32[]{:S(2)}) copy-start(bf16[1,1,128,4096]{3,2,1,0:T(8,128)(2,1)} %param.6) | copy-start | bytes 3145732
  18.6 25.0 %all-to-all-start = ((bf16[4,128,128]{2,1,0:T(8,128)(2,1)}), bf16[4,128,128]{2,1,0:T(8,128)(2,1)S(1)}, u32[]{:S(2)}, u32[]{:S(2)}) async-start(bf16[4,128,128]{2,1,0:T(8,128)(2,1)} %get-tuple-element.11), calls=%async_computation | async-start | bytes 262144 | tf_op jit(solution)/shard_map/all_to_all | solution.py:132
  32.9 25.1 %collective-permute-start.3 = (bf16[16,128,128]{2,1,0:T(8,128)(2,1)}, bf16[16,128,128]{2,1,0:T(8,128)(2,1)S(1)}, u32[]{:S(2)}, u32[]{:S(2)}) collective-permute-start(bf16[16,128,128]{2,1,0:T(8,128)(2,1)} %bitcast.44), channel_id=1, source_target_pairs={{0,4},{4,8},{8,12},{12,0},{1,5},{5,9},{9,13},{13,1},{2,6},{6,10},{... | collective-permute-start | bytes 1572872 | tf_op jit(solution)/shard_map/ppermute | solution.py:137
  36.1 24.7 %collective-permute-start.4 = (bf16[16,128,128]{2,1,0:T(8,128)(2,1)}, bf16[16,128,128]{2,1,0:T(8,128)(2,1)S(1)}, u32[]{:S(2)}, u32[]{:S(2)}) collective-permute-start(bf16[16,128,128]{2,1,0:T(8,128)(2,1)} %bitcast.43), channel_id=1, source_target_pairs={{0,8},{4,12},{8,0},{12,4},{1,9},{5,13},{9,1},{13,5},{2,10},{6,14},... | collective-permute-start | bytes 1572872 | tf_op jit(solution)/shard_map/ppermute | solution.py:137
  40.6 22.3 %collective-permute-start.5 = (bf16[16,128,128]{2,1,0:T(8,128)(2,1)}, bf16[16,128,128]{2,1,0:T(8,128)(2,1)S(1)}, u32[]{:S(2)}, u32[]{:S(2)}) collective-permute-start(bf16[16,128,128]{2,1,0:T(8,128)(2,1)} %bitcast.42), channel_id=1, source_target_pairs={{0,12},{4,0},{8,4},{12,8},{1,13},{5,1},{9,5},{13,9},{2,14},{6,2},{... | collective-permute-start | bytes 1572872 | tf_op jit(solution)/shard_map/ppermute | solution.py:137
  43.6 8.3 %collective-permute-start = (bf16[4,128,128]{2,1,0:T(8,128)(2,1)S(1)}, bf16[4,128,128]{2,1,0:T(8,128)(2,1)S(1)}, u32[]{:S(2)}, u32[]{:S(2)}) collective-permute-start(bf16[4,128,128]{2,1,0:T(8,128)(2,1)S(1)} %all-to-all-done.refs_0_), channel_id=1, source_target_pairs={{0,1},{1,2},{2,3},{3,16},{16,17},{17,18},{18,19},{19,32},{32,33},{... | collective-permute-start | bytes 393224 | tf_op jit(solution)/shard_map/ppermute | solution.py:137
  46.3 10.5 %collective-permute-start.1 = (bf16[4,128,128]{2,1,0:T(8,128)(2,1)S(1)}, bf16[4,128,128]{2,1,0:T(8,128)(2,1)S(1)}, u32[]{:S(2)}, u32[]{:S(2)}) collective-permute-start(bf16[4,128,128]{2,1,0:T(8,128)(2,1)S(1)} %all-to-all-done.refs_0_), channel_id=1, source_target_pairs={{0,2},{1,3},{2,16},{3,17},{16,18},{17,19},{18,32},{19,33},{32,34},... | collective-permute-start | bytes 393224 | tf_op jit(solution)/shard_map/ppermute | solution.py:137
  51.9 6.0 %collective-permute-start.2 = (bf16[4,128,128]{2,1,0:T(8,128)(2,1)S(1)}, bf16[4,128,128]{2,1,0:T(8,128)(2,1)S(1)}, u32[]{:S(2)}, u32[]{:S(2)}) collective-permute-start(bf16[4,128,128]{2,1,0:T(8,128)(2,1)S(1)} %all-to-all-done.refs_0_), channel_id=1, source_target_pairs={{0,51},{1,0},{2,1},{3,2},{16,3},{17,16},{18,17},{19,18},{32,19},{3... | collective-permute-start | bytes 393224 | tf_op jit(solution)/shard_map/ppermute | solution.py:137

commit v10 on v9

--- a/solution.py
+++ b/solution.py
@@ -11,9 +11,10 @@
 LANES = 2 * TILE
 CHUNK = 16
 GROUP = 4
-NEAR = (0, 1, 2, 15)
-COL_LAYER = ("zh", "y", "zl")
-Z = ("zh", "zl")
+NEAR = (0, 1)
+COL_LAYER = ("zh", "y", "zm", "z0")
+Z = ("zh", "zm", "z0")
+FAR = ("zh", "zm")
 ROW_Y = ("row", "y")
 VMEM = pl.BlockSpec(memory_space=pltpu.VMEM)
 ANY = pl.BlockSpec(memory_space=pl.ANY)
@@ -133,8 +134,13 @@
 
 
 def moved(x, axes, distance):
-    peers = lax.axis_size(axes)
-    return lax.ppermute(x, axes, [(i, (i + distance) % peers) for i in range(peers)])
+    rows, peers = lax.axis_size("row"), lax.axis_size(axes)
+    pairs = [
+        (row * peers + i, row * peers + (i + distance * (1 - 2 * (row % 2))) % peers)
+        for row in range(rows)
+        for i in range(peers)
+    ]
+    return lax.ppermute(x, ("row", *axes), pairs)
 
 
 def summed_over_all(x):
@@ -147,10 +153,11 @@
 def slot_table(a_rows, a_cols, a_count):
     rows, cols = a_rows.reshape(-1), a_cols.reshape(-1)
     f = rows % TILE
-    zh, y, zl = f // 16, f // 4 % 4, f % 4
-    y_distance = (y - lax.axis_index("y")) % 4
-    z_distance = (lax.axis_index("zl") - zl) % 4
-    place = ((y_distance * 4 + z_distance) * 4 + zh) * 2 + rows // TILE
+    zh, y, zm, z0 = f // 16, f // 4 % 4, f // 2 % 2, f % 2
+    way = 1 - 2 * (lax.axis_index("row") % 2)
+    y_distance = (way * (y - lax.axis_index("y"))) % 4
+    other = (z0 + lax.axis_index("z0")) % 2
+    place = ((y_distance * 2 + other) * 8 + zh * 2 + zm) * 2 + rows // TILE
     live = jnp.arange(rows.shape[0], dtype=jnp.int32) < a_count.reshape(())
     return jnp.where(live, place, 128) * 16 + cols
 
@@ -159,13 +166,13 @@
     local_rows, _, slots, area = p_tiles.shape
     total_slots = a_tiles.shape[2]
     n_row, n_y = lax.axis_size("row"), lax.axis_size("y")
-    n_zh, n_zl = lax.axis_size("zh"), lax.axis_size("zl")
-    places = n_zh * n_zl * local_rows
+    n_far = lax.axis_size(FAR)
+    places = lax.axis_size(Z) * local_rows
     own_rows, own_turned = pl.pallas_call(
         window_kernel,
         out_shape=(
             jax.ShapeDtypeStruct((n_row, local_rows, TILE, LANES), jnp.bfloat16),
-            jax.ShapeDtypeStruct((n_zh, LANES, LANES), jnp.bfloat16),
+            jax.ShapeDtypeStruct((n_far, LANES, LANES), jnp.bfloat16),
         ),
         in_specs=[VMEM, VMEM],
         out_specs=[VMEM, VMEM],
@@ -185,7 +192,7 @@
         compiler_params=pltpu.CompilerParams(vmem_limit_bytes=8 << 20),
         name="unfold",
     )(in_vmem(a_tiles.reshape(total_slots, area)))
-    pieces = [exchanged(own_turned, "zh")]
+    pieces = [exchanged(own_turned, FAR)]
     products = pl.pallas_call(
         product_kernel,
         out_shape=[jax.ShapeDtypeStruct((places, TILE, LANES), jnp.float32)]
@@ -204,13 +211,13 @@
     )(slot_table(a_rows, a_cols, a_count), in_vmem(unfolded), in_vmem(column_window))
     own, gathered = products[0].reshape(-1, LANES, LANES), []
     for distance in range(1, n_y):
-        gathered.append(moved(products[distance].reshape(-1, LANES, LANES), "y", distance))
+        gathered.append(moved(products[distance].reshape(-1, LANES, LANES), ("y",), distance))
     for distance in NEAR[1:]:
         pieces.append(moved(pieces[0], Z, distance))
     galerkin = pl.pallas_call(
         contract_kernel,
         out_shape=jax.ShapeDtypeStruct((HALF, 3, LANES), jnp.float32),
-        in_specs=[VMEM] * (n_y + n_zl),
+        in_specs=[VMEM] * (n_y + len(NEAR)),
         out_specs=VMEM,
         compiler_params=pltpu.CompilerParams(vmem_limit_bytes=8 << 20),
         name="contract",
@@ -225,8 +232,8 @@
 
 def solution(mesh):
     torus = Mesh(
-        mesh.devices.reshape(mesh.shape["row"], 4, 4, mesh.shape["layer"]),
-        ("row", "zh", "y", "zl"),
+        mesh.devices.reshape(mesh.shape["row"], 4, 4, 2, 2),
+        ("row", "zh", "y", "zm", "z0"),
     )
     in_specs = (
         P("row", COL_LAYER, None, None),

time: 114 us -> 115 us (level)
  starting transfers between devices: 40.7 us -> 25 us
  blocking collectives: 48.9 us -> 63.4 us
  waiting for transfers between devices: 12.7 us -> 15.4 us
    all_to_all x3 -> x4, blocking collectives: 48.9 us -> 63.4 us  [exchanged(): return lax.all_to_all(x, axes, 0, 0, tiled=True)]
    all_to_all x2 -> x1, starting transfers between devices: 20.6 us -> 10.4 us  [exchanged(): return lax.all_to_all(x, axes, 0, 0, tiled=True)]
    ppermute x6 -> x4, starting transfers between devices: 20.1 us -> 14.5 us  [moved(): return lax.ppermute(x, ('row', *axes), pairs)]
    ppermute x6 -> x4, waiting for transfers between devices: 9.86 us -> 15.4 us  [moved(): return lax.ppermute(x, ('row', *axes), pairs)]
    all_to_all x2 -> x1, waiting for transfers between devices: 2.82 us -> 0.01 us  [exchanged(): return lax.all_to_all(x, axes, 0, 0, tiled=True)]
  transfers between devices with their start and end apart: 8 -> 5, of which waited for: 6 -> 2; matrix products, arithmetic and copies ran while one was open for 0% -> 0% of each run, Pallas kernels for 5% -> 5%
where the time goes in v10:
time: 115 us
  blocking collectives  63.4 us (55%)
  starting transfers between devices  25 us (22%)
  waiting for transfers between devices  15.4 us (13%)
  Pallas kernels  8.11 us (7%)
  local copies, waits for them, and re-layouts  1.37 us (1%)
    all_to_all x4, blocking collectives, exchanged(): return lax.all_to_all(x, axes, 0, 0, tiled=True)  63.4 us
    ppermute x4, waiting for transfers between devices, moved(): return lax.ppermute(x, ('row', *axes), pairs)  15.4 us
    ppermute x4, starting transfers between devices, moved(): return lax.ppermute(x, ('row', *axes), pairs)  14.5 us
    all_to_all x1, starting transfers between devices, exchanged(): return lax.all_to_all(x, axes, 0, 0, tiled=True)  10.4 us
    pallas_call x1, Pallas kernels, coarse_blocks(): pl.pallas_call(product_kernel, out_shape=[jax.ShapeDtypeStruct((places, T...  3.82 us
  transfers between devices with their start and end apart: 5, of which 2 were waited for; matrix products, arithmetic and copies ran while one was open for 0% of the time, Pallas kernels for 5%

profile of v10, /device:TPU:1, one launch (start us, length us, event | category | flops | bytes accessed | tf_op | source)
XLA Modules:
  0.0 114.8 jit_solution(10437970518068007058)
XLA Ops:
  0.0 1.9 %window.1 = (bf16[8,2,64,128]{3,2,1,0:T(8,128)(2,1)}, bf16[8,128,128]{2,1,0:T(8,128)(2,1)}) custom-call(s32[2,4]{1,0:T(2,128)} %bitcast.41, bf16[2,4,4096]{2,1,0:T(4,128)(2,1)} %bitcast.36), custom_call_target="tpu_custom_call" | custom-call | tf_op jit(solution)/shard_map/window/pallas_call | solution.py:171
  1.9 0.0 copy-start.1
  2.0 0.0 copy-start.2
  2.0 16.8 %all_to_all.25 = bf16[8,2,64,128]{3,2,1,0:T(8,128)(2,1)S(1)} all-to-all(bf16[8,2,64,128]{3,2,1,0:T(8,128)(2,1)} %get-tuple-element.12), channel_id=1, replica_groups=mesh['row'=8,'zh'=4,'y'=4,'zm'=2,'z0'=2] {'row'}, dimensions={0} | all-to-all | bytes 524288 | tf_op jit(solution)/shard_map/all_to_all | solution.py:133
  18.7 10.4 %all-to-all-start = ((bf16[8,128,128]{2,1,0:T(8,128)(2,1)}), bf16[8,128,128]{2,1,0:T(8,128)(2,1)S(1)}, u32[]{:S(2)}, u32[]{:S(2)}) async-start(bf16[8,128,128]{2,1,0:T(8,128)(2,1)} %get-tuple-element.11), calls=%async_computation | async-start | bytes 524288 | tf_op jit(solution)/shard_map/all_to_all | solution.py:133
  29.8 0.0 copy-start
  29.8 1.2 %copy-done = bf16[1,1,128,4096]{3,2,1,0:T(8,128)(2,1)S(1)} copy-done((bf16[1,1,128,4096]{3,2,1,0:T(8,128)(2,1)S(1)}, bf16[1,1,128,4096]{3,2,1,0:T(8,128)(2,1)}, u32[]{:S(2)}) %copy-start) | copy-done | bytes 1048600
  31.0 1.8 %unfold.1.tiles = bf16[128,64,128]{2,1,0:T(8,128)(2,1)S(1)} custom-call(bf16[128,4096]{1,0:T(8,128)(2,1)S(1)} %bitcast.33), custom_call_target="tpu_custom_call" | custom-call | tf_op jit(solution)/shard_map/unfold/pallas_call | solution.py:186
  32.8 0.0 copy-done.1
  32.8 0.0 copy-done.2
  32.9 3.8 %product.1 = (f32[32,64,128]{2,1,0:T(8,128)S(1)}, bf16[32,64,128]{2,1,0:T(8,128)(2,1)}, bf16[32,64,128]{2,1,0:T(8,128)(2,1)}, bf16[32,64,128]{2,1,0:T(8,128)(2,1)}) custom-call(s32[128]{0:T(128)S(1)} %fusion.3.slots_hbm, bf16[128,64,128]{2,1,0:T(8,128)(2,1)S(1)} %unfold.1.tiles, bf16[16,64,128]{2,1,0:T(8,128)(2,1)S(1)} %bitcast.35), custom_call_target="tpu_custom_call" | custom-call | tf_op jit(solution)/shard_map/product/pallas_call | solution.py:196
  36.7 4.6 %collective-permute-start.1 = (bf16[16,128,128]{2,1,0:T(8,128)(2,1)}, bf16[16,128,128]{2,1,0:T(8,128)(2,1)S(1)}, u32[]{:S(2)}, u32[]{:S(2)}) collective-permute-start(bf16[16,128,128]{2,1,0:T(8,128)(2,1)} %bitcast.44), channel_id=1, source_target_pairs={{0,4},{4,8},{8,12},{12,0},{64,76},{68,64},{72,68},{76,72},{128,132... | collective-permute-start | bytes 1572872 | tf_op jit(solution)/shard_map/ppermute | solution.py:143
  41.4 2.3 %collective-permute-start.2 = (bf16[16,128,128]{2,1,0:T(8,128)(2,1)}, bf16[16,128,128]{2,1,0:T(8,128)(2,1)S(1)}, u32[]{:S(2)}, u32[]{:S(2)}) collective-permute-start(bf16[16,128,128]{2,1,0:T(8,128)(2,1)} %bitcast.43), channel_id=1, source_target_pairs={{0,8},{4,12},{8,0},{12,4},{64,72},{68,76},{72,64},{76,68},{128,136... | collective-permute-start | bytes 1572872 | tf_op jit(solution)/shard_map/ppermute | solution.py:143
  43.6 2.6 %collective-permute-start.3 = (bf16[16,128,128]{2,1,0:T(8,128)(2,1)}, bf16[16,128,128]{2,1,0:T(8,128)(2,1)S(1)}, u32[]{:S(2)}, u32[]{:S(2)}) collective-permute-start(bf16[16,128,128]{2,1,0:T(8,128)(2,1)} %bitcast.42), channel_id=1, source_target_pairs={{0,12},{4,0},{8,4},{12,8},{64,68},{68,72},{72,76},{76,64},{128,140... | collective-permute-start | bytes 1572872 | tf_op jit(solution)/shard_map/ppermute | solution.py:143
  46.2 0.0 all-to-all-done.refs_0_
  46.3 5.0 %collective-permute-start = (bf16[8,128,128]{2,1,0:T(8,128)(2,1)S(1)}, bf16[8,128,128]{2,1,0:T(8,128)(2,1)S(1)}, u32[]{:S(2)}, u32[]{:S(2)}) collective-permute-start(bf16[8,128,128]{2,1,0:T(8,128)(2,1)S(1)} %all-to-all-done.refs_0_), channel_id=1, source_target_pairs={{0,1},{1,2},{2,3},{3,16},{16,17},{17,18},{18,19},{19,32},{32,33},{... | collective-permute-start | bytes 786440 | tf_op jit(solution)/shard_map/ppermute | solution.py:143
  51.3 9.2 %collective-permute-done.1.refs_3_ = bf16[16,128,128]{2,1,0:T(8,128)(2,1)S(1)} collective-permute-done((bf16[16,128,128]{2,1,0:T(8,128)(2,1)}, bf16[16,128,128]{2,1,0:T(8,128)(2,1)S(1)}, u32[]{:S(2)}, u32[]{:S(2)}) %collective-permute-start.1) | collective-permute-done | bytes 524320 | tf_op jit(solution)/shard_map/ppermute | solution.py:143
  60.5 0.0 collective-permute-done.2.refs_4_
  60.5 6.2 %collective-permute-done.3.refs_5_ = bf16[16,128,128]{2,1,0:T(8,128)(2,1)S(1)} collective-permute-done((bf16[16,128,128]{2,1,0:T(8,128)(2,1)}, bf16[16,128,128]{2,1,0:T(8,128)(2,1)S(1)}, u32[]{:S(2)}, u32[]{:S(2)}) %collective-permute-start.3) | collective-permute-done | bytes 524320 | tf_op jit(solution)/shard_map/ppermute | solution.py:143
  66.7 0.0 collective-permute-done.refs_1_
  66.7 0.6 contract.1
  67.2 11.2 %all_to_all.26 = f32[32,3,128]{2,1,0:T(4,128)S(1)} all-to-all(f32[32,3,128]{2,1,0:T(4,128)S(1)} %contract.1), channel_id=1, replica_groups=mesh['row'=8,'zh'=4,'y'=4,'zm'=2,'z0'=2] {'row','y'}, dimensions={0} | all-to-all | bytes 98304 | tf_op jit(solution)/shard_map/all_to_all | solution.py:133
  78.5 23.1 %all_to_all.27 = f32[16,3,128]{2,1,0:T(4,128)S(1)} all-to-all(f32[16,3,128]{2,1,0:T(4,128)S(1)} %broadcast_in_dim.11), channel_id=1, replica_groups=mesh['row'=8,'zh'=4,'y'=4,'zm'=2,'z0'=2] {'zh','zm','z0'}, dimensions={0} | all-to-all | bytes 49152 | tf_op jit(solution)/shard_map/all_to_all | solution.py:133
  101.6 12.3 %all_to_all.28 = f32[32,3,128]{2,1,0:T(4,128)S(1)} all-to-all(f32[32,3,128]{2,1,0:T(4,128)S(1)} %broadcast_in_dim.12), channel_id=1, replica_groups=mesh['row'=8,'zh'=4,'y'=4,'zm'=2,'z0'=2] {'row','y'}, dimensions={0} | all-to-all | bytes 98304 | tf_op jit(solution)/shard_map/all_to_all | solution.py:133
  114.0 0.1 fusion.13
  114.1 0.6 maximum_maximum_fusion
  (6 shorter events, 0.2 us)
Async XLA Ops:
  1.9 30.9 %copy-start.1 = (s32[1,1,128]{2,1,0:T(1,128)S(1)}, s32[1,1,128]{2,1,0:T(1,128)}, u32[]{:S(2)}) copy-start(s32[1,1,128]{2,1,0:T(1,128)} %param.8) | copy-start | bytes 1540
  2.0 30.9 %copy-start.2 = (s32[1,1,128]{2,1,0:T(1,128)S(1)}, s32[1,1,128]{2,1,0:T(1,128)}, u32[]{:S(2)}) copy-start(s32[1,1,128]{2,1,0:T(1,128)} %param.7) | copy-start | bytes 1540
  18.7 27.5 %all-to-all-start = ((bf16[8,128,128]{2,1,0:T(8,128)(2,1)}), bf16[8,128,128]{2,1,0:T(8,128)(2,1)S(1)}, u32[]{:S(2)}, u32[]{:S(2)}) async-start(bf16[8,128,128]{2,1,0:T(8,128)(2,1)} %get-tuple-element.11), calls=%async_computation | async-start | bytes 524288 | tf_op jit(solution)/shard_map/all_to_all | solution.py:133
  29.8 1.2 %copy-start = (bf16[1,1,128,4096]{3,2,1,0:T(8,128)(2,1)S(1)}, bf16[1,1,128,4096]{3,2,1,0:T(8,128)(2,1)}, u32[]{:S(2)}) copy-start(bf16[1,1,128,4096]{3,2,1,0:T(8,128)(2,1)} %param.6) | copy-start | bytes 3145732
  36.7 23.7 %collective-permute-start.1 = (bf16[16,128,128]{2,1,0:T(8,128)(2,1)}, bf16[16,128,128]{2,1,0:T(8,128)(2,1)S(1)}, u32[]{:S(2)}, u32[]{:S(2)}) collective-permute-start(bf16[16,128,128]{2,1,0:T(8,128)(2,1)} %bitcast.44), channel_id=1, source_target_pairs={{0,4},{4,8},{8,12},{12,0},{64,76},{68,64},{72,68},{76,72},{128,132... | collective-permute-start | bytes 1572872 | tf_op jit(solution)/shard_map/ppermute | solution.py:143
  41.4 19.1 %collective-permute-start.2 = (bf16[16,128,128]{2,1,0:T(8,128)(2,1)}, bf16[16,128,128]{2,1,0:T(8,128)(2,1)S(1)}, u32[]{:S(2)}, u32[]{:S(2)}) collective-permute-start(bf16[16,128,128]{2,1,0:T(8,128)(2,1)} %bitcast.43), channel_id=1, source_target_pairs={{0,8},{4,12},{8,0},{12,4},{64,72},{68,76},{72,64},{76,68},{128,136... | collective-permute-start | bytes 1572872 | tf_op jit(solution)/shard_map/ppermute | solution.py:143
  43.6 23.0 %collective-permute-start.3 = (bf16[16,128,128]{2,1,0:T(8,128)(2,1)}, bf16[16,128,128]{2,1,0:T(8,128)(2,1)S(1)}, u32[]{:S(2)}, u32[]{:S(2)}) collective-permute-start(bf16[16,128,128]{2,1,0:T(8,128)(2,1)} %bitcast.42), channel_id=1, source_target_pairs={{0,12},{4,0},{8,4},{12,8},{64,68},{68,72},{72,76},{76,64},{128,140... | collective-permute-start | bytes 1572872 | tf_op jit(solution)/shard_map/ppermute | solution.py:143
  46.3 20.4 %collective-permute-start = (bf16[8,128,128]{2,1,0:T(8,128)(2,1)S(1)}, bf16[8,128,128]{2,1,0:T(8,128)(2,1)S(1)}, u32[]{:S(2)}, u32[]{:S(2)}) collective-permute-start(bf16[8,128,128]{2,1,0:T(8,128)(2,1)S(1)} %all-to-all-done.refs_0_), channel_id=1, source_target_pairs={{0,1},{1,2},{2,3},{3,16},{16,17},{17,18},{18,19},{19,32},{32,33},{... | collective-permute-start | bytes 786440 | tf_op jit(solution)/shard_map/ppermute | solution.py:143

commit v11 on v10

--- a/solution.py
+++ b/solution.py
@@ -14,7 +14,8 @@
 NEAR = (0, 1)
 COL_LAYER = ("zh", "y", "zm", "z0")
 Z = ("zh", "zm", "z0")
-FAR = ("zh", "zm")
+FAR = ("zm", "zh")
+SUM_Z = ("z0", "zm", "zh")
 ROW_Y = ("row", "y")
 VMEM = pl.BlockSpec(memory_space=pltpu.VMEM)
 ANY = pl.BlockSpec(memory_space=pl.ANY)
@@ -146,7 +147,7 @@
 def summed_over_all(x):
     peers, depth = lax.axis_size(ROW_Y), lax.axis_size(Z)
     piece = jnp.sum(exchanged(x, ROW_Y), axis=0)
-    piece = jnp.sum(exchanged(jnp.broadcast_to(piece, (depth, *piece.shape)), Z), axis=0)
+    piece = jnp.sum(exchanged(jnp.broadcast_to(piece, (depth, *piece.shape)), SUM_Z), axis=0)
     return exchanged(jnp.broadcast_to(piece, (peers, *piece.shape)), ROW_Y)
 
 
@@ -157,7 +158,7 @@
     way = 1 - 2 * (lax.axis_index("row") % 2)
     y_distance = (way * (y - lax.axis_index("y"))) % 4
     other = (z0 + lax.axis_index("z0")) % 2
-    place = ((y_distance * 2 + other) * 8 + zh * 2 + zm) * 2 + rows // TILE
+    place = ((y_distance * 2 + other) * 8 + zm * 4 + zh) * 2 + rows // TILE
     live = jnp.arange(rows.shape[0], dtype=jnp.int32) < a_count.reshape(())
     return jnp.where(live, place, 128) * 16 + cols
 

time: 115 us -> 115 us (level)
  no operation moved by 1% of the time
where the time goes in v11:
time: 115 us
  blocking collectives  63.3 us (55%)
  starting transfers between devices  25 us (22%)
  waiting for transfers between devices  15.4 us (13%)
  Pallas kernels  8.11 us (7%)
  local copies, waits for them, and re-layouts  1.37 us (1%)
    all_to_all x4, blocking collectives, exchanged(): return lax.all_to_all(x, axes, 0, 0, tiled=True)  63.3 us
    ppermute x4, waiting for transfers between devices, moved(): return lax.ppermute(x, ('row', *axes), pairs)  15.4 us
    ppermute x4, starting transfers between devices, moved(): return lax.ppermute(x, ('row', *axes), pairs)  14.5 us
    all_to_all x1, starting transfers between devices, exchanged(): return lax.all_to_all(x, axes, 0, 0, tiled=True)  10.4 us
    pallas_call x1, Pallas kernels, coarse_blocks(): pl.pallas_call(product_kernel, out_shape=[jax.ShapeDtypeStruct((places, T...  3.82 us
  transfers between devices with their start and end apart: 5, of which 2 were waited for; matrix products, arithmetic and copies ran while one was open for 0% of the time, Pallas kernels for 5%

profile of v11, /device:TPU:1, one launch (start us, length us, event | category | flops | bytes accessed | tf_op | source)
XLA Modules:
  0.0 114.6 jit_solution(7524900798254948418)
XLA Ops:
  0.0 1.9 %window.1 = (bf16[8,2,64,128]{3,2,1,0:T(8,128)(2,1)}, bf16[8,128,128]{2,1,0:T(8,128)(2,1)}) custom-call(s32[2,4]{1,0:T(2,128)} %bitcast.41, bf16[2,4,4096]{2,1,0:T(4,128)(2,1)} %bitcast.36), custom_call_target="tpu_custom_call" | custom-call | tf_op jit(solution)/shard_map/window/pallas_call | solution.py:172
  1.9 0.0 copy-start.1
  2.0 0.0 copy-start.2
  2.0 16.8 %all_to_all.25 = bf16[8,2,64,128]{3,2,1,0:T(8,128)(2,1)S(1)} all-to-all(bf16[8,2,64,128]{3,2,1,0:T(8,128)(2,1)} %get-tuple-element.12), channel_id=1, replica_groups=mesh['row'=8,'zh'=4,'y'=4,'zm'=2,'z0'=2] {'row'}, dimensions={0} | all-to-all | bytes 524288 | tf_op jit(solution)/shard_map/all_to_all | solution.py:134
  18.7 10.4 %all-to-all-start = ((bf16[8,128,128]{2,1,0:T(8,128)(2,1)}), bf16[8,128,128]{2,1,0:T(8,128)(2,1)S(1)}, u32[]{:S(2)}, u32[]{:S(2)}) async-start(bf16[8,128,128]{2,1,0:T(8,128)(2,1)} %get-tuple-element.11), calls=%async_computation | async-start | bytes 524288 | tf_op jit(solution)/shard_map/all_to_all | solution.py:134
  29.8 0.0 copy-start
  29.8 1.2 %copy-done = bf16[1,1,128,4096]{3,2,1,0:T(8,128)(2,1)S(1)} copy-done((bf16[1,1,128,4096]{3,2,1,0:T(8,128)(2,1)S(1)}, bf16[1,1,128,4096]{3,2,1,0:T(8,128)(2,1)}, u32[]{:S(2)}) %copy-start) | copy-done | bytes 1048600
  31.0 1.8 %unfold.1.tiles = bf16[128,64,128]{2,1,0:T(8,128)(2,1)S(1)} custom-call(bf16[128,4096]{1,0:T(8,128)(2,1)S(1)} %bitcast.33), custom_call_target="tpu_custom_call" | custom-call | tf_op jit(solution)/shard_map/unfold/pallas_call | solution.py:187
  32.8 0.0 copy-done.1
  32.8 0.0 copy-done.2
  32.9 3.8 %product.1 = (f32[32,64,128]{2,1,0:T(8,128)S(1)}, bf16[32,64,128]{2,1,0:T(8,128)(2,1)}, bf16[32,64,128]{2,1,0:T(8,128)(2,1)}, bf16[32,64,128]{2,1,0:T(8,128)(2,1)}) custom-call(s32[128]{0:T(128)S(1)} %fusion.2.slots_hbm, bf16[128,64,128]{2,1,0:T(8,128)(2,1)S(1)} %unfold.1.tiles, bf16[16,64,128]{2,1,0:T(8,128)(2,1)S(1)} %bitcast.35), custom_call_target="tpu_custom_call" | custom-call | tf_op jit(solution)/shard_map/product/pallas_call | solution.py:197
  36.7 4.6 %collective-permute-start.1 = (bf16[16,128,128]{2,1,0:T(8,128)(2,1)}, bf16[16,128,128]{2,1,0:T(8,128)(2,1)S(1)}, u32[]{:S(2)}, u32[]{:S(2)}) collective-permute-start(bf16[16,128,128]{2,1,0:T(8,128)(2,1)} %bitcast.44), channel_id=1, source_target_pairs={{0,4},{4,8},{8,12},{12,0},{64,76},{68,64},{72,68},{76,72},{128,132... | collective-permute-start | bytes 1572872 | tf_op jit(solution)/shard_map/ppermute | solution.py:144
  41.4 2.3 %collective-permute-start.2 = (bf16[16,128,128]{2,1,0:T(8,128)(2,1)}, bf16[16,128,128]{2,1,0:T(8,128)(2,1)S(1)}, u32[]{:S(2)}, u32[]{:S(2)}) collective-permute-start(bf16[16,128,128]{2,1,0:T(8,128)(2,1)} %bitcast.43), channel_id=1, source_target_pairs={{0,8},{4,12},{8,0},{12,4},{64,72},{68,76},{72,64},{76,68},{128,136... | collective-permute-start | bytes 1572872 | tf_op jit(solution)/shard_map/ppermute | solution.py:144
  43.6 2.6 %collective-permute-start.3 = (bf16[16,128,128]{2,1,0:T(8,128)(2,1)}, bf16[16,128,128]{2,1,0:T(8,128)(2,1)S(1)}, u32[]{:S(2)}, u32[]{:S(2)}) collective-permute-start(bf16[16,128,128]{2,1,0:T(8,128)(2,1)} %bitcast.42), channel_id=1, source_target_pairs={{0,12},{4,0},{8,4},{12,8},{64,68},{68,72},{72,76},{76,64},{128,140... | collective-permute-start | bytes 1572872 | tf_op jit(solution)/shard_map/ppermute | solution.py:144
  46.2 0.0 all-to-all-done.refs_0_
  46.3 5.0 %collective-permute-start = (bf16[8,128,128]{2,1,0:T(8,128)(2,1)S(1)}, bf16[8,128,128]{2,1,0:T(8,128)(2,1)S(1)}, u32[]{:S(2)}, u32[]{:S(2)}) collective-permute-start(bf16[8,128,128]{2,1,0:T(8,128)(2,1)S(1)} %all-to-all-done.refs_0_), channel_id=1, source_target_pairs={{0,1},{1,2},{2,3},{3,16},{16,17},{17,18},{18,19},{19,32},{32,33},{... | collective-permute-start | bytes 786440 | tf_op jit(solution)/shard_map/ppermute | solution.py:144
  51.3 9.2 %collective-permute-done.1.refs_3_ = bf16[16,128,128]{2,1,0:T(8,128)(2,1)S(1)} collective-permute-done((bf16[16,128,128]{2,1,0:T(8,128)(2,1)}, bf16[16,128,128]{2,1,0:T(8,128)(2,1)S(1)}, u32[]{:S(2)}, u32[]{:S(2)}) %collective-permute-start.1) | collective-permute-done | bytes 524320 | tf_op jit(solution)/shard_map/ppermute | solution.py:144
  60.5 0.0 collective-permute-done.2.refs_4_
  60.5 6.2 %collective-permute-done.3.refs_5_ = bf16[16,128,128]{2,1,0:T(8,128)(2,1)S(1)} collective-permute-done((bf16[16,128,128]{2,1,0:T(8,128)(2,1)}, bf16[16,128,128]{2,1,0:T(8,128)(2,1)S(1)}, u32[]{:S(2)}, u32[]{:S(2)}) %collective-permute-start.3) | collective-permute-done | bytes 524320 | tf_op jit(solution)/shard_map/ppermute | solution.py:144
  66.7 0.0 collective-permute-done.refs_1_
  66.7 0.6 contract.1
  67.2 11.2 %all_to_all.26 = f32[32,3,128]{2,1,0:T(4,128)S(1)} all-to-all(f32[32,3,128]{2,1,0:T(4,128)S(1)} %contract.1), channel_id=1, replica_groups=mesh['row'=8,'zh'=4,'y'=4,'zm'=2,'z0'=2] {'row','y'}, dimensions={0} | all-to-all | bytes 98304 | tf_op jit(solution)/shard_map/all_to_all | solution.py:134
  78.5 23.0 %all_to_all.27 = f32[16,3,128]{2,1,0:T(4,128)S(1)} all-to-all(f32[16,3,128]{2,1,0:T(4,128)S(1)} %broadcast_in_dim.11), channel_id=1, replica_groups=mesh['row'=8,'zh'=4,'y'=4,'zm'=2,'z0'=2] {'z0','zm','zh'}, dimensions={0} | all-to-all | bytes 49152 | tf_op jit(solution)/shard_map/all_to_all | solution.py:134
  101.5 12.4 %all_to_all.28 = f32[32,3,128]{2,1,0:T(4,128)S(1)} all-to-all(f32[32,3,128]{2,1,0:T(4,128)S(1)} %broadcast_in_dim.12), channel_id=1, replica_groups=mesh['row'=8,'zh'=4,'y'=4,'zm'=2,'z0'=2] {'row','y'}, dimensions={0} | all-to-all | bytes 98304 | tf_op jit(solution)/shard_map/all_to_all | solution.py:134
  113.9 0.1 fusion.15
  114.0 0.6 maximum_maximum_fusion
  (6 shorter events, 0.2 us)
Async XLA Ops:
  1.9 30.9 %copy-start.1 = (s32[1,1,128]{2,1,0:T(1,128)S(1)}, s32[1,1,128]{2,1,0:T(1,128)}, u32[]{:S(2)}) copy-start(s32[1,1,128]{2,1,0:T(1,128)} %param.8) | copy-start | bytes 1540
  2.0 30.9 %copy-start.2 = (s32[1,1,128]{2,1,0:T(1,128)S(1)}, s32[1,1,128]{2,1,0:T(1,128)}, u32[]{:S(2)}) copy-start(s32[1,1,128]{2,1,0:T(1,128)} %param.7) | copy-start | bytes 1540
  18.7 27.5 %all-to-all-start = ((bf16[8,128,128]{2,1,0:T(8,128)(2,1)}), bf16[8,128,128]{2,1,0:T(8,128)(2,1)S(1)}, u32[]{:S(2)}, u32[]{:S(2)}) async-start(bf16[8,128,128]{2,1,0:T(8,128)(2,1)} %get-tuple-element.11), calls=%async_computation | async-start | bytes 524288 | tf_op jit(solution)/shard_map/all_to_all | solution.py:134
  29.8 1.2 %copy-start = (bf16[1,1,128,4096]{3,2,1,0:T(8,128)(2,1)S(1)}, bf16[1,1,128,4096]{3,2,1,0:T(8,128)(2,1)}, u32[]{:S(2)}) copy-start(bf16[1,1,128,4096]{3,2,1,0:T(8,128)(2,1)} %param.6) | copy-start | bytes 3145732
  36.7 23.7 %collective-permute-start.1 = (bf16[16,128,128]{2,1,0:T(8,128)(2,1)}, bf16[16,128,128]{2,1,0:T(8,128)(2,1)S(1)}, u32[]{:S(2)}, u32[]{:S(2)}) collective-permute-start(bf16[16,128,128]{2,1,0:T(8,128)(2,1)} %bitcast.44), channel_id=1, source_target_pairs={{0,4},{4,8},{8,12},{12,0},{64,76},{68,64},{72,68},{76,72},{128,132... | collective-permute-start | bytes 1572872 | tf_op jit(solution)/shard_map/ppermute | solution.py:144
  41.4 19.1 %collective-permute-start.2 = (bf16[16,128,128]{2,1,0:T(8,128)(2,1)}, bf16[16,128,128]{2,1,0:T(8,128)(2,1)S(1)}, u32[]{:S(2)}, u32[]{:S(2)}) collective-permute-start(bf16[16,128,128]{2,1,0:T(8,128)(2,1)} %bitcast.43), channel_id=1, source_target_pairs={{0,8},{4,12},{8,0},{12,4},{64,72},{68,76},{72,64},{76,68},{128,136... | collective-permute-start | bytes 1572872 | tf_op jit(solution)/shard_map/ppermute | solution.py:144
  43.6 23.0 %collective-permute-start.3 = (bf16[16,128,128]{2,1,0:T(8,128)(2,1)}, bf16[16,128,128]{2,1,0:T(8,128)(2,1)S(1)}, u32[]{:S(2)}, u32[]{:S(2)}) collective-permute-start(bf16[16,128,128]{2,1,0:T(8,128)(2,1)} %bitcast.42), channel_id=1, source_target_pairs={{0,12},{4,0},{8,4},{12,8},{64,68},{68,72},{72,76},{76,64},{128,140... | collective-permute-start | bytes 1572872 | tf_op jit(solution)/shard_map/ppermute | solution.py:144
  46.3 20.4 %collective-permute-start = (bf16[8,128,128]{2,1,0:T(8,128)(2,1)S(1)}, bf16[8,128,128]{2,1,0:T(8,128)(2,1)S(1)}, u32[]{:S(2)}, u32[]{:S(2)}) collective-permute-start(bf16[8,128,128]{2,1,0:T(8,128)(2,1)S(1)} %all-to-all-done.refs_0_), channel_id=1, source_target_pairs={{0,1},{1,2},{2,3},{3,16},{16,17},{17,18},{18,19},{19,32},{32,33},{... | collective-permute-start | bytes 786440 | tf_op jit(solution)/shard_map/ppermute | solution.py:144
